TPU v7x, 128 devices: a whole 4x4x4 slice. The times are simulated.
128 devices in a mesh: gx: 16 (over z, y_lo, core), gy: 8 (over x, y_hi).
Axes of the slice: x: 4, y: 4 (y_hi: 2, y_lo: 2; y = y_hi * 2 + y_lo), z: 4, core: 2. Of those that a mesh axis runs over, the one named last changes fastest.
Arguments:
- velocity: float32 [3, 4096, 1024], P(None, 'gx', 'gy'), may hold values from 0.4 to 1.6
- adjoint_seed: float32 [3, 4096, 1024], P(None, 'gx', 'gy'), may hold values from -6 to 6
- courant: float32 [3, 4096, 1024], P(None, 'gx', 'gy'), may hold values from 0.1 to 0.45
- viscosity: float32 [3, 4096, 1024], P(None, 'gx', 'gy'), may hold values from 0.02 to 0.1
- turbine_tile: int32 [512, 1], P(('gx', 'gy')), may hold values from 0 to 127; in each aligned block of 512 rows (0 to 511, 512 to 1023, ...) at most 12 rows name the same one
- turbine_offset: int32 [512, 2], P(('gx', 'gy')), may hold values from 0 to 64
- thrust: float32 [512], P(('gx', 'gy')), may hold values from 0.5 to 2
- disk_width: float32 [512], P(('gx', 'gy')), may hold values from 8 to 16
Outputs:
- adjoint_start: float32 [3, 4096, 1024], P(None, 'gx', 'gy')
- thrust_grad: float32 [512], P(('gx', 'gy'))
Inputs may be any that keep to these rules, and one draw needn't show every extreme that they name: `turbine_tile`: each turbine's tile is the index along gx times the number of devices of gy plus the index along gy of the device whose cells hold its footprint. No tile holds more than 12 turbines, and some tile holds exactly 12.
All inputs are finite; a program needn't handle non-finite values.
Results may differ from a plain program's by a relative error of at most 0.00002.
Values sent between devices are 32-bit elements; how exact they have to be, the bound alone decides.
A program may use at most 128 MiB of HBM per device.

v0:
```python
import functools

import jax
import jax.numpy as jnp
from jax import lax
from jax.experimental import pallas as pl
from jax.experimental.pallas import tpu as pltpu
from jax.sharding import PartitionSpec as P

LEV = 3
STEPS = 8
FP = 64
MARGIN = 2 * (STEPS - 1)

VERTICAL_MIX = 0.05
DRAG_SCALE = 0.01
HIGHEST = lax.Precision.HIGHEST


MESH_ID = pl.DeviceIdType.MESH


HALO_MOVES = ((1, 0), (-1, 0), (0, 1), (0, -1), (1, 1), (1, -1), (-1, 1), (-1, -1))


def enter(n_gy, n_dev, me):
    barrier = pltpu.get_barrier_semaphore()
    for step in range(1, n_dev):
        target = lax.rem(me + step, n_dev)
        pl.semaphore_signal(
            barrier, inc=1, device_id=(target // n_gy, target % n_gy), device_id_type=MESH_ID
        )
    pl.semaphore_wait(barrier, n_dev - 1)


def spread_rows(n_gy, n_dev, me, src_of, slots, send_sem, recv_sem):
    for step in range(1, n_dev):
        target = lax.rem(me + step, n_dev)
        pltpu.make_async_remote_copy(
            src_of(target),
            slots.at[pl.ds(me, 1)],
            send_sem,
            recv_sem,
            device_id=(target // n_gy, target % n_gy),
            device_id_type=MESH_ID,
        ).start()
    first = lax.rem(me + 1, n_dev)
    rest = pl.ds(0, n_dev - 1)
    return pltpu.make_async_remote_copy(
        slots.at[rest],
        slots.at[rest],
        send_sem,
        recv_sem,
        device_id=(first // n_gy, first % n_gy),
        device_id_type=MESH_ID,
    )


def open_kernel(n_gx, n_gy, *refs):
    n_dev = n_gx * n_gy
    n_halo = len(HALO_MOVES)
    info_ref = refs[0]
    pieces = refs[1 : 1 + n_halo]
    gathered = refs[1 + n_halo]
    landed = refs[2 + n_halo : 2 + 2 * n_halo]
    slots, send_sem, recv_sem, local_sem, halo_send, halo_recv = refs[2 + 2 * n_halo :]
    gx = lax.axis_index("gx")
    gy = lax.axis_index("gy")
    me = gx * n_gy + gy
    enter(n_gy, n_dev, me)
    local = pltpu.make_async_copy(info_ref, slots.at[pl.ds(me, 1)], local_sem)
    local.start()
    halo = []
    for index, (dx, dy) in enumerate(HALO_MOVES):
        copy = pltpu.make_async_remote_copy(
            pieces[index],
            landed[index],
            halo_send.at[index],
            halo_recv.at[index],
            device_id=(lax.rem(gx + dx + n_gx, n_gx), lax.rem(gy + dy + n_gy, n_gy)),
            device_id_type=MESH_ID,
        )
        copy.start()
        halo.append(copy)
    every = spread_rows(n_gy, n_dev, me, lambda target: info_ref, slots, send_sem, recv_sem)
    local.wait()
    for copy in halo:
        copy.wait()
    every.wait_send()
    every.wait_recv()
    gathered[...] = slots[...]


def open_exchange(info_row, pieces):
    n_gx = lax.axis_size("gx")
    n_gy = lax.axis_size("gy")
    n_dev = n_gx * n_gy
    vmem = pl.BlockSpec(memory_space=pltpu.VMEM)
    out_shape = [jax.ShapeDtypeStruct((n_dev, info_row.shape[1]), jnp.float32)] + [
        jax.ShapeDtypeStruct(piece.shape, piece.dtype) for piece in pieces
    ]
    return pl.pallas_call(
        functools.partial(open_kernel, n_gx, n_gy),
        out_shape=out_shape,
        in_specs=[vmem] * (1 + len(pieces)),
        out_specs=[vmem] * len(out_shape),
        scratch_shapes=[
            pltpu.VMEM((n_dev, info_row.shape[1]), jnp.float32),
            pltpu.SemaphoreType.DMA,
            pltpu.SemaphoreType.DMA,
            pltpu.SemaphoreType.DMA,
            pltpu.SemaphoreType.DMA((len(pieces),)),
            pltpu.SemaphoreType.DMA((len(pieces),)),
        ],
        compiler_params=pltpu.CompilerParams(has_side_effects=True, collective_id=0),
    )(info_row, *pieces)


def close_kernel(n_gy, n_dev, src_ref, out_ref, slots, send_sem, recv_sem, local_sem):
    gx = lax.axis_index("gx")
    gy = lax.axis_index("gy")
    me = gx * n_gy + gy
    enter(n_gy, n_dev, me)
    local = pltpu.make_async_copy(src_ref.at[pl.ds(me, 1)], slots.at[pl.ds(me, 1)], local_sem)
    local.start()
    every = spread_rows(
        n_gy, n_dev, me, lambda target: src_ref.at[pl.ds(target, 1)], slots, send_sem, recv_sem
    )
    local.wait()
    every.wait_send()
    every.wait_recv()
    out_ref[...] = jnp.sum(slots[...], axis=0, keepdims=True)


def close_scatter(rows):
    n_gy = lax.axis_size("gy")
    n_dev = lax.axis_size("gx") * n_gy
    vmem = pl.BlockSpec(memory_space=pltpu.VMEM)
    return pl.pallas_call(
        functools.partial(close_kernel, n_gy, n_dev),
        out_shape=jax.ShapeDtypeStruct((1, rows.shape[1]), jnp.float32),
        in_specs=[vmem],
        out_specs=vmem,
        scratch_shapes=[
            pltpu.VMEM(rows.shape, jnp.float32),
            pltpu.SemaphoreType.DMA,
            pltpu.SemaphoreType.DMA,
            pltpu.SemaphoreType.DMA,
        ],
        compiler_params=pltpu.CompilerParams(has_side_effects=True, collective_id=1),
    )(rows)


def halo_pieces(block, m):
    depth = block.shape[0]
    last_r, first_r = block[:, -m:, :], block[:, :m, :]
    last_c = jnp.swapaxes(block[:, :, -m:], 1, 2)
    first_c = jnp.swapaxes(block[:, :, :m], 1, 2)
    pieces = (
        last_r,
        first_r,
        last_c,
        first_c,
        last_r[:, :, -m:],
        last_r[:, :, :m],
        first_r[:, :, -m:],
        first_r[:, :, :m],
    )
    return tuple(piece.reshape(depth * m, piece.shape[2]) for piece in pieces)


def assemble(block, landed, m, size_r, size_c):
    depth, rows, cols = block.shape
    row_low, row_high, col_low, col_high, c_ll, c_lh, c_hl, c_hh = (
        piece.reshape(depth, m, piece.shape[1]) for piece in landed
    )
    col_low = jnp.swapaxes(col_low, 1, 2)
    col_high = jnp.swapaxes(col_high, 1, 2)
    gap_c = size_c - cols - 2 * m
    gap_r = size_r - rows - 2 * m

    def band(left, middle, right):
        fill = jnp.zeros(left.shape[:2] + (gap_c,), jnp.float32)
        return jnp.concatenate([left, middle, fill, right], axis=2)

    fill = jnp.zeros((depth, gap_r, size_c), jnp.float32)
    return jnp.concatenate(
        [
            band(block, col_high, col_low),
            band(row_high, c_hh, c_hl),
            fill,
            band(row_low, c_lh, c_ll),
        ],
        axis=1,
    )


def stencil_kernel(levels, steps, ext_ref, drag_ref, lam_out, sens_out, states, lams):
    size_r, size_c = ext_ref.shape[1:]

    def west(x):
        return pltpu.roll(x, 1, 0)

    def east(x):
        return pltpu.roll(x, size_r - 1, 0)

    def south(x):
        return pltpu.roll(x, 1, 1)

    def north(x):
        return pltpu.roll(x, size_c - 1, 1)

    def vertical(plane, level, center):
        mix = None
        if level + 1 < levels:
            mix = plane(level + 1) - center
        if level > 0:
            below = plane(level - 1) - center
            mix = below if mix is None else mix + below
        return mix

    for level in range(levels):
        states[0, level] = ext_ref[level]

    def forward(n, carry):
        for level in range(levels):
            center = states[n, level]
            upwind = west(center)
            advect = ext_ref[levels + level]
            diffuse = ext_ref[2 * levels + level]
            states[n + 1, level] = (
                center
                + advect * (upwind - center)
                + diffuse * (east(center) + upwind + north(center) + south(center) - 4.0 * center)
                + VERTICAL_MIX * vertical(lambda l: states[n, l], level, center)
                - drag_ref[level] * (center * jnp.sqrt(center * center + 1.0))
            )
        return carry

    lax.fori_loop(0, steps - 1, forward, 0)
    for level in range(levels):
        lams[0, level] = ext_ref[3 * levels + level]
        sens_out[level] = jnp.zeros(sens_out.shape[1:], jnp.float32)

    def backward(i, carry):
        n = steps - 1 - i
        now = i % 2
        for level in range(levels):
            adjoint = lams[now, level]
            state = states[n, level]
            sens_out[level] = sens_out[level] - adjoint * (state * jnp.sqrt(state * state + 1.0))
            flux_adv = ext_ref[levels + level] * adjoint
            flux_dif = ext_ref[2 * levels + level] * adjoint
            square_one = state * state + 1.0
            slope = (square_one + state * state) / jnp.sqrt(square_one)
            lams[1 - now, level] = (
                adjoint
                - flux_adv
                - 4.0 * flux_dif
                + east(flux_adv)
                + (east(flux_dif) + west(flux_dif) + north(flux_dif) + south(flux_dif))
                + VERTICAL_MIX * vertical(lambda l: lams[now, l], level, adjoint)
                - drag_ref[level] * slope * adjoint
            )
        return carry

    lax.fori_loop(0, steps, backward, 0)
    for level in range(levels):
        lam_out[level] = lams[steps % 2, level]


def stencil(ext, drag, levels):
    size_r, size_c = ext.shape[1:]
    vmem = pl.BlockSpec(memory_space=pltpu.VMEM)
    plane = jax.ShapeDtypeStruct((levels, size_r, size_c), jnp.float32)
    cells = levels * size_r * size_c
    return pl.pallas_call(
        functools.partial(stencil_kernel, levels, STEPS),
        out_shape=[plane, plane],
        in_specs=[vmem, vmem],
        out_specs=[vmem, vmem],
        scratch_shapes=[
            pltpu.VMEM((STEPS, levels, size_r, size_c), jnp.float32),
            pltpu.VMEM((2, levels, size_r, size_c), jnp.float32),
        ],
        compiler_params=pltpu.CompilerParams(vmem_limit_bytes=48 * 1024 * 1024),
        cost_estimate=pl.CostEstimate(
            flops=60 * STEPS * cells, transcendentals=3 * STEPS * cells, bytes_accessed=28 * cells
        ),
    )(ext, drag)


def drag_law(state):
    return state * jnp.sqrt(state * state + 1.0)


def drag_slope(state):
    square_one = state * state + 1.0
    return (square_one + state * state) / jnp.sqrt(square_one)


def vertical(center):
    zero_row = jnp.zeros_like(center[:1])
    from_above = jnp.concatenate([center[1:] - center[:-1], zero_row], axis=0)
    from_below = jnp.concatenate([zero_row, center[:-1] - center[1:]], axis=0)
    return from_above + from_below


def advance(padded, advect, diffuse, drag_coef):
    center = padded[:, 1:-1, 1:-1]
    upwind = padded[:, :-2, 1:-1]
    downwind = padded[:, 2:, 1:-1]
    left_cell = padded[:, 1:-1, :-2]
    right_cell = padded[:, 1:-1, 2:]
    return (
        center
        + advect * (upwind - center)
        + diffuse * (downwind + upwind + right_cell + left_cell - 4.0 * center)
        + VERTICAL_MIX * vertical(center)
        - drag_coef * drag_law(center)
    )


def retreat(padded, advect_ext, diffuse_ext, drag_coef, state):
    flux_adv = advect_ext * padded
    flux_dif = diffuse_ext * padded
    center = padded[:, 1:-1, 1:-1]
    return (
        center
        - flux_adv[:, 1:-1, 1:-1]
        - 4.0 * flux_dif[:, 1:-1, 1:-1]
        + flux_adv[:, 2:, 1:-1]
        + (
            flux_dif[:, 2:, 1:-1]
            + flux_dif[:, :-2, 1:-1]
            + flux_dif[:, 1:-1, 2:]
            + flux_dif[:, 1:-1, :-2]
        )
        + VERTICAL_MIX * vertical(center)
        - drag_coef * drag_slope(state) * center
    )


def trim(array, margin, wanted):
    excess = margin - wanted
    if excess == 0:
        return array
    return array[:, excess:-excess, excess:-excess]


def profiles(first, starts, widths, period, length, inner):
    cells = jnp.arange(length, dtype=jnp.int32)
    cells = jnp.where(cells < inner, cells, cells - length)
    pos = (first + cells - starts[..., None]) % period
    cell_pos = pos.astype(jnp.float32) - (FP - 1) / 2.0
    profile = jnp.exp(-(cell_pos * cell_pos) / (2.0 * widths[..., None] * widths[..., None]))
    return jnp.where(pos < FP, profile, 0.0)


def level_gain():
    level_pos = jnp.arange(LEV, dtype=jnp.float32) - (LEV - 1) / 2.0
    return DRAG_SCALE * jnp.exp(-0.5 * level_pos * level_pos)


def shards(
    velocity, adjoint_seed, courant, viscosity, turbine_tile, turbine_offset, thrust, disk_width
):
    levels, rows, cols = velocity.shape
    n_gx = lax.axis_size("gx")
    n_gy = lax.axis_size("gy")
    m = MARGIN
    per = thrust.shape[0]
    fields = (
        turbine_tile[:, 0].astype(jnp.float32),
        turbine_offset[:, 0].astype(jnp.float32),
        turbine_offset[:, 1].astype(jnp.float32),
        thrust,
        disk_width,
    )
    info_row = jnp.pad(jnp.concatenate(fields)[None, :], ((0, 0), (0, 128 - len(fields) * per)))
    stack = jnp.concatenate([velocity, courant, viscosity, adjoint_seed], axis=0)
    opened = open_exchange(info_row, halo_pieces(stack, m))
    info = opened[0]
    tiles = info[:, 0:per].astype(jnp.int32)
    row_start = tiles // n_gy * rows + info[:, per : 2 * per].astype(jnp.int32)
    col_start = tiles % n_gy * cols + info[:, 2 * per : 3 * per].astype(jnp.int32)
    thrusts = info[:, 3 * per : 4 * per]
    widths = info[:, 4 * per : 5 * per]
    gx = lax.axis_index("gx")
    gy = lax.axis_index("gy")
    size_r = -(-(rows + 2 * m) // 8) * 8
    size_c = -(-(cols + 2 * m) // 128) * 128
    inner_r = rows + (size_r - rows) // 2
    inner_c = cols + (size_c - cols) // 2
    prof_r = profiles(gx * rows, row_start, widths, n_gx * rows, size_r, inner_r)
    prof_c = profiles(gy * cols, col_start, widths, n_gy * cols, size_c, inner_c)
    gain = level_gain()
    plane = jnp.einsum("dkr,dkc->rc", thrusts[..., None] * prof_r, prof_c, precision=HIGHEST)
    drag = gain[:, None, None] * plane[None]
    ext = assemble(stack, opened[1:], m, size_r, size_c)
    adjoint_full, sens_full = stencil(ext, drag, levels)
    adjoint = adjoint_full[:, :rows, :cols]
    sensitivity = sens_full[:, :rows, :cols]

    weighted = jnp.einsum("l,lrc->rc", gain, sensitivity, precision=HIGHEST)
    own_r = prof_r[..., :rows]
    own_c = prof_c[..., :cols]
    across = jnp.einsum("rc,dkc->dkr", weighted, own_c, precision=HIGHEST)
    totals = jnp.sum(own_r * across, axis=2)
    values = thrusts * totals
    spread = jnp.pad(values, ((0, 0), (0, 128 - per)))
    grad = close_scatter(spread)[0, :per]
    return adjoint, grad


def solution(mesh):
    placed = (
        P(None, "gx", "gy"),
        P(None, "gx", "gy"),
        P(None, "gx", "gy"),
        P(None, "gx", "gy"),
        P(("gx", "gy"), None),
        P(("gx", "gy"), None),
        P(("gx", "gy")),
        P(("gx", "gy")),
    )
    return jax.shard_map(
        shards,
        mesh=mesh,
        in_specs=placed,
        out_specs=(P(None, "gx", "gy"), P(("gx", "gy"))),
        check_vma=False,
    )
```

profile of v0, /device:TPU:1, one launch (start us, length us, event | category | flops | bytes accessed | tf_op | source)
XLA Modules:
  0.0 115.9 jit_solution(16612085427666663612)
XLA Ops:
  0.6 0.8 convert_bitcast_fusion
  1.4 0.7 concatenate.19
  2.1 0.5 pad.8.refs_0_
  2.7 1.0 constant_dynamic-update-slice_fusion.3
  3.7 1.0 constant_dynamic-update-slice_fusion.2
  4.7 1.0 constant_dynamic-update-slice_fusion.1
  5.7 1.0 constant_dynamic-update-slice_fusion
  6.8 0.0 copy-start
  6.8 0.7 reshape.88.refs_1_
  7.5 0.6 reshape.89.refs_2_
  8.2 1.7 %slice_bitcast_fusion = (f32[12,14,256]{1,2,0:T(8,128)S(1)}, f32[12,14,256]{1,2,0:T(8,128)}) fusion(f32[12,256,128]{2,1,0:T(8,128)S(1)} %constant_dynamic-update-slice_fusion), kind=kLoop, calls=%fused_computation.1 | loop fusion | bytes 688128 | tf_op jit(solution)/shard_map/transpose | solution.py:158
  9.8 1.9 %copy.69 = f32[12,14,256]{2,1,0:T(8,128)S(1)} copy(f32[12,14,256]{1,2,0:T(8,128)} %get-tuple-element.31) | data formatting | bytes 344064 | tf_op jit(solution)/shard_map/transpose | solution.py:157
  11.7 0.7 reshape.90.refs_3_
  12.4 0.5 copy.70
  12.9 0.7 reshape.91.refs_4_
  13.6 0.0 copy-done
  13.6 0.1 fusion.32
  13.7 0.6 reshape.108.refs_5_
  14.4 0.6 reshape.109.refs_6_
  15.0 0.7 reshape.110.refs_7_
  15.6 0.6 reshape.111.refs_8_
  16.3 32.1 %shard_map.95 = (f32[128,128]{1,0:T(8,128)}, f32[168,128]{1,0:T(8,128)}, f32[168,128]{1,0:T(8,128)}, f32[168,256]{1,0:T(8,128)}, f32[168,256]{1,0:T(8,128)}, /*i...) custom-call(f32[1,128]{1,0:T(1,128)} %pad.8.refs_0_, f32[168,128]{1,0:T(8,128)} %reshape.88.refs_1_, ...), custom_call_target="tpu_custom_call" | custom-call | tf_op jit(solution)/shard_map/pallas_call | solution.py:102
  48.4 1.5 %reshape.115 = f32[12,14,14]{2,1,0:T(8,128)} reshape(f32[168,14]{1,0:T(8,128)} %get-tuple-element.20) | data formatting | bytes 18816 | tf_op jit(solution)/shard_map/reshape | solution.py:175
  49.9 1.5 %reshape.114 = f32[12,14,14]{2,1,0:T(8,128)} reshape(f32[168,14]{1,0:T(8,128)} %get-tuple-element.19) | data formatting | bytes 18816 | tf_op jit(solution)/shard_map/reshape | solution.py:175
  51.5 1.5 %reshape.101 = f32[12,14,128]{2,1,0:T(8,128)} reshape(f32[168,128]{1,0:T(8,128)} %get-tuple-element.18) | data formatting | bytes 172032 | tf_op jit(solution)/shard_map/reshape | solution.py:175
  53.0 1.5 %reshape.113 = f32[12,14,14]{2,1,0:T(8,128)} reshape(f32[168,14]{1,0:T(8,128)} %get-tuple-element.17) | data formatting | bytes 18816 | tf_op jit(solution)/shard_map/reshape | solution.py:175
  54.5 1.5 %reshape.112 = f32[12,14,14]{2,1,0:T(8,128)} reshape(f32[168,14]{1,0:T(8,128)} %get-tuple-element.16) | data formatting | bytes 18816 | tf_op jit(solution)/shard_map/reshape | solution.py:175
  56.1 1.5 %reshape.98 = f32[12,14,128]{2,1,0:T(8,128)} reshape(f32[168,128]{1,0:T(8,128)} %get-tuple-element.15) | data formatting | bytes 172032 | tf_op jit(solution)/shard_map/reshape | solution.py:175
  57.6 0.9 reshape.97
  58.5 1.7 %copy.80 = f32[12,14,256]{1,2,0:T(8,128)} copy(f32[12,14,256]{2,1,0:T(8,128)S(1)} %reshape.97) | data formatting | bytes 344064 | tf_op jit(solution)/shard_map/reshape | solution.py:175
  60.2 0.9 reshape.96
  61.1 1.7 %copy.79 = f32[12,14,256]{1,2,0:T(8,128)} copy(f32[12,14,256]{2,1,0:T(8,128)S(1)} %reshape.96) | data formatting | bytes 344064 | tf_op jit(solution)/shard_map/reshape | solution.py:175
  62.8 0.1 pad.18.clone
  62.9 0.1 pad.12.clone
  63.0 0.0 copy-start.1
  63.0 4.5 %maximum_maximum_fusion.ext_ref = f32[12,288,256]{2,1,0:T(8,128)S(1)} fusion(f32[12,14,14]{2,1,0:T(8,128)} %reshape.115, f32[12,14,100]{2,1,0:T(8,128)S(1)} %broadcast.97, f32[12,14,14]{2,1,0:T(8,128)} %reshape.114, f32[12,14,128]{2,1,0:T(8,128)} %reshape.101, f32[12,14,14]{2,1,0:T(8,128)} %reshape.113, f32[12,14,14]{2,1,0:T(8,128)} %reshape.112, ...), kind=kLoop, calls=%fused_computation | loop fusion | flops 10616832 | bytes 6028800 | tf_op jit(solution)/shard_map/concatenate | solution.py:187
  67.6 0.0 copy-done.1
  67.6 0.7 multiply_multiply_fusion
  68.3 1.5 %copy.89 = f32[128,4]{0,1:T(4,128)} copy(f32[128,4]{1,0:T(8,128)} %get-tuple-element.35) | data formatting | bytes 4096 | tf_op jit(solution)/shard_map/slice | solution.py:387
  69.8 0.9 copy.93
  70.7 1.7 %fusion.11 = (s32[128,4]{1,0:T(8,128)}, pred[128,4]{1,0:T(8,128)(4,1)S(1)}) fusion(f32[128,128]{1,0:T(8,128)} %get-tuple-element.21), kind=kLoop, calls=%fused_computation.35 | loop fusion | flops 7680 | bytes 6656 | tf_op jit(solution)/shard_map/add | solution.py:386
  72.3 1.6 %fusion.9 = s32[128,4]{1,0:T(8,128)} fusion(f32[128,128]{1,0:T(8,128)} %get-tuple-element.21, pred[128,4]{1,0:T(8,128)(4,1)S(1)} %get-tuple-element.25), kind=kLoop, calls=%fused_computation.33 | loop fusion | flops 7680 | bytes 6656 | tf_op jit(solution)/shard_map/add | solution.py:385
  74.0 0.9 copy.91
  74.9 0.9 copy.95
  75.8 3.0 %convolution_bitcast_fusion = f32[288,256]{1,0:T(8,128)S(1)} fusion(f32[128,4]{0,1:T(4,128)} %copy.89, f32[128,4]{0,1:T(4,128)S(1)} %copy.93, s32[128,4]{0,1:T(4,128)S(1)} %copy.91, s32[288]{0:T(512)S(1)} %fusion.14, s32[128,4]{0,1:T(4,128)S(1)} %copy.95, s32[256]{0:T(256)S(1)} %fusion.15), kind=kOutput, calls=%fused_computation.9 | convolution fusion | flops 458424320 | bytes 305280 | tf_op jit(solution)/shard_map/dkr,dkc->rc/dot_general | solution.py:398
  78.8 0.1 broadcast_multiply_fusion.drag_ref
  79.0 18.7 %shard_map.96 = (f32[3,288,256]{2,1,0:T(8,128)S(1)}, f32[3,288,256]{2,1,0:T(8,128)S(1)}) custom-call(f32[12,288,256]{2,1,0:T(8,128)S(1)} %maximum_maximum_fusion.ext_ref, f32[3,288,256]{2,1,0:T(8,128)S(1)} %broadcast_multiply_fusion.drag_ref), custom_call_target="tpu_custom_call" | custom-call | flops 106168320 | bytes 6193152 | tf_op jit(solution)/shard_map/pallas_call | solution.py:277
  97.7 0.0 copy-start.2
  97.7 0.8 slice.79
  98.5 1.2 fusion.4
  99.6 0.6 exponential_select_fusion
  100.3 0.4 exponential_select_fusion.1
  100.7 0.7 fusion
  101.4 0.1 copy.98
  101.5 0.0 copy-done.2
  101.5 0.1 slice_multiply_fusion
  101.6 0.6 pad.9.src_ref
  102.2 12.6 %shard_map.97 = f32[1,128]{1,0:T(1,128)} custom-call(f32[128,128]{1,0:T(8,128)} %pad.9.src_ref), custom_call_target="tpu_custom_call" | custom-call | tf_op jit(solution)/shard_map/pallas_call | solution.py:139
  114.8 1.1 slice_bitcast_fusion.2
  (8 shorter events, 0.1 us)
Async XLA Ops:
  6.8 6.8 %copy-start = (f32[12,256,128]{2,1,0:T(8,128)}, f32[12,256,128]{2,1,0:T(8,128)S(1)}, u32[]{:S(2)}) copy-start(f32[12,256,128]{2,1,0:T(8,128)S(1)} %constant_dynamic-update-slice_fusion) | copy-start | bytes 4718596
  63.0 4.5 %copy-start.1 = (f32[128,128]{1,0:T(8,128)S(1)}, f32[128,128]{1,0:T(8,128)}, u32[]{:S(2)}) copy-start(f32[128,128]{1,0:T(8,128)} %get-tuple-element.21) | copy-start | bytes 196612
  97.7 3.8 %copy-start.2 = (f32[128,128]{1,0:T(8,128)S(1)}, f32[128,128]{1,0:T(8,128)}, u32[]{:S(2)}) copy-start(f32[128,128]{1,0:T(8,128)} %get-tuple-element.21) | copy-start | bytes 196612
where the time goes:
time: 117 us; the launch traced here: 116 us
  Pallas kernels  63.4 us (54%)
  local copies, waits for them, and re-layouts  36.3 us (31%)
  other arithmetic  10.6 us (9%)
  matrix products  4.83 us (4%)
    pallas_call x1, Pallas kernels, open_exchange(): pl.pallas_call(functools.partial(open_kernel, n_gx, n_gy), out_shape=out_...  32.1 us
    pallas_call x1, Pallas kernels, stencil(): pl.pallas_call(functools.partial(stencil_kernel, levels, STEPS), out_shap...  18.7 us
    reshape x10, local copies, waits for them, and re-layouts, assemble(): piece.reshape(depth, m, piece.shape[1])  14.4 us
    pallas_call x1, Pallas kernels, close_scatter(): pl.pallas_call(functools.partial(close_kernel, n_gy, n_dev), out_shape=ja...  12.6 us
    reshape x8, local copies, waits for them, and re-layouts, halo_pieces(): return tuple((piece.reshape(depth * m, piece.shape[2]) for piece in pieces))  5.32 us
    concatenate x1, other arithmetic, assemble(): jnp.concatenate([band(block, col_high, col_low), band(row_high, c_hh, c_h...  4.51 us
    unnamed x9, local copies, waits for them, and re-layouts  3.08 us
    dot_general x1, matrix products, shards(): jnp.einsum('dkr,dkc->rc', thrusts[..., None] * prof_r, prof_c, precision=...  3 us

commit v1 on v0

--- a/solution.py
+++ b/solution.py
@@ -10,7 +10,7 @@
 LEV = 3
 STEPS = 8
 FP = 64
-MARGIN = 2 * (STEPS - 1)
+MARGIN = 2 * STEPS
 
 VERTICAL_MIX = 0.05
 DRAG_SCALE = 0.01
@@ -152,28 +152,22 @@
 
 
 def halo_pieces(block, m):
-    depth = block.shape[0]
     last_r, first_r = block[:, -m:, :], block[:, :m, :]
-    last_c = jnp.swapaxes(block[:, :, -m:], 1, 2)
-    first_c = jnp.swapaxes(block[:, :, :m], 1, 2)
-    pieces = (
+    return (
         last_r,
         first_r,
-        last_c,
-        first_c,
+        jnp.swapaxes(block[:, :, -m:], 1, 2),
+        jnp.swapaxes(block[:, :, :m], 1, 2),
         last_r[:, :, -m:],
         last_r[:, :, :m],
         first_r[:, :, -m:],
         first_r[:, :, :m],
     )
-    return tuple(piece.reshape(depth * m, piece.shape[2]) for piece in pieces)
 
 
 def assemble(block, landed, m, size_r, size_c):
     depth, rows, cols = block.shape
-    row_low, row_high, col_low, col_high, c_ll, c_lh, c_hl, c_hh = (
-        piece.reshape(depth, m, piece.shape[1]) for piece in landed
-    )
+    row_low, row_high, col_low, col_high, c_ll, c_lh, c_hl, c_hh = landed
     col_low = jnp.swapaxes(col_low, 1, 2)
     col_high = jnp.swapaxes(col_high, 1, 2)
     gap_c = size_c - cols - 2 * m
@@ -183,16 +177,11 @@
         fill = jnp.zeros(left.shape[:2] + (gap_c,), jnp.float32)
         return jnp.concatenate([left, middle, fill, right], axis=2)
 
-    fill = jnp.zeros((depth, gap_r, size_c), jnp.float32)
-    return jnp.concatenate(
-        [
-            band(block, col_high, col_low),
-            band(row_high, c_hh, c_hl),
-            fill,
-            band(row_low, c_lh, c_ll),
-        ],
-        axis=1,
-    )
+    parts = [band(block, col_high, col_low), band(row_high, c_hh, c_hl)]
+    if gap_r:
+        parts.append(jnp.zeros((depth, gap_r, size_c), jnp.float32))
+    parts.append(band(row_low, c_lh, c_ll))
+    return jnp.concatenate(parts, axis=1)
 
 
 def stencil_kernel(levels, steps, ext_ref, drag_ref, lam_out, sens_out, states, lams):

time: 117 us -> 107 us (0.915)
  local copies, waits for them, and re-layouts: 36.3 us -> 24.4 us
  Pallas kernels: 63.4 us -> 65.6 us
    reshape x18 -> x0, local copies, waits for them, and re-layouts: 19.7 us -> none  [the longest x10 14.4 us: assemble(): piece.reshape(depth, m, piece.shape[1])]
    pallas_call x0 -> x2, local copies, waits for them, and re-layouts: none -> 5.12 us  [open_exchange(): pl.pallas_call(functools.partial(open_kernel, n_gx, n_gy), out_shape=out_...]
    pallas_call x1, Pallas kernels: 32.1 us -> 34.4 us  [open_exchange(): pl.pallas_call(functools.partial(open_kernel, n_gx, n_gy), out_shape=out_...]
    transpose x3, local copies, waits for them, and re-layouts: 4.03 us -> 5.33 us  [the longest x2 2.81 us: halo_pieces(): jnp.swapaxes(block[:, :, :m], 1, 2)]
where the time goes in v1:
time: 107 us; the launch traced here: 106 us
  Pallas kernels  65.6 us (61%)
  local copies, waits for them, and re-layouts  24.4 us (23%)
  other arithmetic  10.5 us (10%)
  matrix products  4.83 us (5%)
    pallas_call x1, Pallas kernels, open_exchange(): pl.pallas_call(functools.partial(open_kernel, n_gx, n_gy), out_shape=out_...  34.4 us
    pallas_call x1, Pallas kernels, stencil(): pl.pallas_call(functools.partial(stencil_kernel, levels, STEPS), out_shap...  18.7 us
    pallas_call x1, Pallas kernels, close_scatter(): pl.pallas_call(functools.partial(close_kernel, n_gy, n_dev), out_shape=ja...  12.6 us
    pallas_call x2, local copies, waits for them, and re-layouts, open_exchange(): pl.pallas_call(functools.partial(open_kernel, n_gx, n_gy), out_shape=out_...  5.12 us
    concatenate x1, other arithmetic, assemble(): return jnp.concatenate(parts, axis=1)  4.42 us
    unnamed x9, local copies, waits for them, and re-layouts  3.08 us
    dot_general x1, matrix products, shards(): jnp.einsum('dkr,dkc->rc', thrusts[..., None] * prof_r, prof_c, precision=...  3 us
    transpose x2, local copies, waits for them, and re-layouts, halo_pieces(): jnp.swapaxes(block[:, :, :m], 1, 2)  2.81 us

profile of v1, /device:TPU:1, one launch (start us, length us, event | category | flops | bytes accessed | tf_op | source)
XLA Modules:
  0.0 106.1 jit_solution(7621285013272438343)
XLA Ops:
  0.6 0.8 convert_bitcast_fusion
  1.4 0.7 concatenate.19
  2.1 0.5 pad.8.refs_0_
  2.7 1.0 constant_dynamic-update-slice_fusion.3
  3.7 1.0 constant_dynamic-update-slice_fusion.2
  4.7 1.0 constant_dynamic-update-slice_fusion.1
  5.7 1.0 constant_dynamic-update-slice_fusion
  6.8 0.0 copy-start
  6.8 0.7 fusion.33
  7.5 1.7 %slice_bitcast_fusion = (f32[12,16,256]{1,2,0:T(8,128)S(1)}, f32[12,16,256]{1,2,0:T(8,128)}) fusion(f32[12,256,128]{2,1,0:T(8,128)S(1)} %constant_dynamic-update-slice_fusion), kind=kLoop, calls=%fused_computation.1 | loop fusion | bytes 786432 | tf_op jit(solution)/shard_map/transpose | solution.py:160
  9.2 2.5 %copy.31.refs_3_ = f32[12,16,256]{2,1,0:T(8,128)} copy(f32[12,16,256]{1,2,0:T(8,128)} %get-tuple-element.31) | data formatting | bytes 393216 | tf_op jit(solution)/shard_map/transpose | solution.py:159
  11.7 1.1 %copy.32.refs_4_ = f32[12,16,256]{2,1,0:T(8,128)} copy(f32[12,16,256]{1,2,0:T(8,128)S(1)} %get-tuple-element.30) | data formatting | bytes 393216 | tf_op jit(solution)/shard_map/transpose | solution.py:160
  12.9 0.0 copy-done
  12.9 0.8 fusion.32
  13.7 34.4 %shard_map.95 = (f32[128,128]{1,0:T(8,128)}, f32[12,16,128]{2,1,0:T(8,128)}, f32[12,16,128]{2,1,0:T(8,128)}, f32[12,16,256]{2,1,0:T(8,128)}, f32[12,16,256]{2,1,...) custom-call(f32[1,128]{1,0:T(1,128)} %pad.8.refs_0_, ...), custom_call_target="tpu_custom_call" | custom-call | tf_op jit(solution)/shard_map/pallas_call | solution.py:102
  48.1 2.6 %copy.34 = f32[12,16,256]{1,2,0:T(8,128)} copy(f32[12,16,256]{2,1,0:T(8,128)} %get-tuple-element.14) | data formatting | bytes 393216 | tf_op jit(solution)/shard_map/pallas_call | solution.py:102
  50.6 2.6 %copy.33 = f32[12,16,256]{1,2,0:T(8,128)} copy(f32[12,16,256]{2,1,0:T(8,128)} %get-tuple-element.13) | data formatting | bytes 393216 | tf_op jit(solution)/shard_map/pallas_call | solution.py:102
  53.2 0.1 pad.12.clone
  53.3 0.0 copy-start.1
  53.3 4.4 %maximum_maximum_fusion.ext_ref = f32[12,288,256]{2,1,0:T(8,128)S(1)} fusion(f32[12,16,16]{2,1,0:T(8,128)} %get-tuple-element.20, f32[12,16,96]{2,1,0:T(8,128)S(1)} %broadcast.97, f32[12,16,16]{2,1,0:T(8,128)} %get-tuple-element.19, f32[12,16,128]{2,1,0:T(8,128)} %get-tuple-element.18, f32[12,16,16]{2,1,0:T(8,128)} %get-tuple-element.17, ...), kind=kLoop, calls=%fused_computation | loop fusion | flops 9732096 | bytes 6119424 | tf_op jit(solution)/shard_map/concatenate | solution.py:184
  57.8 0.0 copy-done.1
  57.8 0.7 multiply_multiply_fusion
  58.5 1.5 %copy.35 = f32[128,4]{0,1:T(4,128)} copy(f32[128,4]{1,0:T(8,128)} %get-tuple-element.35) | data formatting | bytes 4096 | tf_op jit(solution)/shard_map/slice | solution.py:376
  60.0 0.9 copy.39
  60.9 1.7 %fusion.11 = (s32[128,4]{1,0:T(8,128)}, pred[128,4]{1,0:T(8,128)(4,1)S(1)}) fusion(f32[128,128]{1,0:T(8,128)} %get-tuple-element.21), kind=kLoop, calls=%fused_computation.35 | loop fusion | flops 7680 | bytes 6656 | tf_op jit(solution)/shard_map/add | solution.py:375
  62.5 1.6 %fusion.9 = s32[128,4]{1,0:T(8,128)} fusion(f32[128,128]{1,0:T(8,128)} %get-tuple-element.21, pred[128,4]{1,0:T(8,128)(4,1)S(1)} %get-tuple-element.25), kind=kLoop, calls=%fused_computation.33 | loop fusion | flops 7680 | bytes 6656 | tf_op jit(solution)/shard_map/add | solution.py:374
  64.2 0.9 copy.37
  65.1 0.9 copy.41
  66.0 3.0 %convolution_bitcast_fusion = f32[288,256]{1,0:T(8,128)S(1)} fusion(f32[128,4]{0,1:T(4,128)} %copy.35, f32[128,4]{0,1:T(4,128)S(1)} %copy.39, s32[128,4]{0,1:T(4,128)S(1)} %copy.37, s32[288]{0:T(512)S(1)} %fusion.14, s32[128,4]{0,1:T(4,128)S(1)} %copy.41, s32[256]{0:T(256)S(1)} %fusion.15), kind=kOutput, calls=%fused_computation.9 | convolution fusion | flops 458424320 | bytes 305280 | tf_op jit(solution)/shard_map/dkr,dkc->rc/dot_general | solution.py:387
  69.0 0.1 broadcast_multiply_fusion.drag_ref
  69.2 18.7 %shard_map.96 = (f32[3,288,256]{2,1,0:T(8,128)S(1)}, f32[3,288,256]{2,1,0:T(8,128)S(1)}) custom-call(f32[12,288,256]{2,1,0:T(8,128)S(1)} %maximum_maximum_fusion.ext_ref, f32[3,288,256]{2,1,0:T(8,128)S(1)} %broadcast_multiply_fusion.drag_ref), custom_call_target="tpu_custom_call" | custom-call | flops 106168320 | bytes 6193152 | tf_op jit(solution)/shard_map/pallas_call | solution.py:266
  87.9 0.0 copy-start.2
  87.9 0.8 slice.79
  88.7 1.2 %fusion.4 = f32[1,256,128]{2,0,1:T(1,128)S(1)} fusion(f32[3,256,128]{2,1,0:T(8,128)S(1)} %slice.82), kind=kOutput, calls=%fused_computation.20 | convolution fusion | flops 1179660 | bytes 524288 | tf_op jit(solution)/shard_map/l,lrc->rc/dot_general | solution.py:394
  89.8 0.6 exponential_select_fusion
  90.5 0.4 exponential_select_fusion.1
  90.9 0.7 fusion
  91.6 0.1 copy.44
  91.7 0.0 copy-done.2
  91.7 0.1 slice_multiply_fusion
  91.8 0.6 pad.9.src_ref
  92.4 12.6 %shard_map.97 = f32[1,128]{1,0:T(1,128)} custom-call(f32[128,128]{1,0:T(8,128)} %pad.9.src_ref), custom_call_target="tpu_custom_call" | custom-call | tf_op jit(solution)/shard_map/pallas_call | solution.py:139
  105.0 1.1 %slice_bitcast_fusion.2 = f32[4]{0:T(128)} fusion(f32[1,128]{1,0:T(1,128)} %shard_map.97), kind=kLoop, calls=%fused_computation.52 | loop fusion | bytes 32 | tf_op jit(solution)/shard_map/squeeze | solution.py:401
  (6 shorter events, 0.1 us)
Async XLA Ops:
  6.8 6.1 %copy-start = (f32[12,256,128]{2,1,0:T(8,128)}, f32[12,256,128]{2,1,0:T(8,128)S(1)}, u32[]{:S(2)}) copy-start(f32[12,256,128]{2,1,0:T(8,128)S(1)} %constant_dynamic-update-slice_fusion) | copy-start | bytes 4718596
  53.3 4.4 %copy-start.1 = (f32[128,128]{1,0:T(8,128)S(1)}, f32[128,128]{1,0:T(8,128)}, u32[]{:S(2)}) copy-start(f32[128,128]{1,0:T(8,128)} %get-tuple-element.21) | copy-start | bytes 196612
  87.9 3.8 %copy-start.2 = (f32[128,128]{1,0:T(8,128)S(1)}, f32[128,128]{1,0:T(8,128)}, u32[]{:S(2)}) copy-start(f32[128,128]{1,0:T(8,128)} %get-tuple-element.21) | copy-start | bytes 196612

commit v2 on v1

--- a/solution.py
+++ b/solution.py
@@ -165,27 +165,35 @@
     )
 
 
-def assemble(block, landed, m, size_r, size_c):
-    depth, rows, cols = block.shape
+def column_band(landed, m, size_r, size_c, cols):
     row_low, row_high, col_low, col_high, c_ll, c_lh, c_hl, c_hh = landed
-    col_low = jnp.swapaxes(col_low, 1, 2)
-    col_high = jnp.swapaxes(col_high, 1, 2)
-    gap_c = size_c - cols - 2 * m
-    gap_r = size_r - rows - 2 * m
-
-    def band(left, middle, right):
-        fill = jnp.zeros(left.shape[:2] + (gap_c,), jnp.float32)
-        return jnp.concatenate([left, middle, fill, right], axis=2)
-
-    parts = [band(block, col_high, col_low), band(row_high, c_hh, c_hl)]
-    if gap_r:
-        parts.append(jnp.zeros((depth, gap_r, size_c), jnp.float32))
-    parts.append(band(row_low, c_lh, c_ll))
-    return jnp.concatenate(parts, axis=1)
-
-
-def stencil_kernel(levels, steps, ext_ref, drag_ref, lam_out, sens_out, states, lams):
+    depth = col_low.shape[0]
+    width = size_c - cols
+    span = -(-size_r // 128) * 128
+
+    def edge(column, high_corner, low_corner):
+        fill = jnp.zeros((depth, m, span - size_r), jnp.float32)
+        return jnp.concatenate(
+            [column, jnp.swapaxes(high_corner, 1, 2), jnp.swapaxes(low_corner, 1, 2), fill],
+            axis=2,
+        )
+
+    fill = jnp.zeros((depth, width - 2 * m, span), jnp.float32)
+    return jnp.concatenate([edge(col_high, c_hh, c_lh), fill, edge(col_low, c_hl, c_ll)], axis=1)
+
+
+def stencil_kernel(
+    levels, steps, block_ref, high_ref, low_ref, band_ref, drag_ref, lam_out, sens_out,
+    ext_ref, states, lams,
+):
     size_r, size_c = ext_ref.shape[1:]
+    rows, cols = block_ref.shape[1:]
+    m = high_ref.shape[1]
+    for depth in range(ext_ref.shape[0]):
+        ext_ref[depth, :rows, :cols] = block_ref[depth]
+        ext_ref[depth, rows : rows + m, :cols] = high_ref[depth]
+        ext_ref[depth, size_r - m :, :cols] = low_ref[depth]
+        ext_ref[depth, :, cols:] = band_ref[depth].T[:size_r]
 
     def west(x):
         return pltpu.roll(x, 1, 0)
@@ -258,17 +266,19 @@
         lam_out[level] = lams[steps % 2, level]
 
 
-def stencil(ext, drag, levels):
-    size_r, size_c = ext.shape[1:]
+def stencil(block, landed, band, drag, levels):
+    size_r, size_c = drag.shape[1:]
+    depth = block.shape[0]
     vmem = pl.BlockSpec(memory_space=pltpu.VMEM)
     plane = jax.ShapeDtypeStruct((levels, size_r, size_c), jnp.float32)
     cells = levels * size_r * size_c
     return pl.pallas_call(
         functools.partial(stencil_kernel, levels, STEPS),
         out_shape=[plane, plane],
-        in_specs=[vmem, vmem],
+        in_specs=[vmem] * 5,
         out_specs=[vmem, vmem],
         scratch_shapes=[
+            pltpu.VMEM((depth, size_r, size_c), jnp.float32),
             pltpu.VMEM((STEPS, levels, size_r, size_c), jnp.float32),
             pltpu.VMEM((2, levels, size_r, size_c), jnp.float32),
         ],
@@ -276,7 +286,7 @@
         cost_estimate=pl.CostEstimate(
             flops=60 * STEPS * cells, transcendentals=3 * STEPS * cells, bytes_accessed=28 * cells
         ),
-    )(ext, drag)
+    )(block, landed[1], landed[0], band, drag)
 
 
 def drag_law(state):
@@ -386,8 +396,8 @@
     gain = level_gain()
     plane = jnp.einsum("dkr,dkc->rc", thrusts[..., None] * prof_r, prof_c, precision=HIGHEST)
     drag = gain[:, None, None] * plane[None]
-    ext = assemble(stack, opened[1:], m, size_r, size_c)
-    adjoint_full, sens_full = stencil(ext, drag, levels)
+    band = column_band(opened[1:], m, size_r, size_c, cols)
+    adjoint_full, sens_full = stencil(stack, opened[1:], band, drag, levels)
     adjoint = adjoint_full[:, :rows, :cols]
     sensitivity = sens_full[:, :rows, :cols]
 

time: 107 us -> 95.2 us (0.89)
  local copies, waits for them, and re-layouts: 24.4 us -> 16.7 us
  other arithmetic: 10.5 us -> 4.45 us
  Pallas kernels: 65.6 us -> 68.6 us
    pallas_call x1, Pallas kernels: 18.7 us -> 21.6 us  [stencil(): pl.pallas_call(functools.partial(stencil_kernel, levels, STEPS), out_shap...]
    concatenate x1, other arithmetic: 4.42 us -> 2.85 us  [column_band(): jnp.concatenate([edge(col_high, c_hh, c_lh), fill, edge(col_low, c_hl, c_...]
    add x1, other arithmetic: 1.63 us -> 0.09 us  [shards(): row_start = tiles // n_gy * rows + info[:, per:2 * per].astype(jnp.int32)]
    add x1, other arithmetic: 1.65 us -> 0.11 us  [shards(): col_start = tiles % n_gy * cols + info[:, 2 * per:3 * per].astype(jnp.int32)]
    slice x1, local copies, waits for them, and re-layouts: 1.47 us -> 0.06 us  [shards(): thrusts = info[:, 3 * per:4 * per]]
    pallas_call x2 -> x4, local copies, waits for them, and re-layouts: 5.12 us -> 3.9 us  [open_exchange(): pl.pallas_call(functools.partial(open_kernel, n_gx, n_gy), out_shape=out_...]
    unnamed x9 -> x21, local copies, waits for them, and re-layouts: 3.08 us -> 2.18 us
where the time goes in v2:
time: 95.2 us; the launch traced here: 94.8 us
  Pallas kernels  68.6 us (72%)
  local copies, waits for them, and re-layouts  16.7 us (18%)
  other arithmetic  4.45 us (5%)
  matrix products  4.14 us (4%)
    pallas_call x1, Pallas kernels, open_exchange(): pl.pallas_call(functools.partial(open_kernel, n_gx, n_gy), out_shape=out_...  34.3 us
    pallas_call x1, Pallas kernels, stencil(): pl.pallas_call(functools.partial(stencil_kernel, levels, STEPS), out_shap...  21.6 us
    pallas_call x1, Pallas kernels, close_scatter(): pl.pallas_call(functools.partial(close_kernel, n_gy, n_dev), out_shape=ja...  12.6 us
    pallas_call x4, local copies, waits for them, and re-layouts, open_exchange(): pl.pallas_call(functools.partial(open_kernel, n_gx, n_gy), out_shape=out_...  3.9 us
    concatenate x1, other arithmetic, column_band(): jnp.concatenate([edge(col_high, c_hh, c_lh), fill, edge(col_low, c_hl, c_...  2.85 us
    transpose x2, local copies, waits for them, and re-layouts, halo_pieces(): jnp.swapaxes(block[:, :, :m], 1, 2)  2.83 us
    transpose x1, local copies, waits for them, and re-layouts, halo_pieces(): jnp.swapaxes(block[:, :, -m:], 1, 2)  2.52 us
    dot_general x1, matrix products, shards(): jnp.einsum('dkr,dkc->rc', thrusts[..., None] * prof_r, prof_c, precision=...  2.33 us

profile of v2, /device:TPU:1, one launch (start us, length us, event | category | flops | bytes accessed | tf_op | source)
XLA Modules:
  0.0 94.8 jit_solution(6806330691535473881)
XLA Ops:
  0.6 0.0 copy-start.3
  0.6 0.0 copy-start.4
  0.7 0.0 copy-start.5
  0.7 0.0 copy-start.6
  0.7 0.0 copy-start.7
  0.7 0.0 copy-start.8
  0.7 1.1 %constant_dynamic-update-slice_fusion.3 = f32[12,256,128]{2,1,0:T(8,128)S(1)} fusion(f32[3,256,128]{2,1,0:T(8,128)} %param.8), kind=kLoop, calls=%fused_computation.43 | loop fusion | bytes 786432
  1.8 1.0 %constant_dynamic-update-slice_fusion.2 = f32[12,256,128]{2,1,0:T(8,128)S(1)} fusion(f32[12,256,128]{2,1,0:T(8,128)S(1)} %constant_dynamic-update-slice_fusion.3, f32[3,256,128]{2,1,0:T(8,128)} %param.10), kind=kLoop, calls=%fused_computation.42 | loop fusion | bytes 786432
  2.8 0.0 copy-done.3
  2.9 0.0 copy-done.4
  2.9 0.0 copy-done.5
  2.9 0.0 copy-done.6
  2.9 0.0 copy-done.7
  2.9 0.0 copy-done.8
  3.0 0.1 concatenate.16
  3.0 0.5 pad.8.refs_0_
  3.6 0.7 fusion.33
  4.2 1.7 %slice_bitcast_fusion = (f32[12,16,256]{1,2,0:T(8,128)S(1)}, f32[12,16,256]{1,2,0:T(8,128)}) fusion(f32[12,256,128]{2,1,0:T(8,128)S(1)} %constant_dynamic-update-slice_fusion.block_ref), kind=kLoop, calls=%fused_computation.1 | loop fusion | bytes 786432 | tf_op jit(solution)/shard_map/transpose | solution.py:160
  6.0 2.5 %copy.35.refs_3_ = f32[12,16,256]{2,1,0:T(8,128)} copy(f32[12,16,256]{1,2,0:T(8,128)} %get-tuple-element.31) | data formatting | bytes 393216 | tf_op jit(solution)/shard_map/transpose | solution.py:159
  8.5 1.1 %copy.36.refs_4_ = f32[12,16,256]{2,1,0:T(8,128)} copy(f32[12,16,256]{1,2,0:T(8,128)S(1)} %get-tuple-element.30) | data formatting | bytes 393216 | tf_op jit(solution)/shard_map/transpose | solution.py:160
  9.6 0.8 fusion.32
  10.5 34.3 %shard_map.95 = (f32[128,128]{1,0:T(8,128)}, f32[12,16,128]{2,1,0:T(8,128)}, f32[12,16,128]{2,1,0:T(8,128)}, f32[12,16,256]{2,1,0:T(8,128)}, f32[12,16,256]{2,1,...) custom-call(f32[1,128]{1,0:T(1,128)} %pad.8.refs_0_, ...), custom_call_target="tpu_custom_call" | custom-call | tf_op jit(solution)/shard_map/pallas_call | solution.py:102
  44.8 1.0 %copy.40 = f32[12,16,16]{1,2,0:T(8,128)S(1)} copy(f32[12,16,16]{2,1,0:T(8,128)} %get-tuple-element.20) | data formatting | bytes 24576 | tf_op jit(solution)/shard_map/pallas_call | solution.py:102
  45.7 1.0 %copy.39 = f32[12,16,16]{1,2,0:T(8,128)S(1)} copy(f32[12,16,16]{2,1,0:T(8,128)} %get-tuple-element.19) | data formatting | bytes 24576 | tf_op jit(solution)/shard_map/pallas_call | solution.py:102
  46.7 1.0 %copy.38 = f32[12,16,16]{1,2,0:T(8,128)S(1)} copy(f32[12,16,16]{2,1,0:T(8,128)} %get-tuple-element.17) | data formatting | bytes 24576 | tf_op jit(solution)/shard_map/pallas_call | solution.py:102
  47.7 1.0 %copy.37 = f32[12,16,16]{1,2,0:T(8,128)S(1)} copy(f32[12,16,16]{2,1,0:T(8,128)} %get-tuple-element.16) | data formatting | bytes 24576 | tf_op jit(solution)/shard_map/pallas_call | solution.py:102
  48.7 0.1 pad.14.clone
  48.8 0.0 copy-start.2
  48.8 2.9 %maximum_maximum_fusion.band_ref = f32[12,128,384]{2,1,0:T(8,128)} fusion(f32[12,16,96]{2,1,0:T(8,128)S(1)} %broadcast.97, f32[12,16,16]{2,1,0:T(8,128)S(1)} %bitcast.27, f32[12,16,16]{2,1,0:T(8,128)S(1)} %bitcast.28, f32[12,16,256]{2,1,0:T(8,128)} %get-tuple-element.18, f32[12,16,16]{2,1,0:T(8,128)S(1)} %bitcast.29, f32[12,16,16]{2,1,0:T(8,128)S(1)} %bitcast.30, ...), kind=kLoop, calls=%fused_computation | loop fusion | flops 4718592 | bytes 2875904 | tf_op jit(solution)/shard_map/concatenate | solution.py:182
  51.6 0.0 copy-done.2
  51.6 0.1 multiply_multiply_fusion
  51.7 0.1 copy.41
  51.8 0.1 copy.45
  51.9 0.1 fusion.11
  52.0 0.1 fusion.9
  52.1 0.1 copy.43
  52.2 0.1 copy.47
  52.2 0.0 copy-start
  52.2 0.0 copy-start.1
  52.3 2.3 %convolution_bitcast_fusion = f32[288,256]{1,0:T(8,128)S(1)} fusion(f32[128,4]{0,1:T(4,128)S(1)} %copy.41, f32[128,4]{0,1:T(4,128)S(1)} %copy.45, s32[128,4]{0,1:T(4,128)S(1)} %copy.43, s32[288]{0:T(512)S(1)} %fusion.14, s32[128,4]{0,1:T(4,128)S(1)} %copy.47, s32[256]{0:T(256)S(1)} %fusion.15), kind=kOutput, calls=%fused_computation.9 | convolution fusion | flops 458424320 | bytes 305280 | tf_op jit(solution)/shard_map/dkr,dkc->rc/dot_general | solution.py:397
  54.6 0.1 broadcast_multiply_fusion.drag_ref
  54.8 0.0 copy-done
  54.8 0.0 copy-done.1
  54.8 21.6 %shard_map.96 = (f32[3,288,256]{2,1,0:T(8,128)S(1)}, f32[3,288,256]{2,1,0:T(8,128)S(1)}) custom-call(f32[12,256,128]{2,1,0:T(8,128)S(1)} %constant_dynamic-update-slice_fusion.block_ref, f32[12,16,128]{2,1,0:T(8,128)S(1)} %copy-done.1, f32[12,16,128]{2,1,0:T(8,128)S(1)} %copy-done, f32[12,128,384]{2,1,0:T(8,128)} %maximum_maximum_fusion.band_ref, ...), custom_call_target="tpu_custom_call" | custom-call | flops 106168320 | bytes 6193152 | tf_op jit(solution)/shard_map/pallas_call | solution.py:275
  76.4 0.8 slice.79
  77.2 1.2 %fusion.4 = f32[1,256,128]{2,0,1:T(1,128)S(1)} fusion(f32[3,256,128]{2,1,0:T(8,128)S(1)} %slice.82), kind=kOutput, calls=%fused_computation.20 | convolution fusion | flops 1179660 | bytes 524288 | tf_op jit(solution)/shard_map/l,lrc->rc/dot_general | solution.py:404
  78.4 0.6 exponential_select_fusion
  79.0 0.4 exponential_select_fusion.1
  79.5 0.7 fusion
  80.1 0.1 copy.50
  80.2 0.1 slice_multiply_fusion
  80.3 0.6 pad.9.src_ref
  81.0 12.6 %shard_map.97 = f32[1,128]{1,0:T(1,128)} custom-call(f32[128,128]{1,0:T(8,128)} %pad.9.src_ref), custom_call_target="tpu_custom_call" | custom-call | tf_op jit(solution)/shard_map/pallas_call | solution.py:139
  93.6 1.2 %slice_bitcast_fusion.2 = f32[4]{0:T(128)} fusion(f32[1,128]{1,0:T(1,128)} %shard_map.97), kind=kLoop, calls=%fused_computation.52 | loop fusion | bytes 32 | tf_op jit(solution)/shard_map/squeeze | solution.py:411
  (9 shorter events, 0.1 us)
Async XLA Ops:
  0.6 2.2 %copy-start.3 = (f32[3,256,128]{2,1,0:T(8,128)S(1)}, f32[3,256,128]{2,1,0:T(8,128)}, u32[]{:S(2)}) copy-start(f32[3,256,128]{2,1,0:T(8,128)} %param.11) | copy-start | bytes 1179652
  0.6 2.2 %copy-start.4 = (f32[3,256,128]{2,1,0:T(8,128)S(1)}, f32[3,256,128]{2,1,0:T(8,128)}, u32[]{:S(2)}) copy-start(f32[3,256,128]{2,1,0:T(8,128)} %param.9) | copy-start | bytes 1179652
  0.7 2.3 %copy-start.5 = (s32[4,2]{0,1:T(2,128)S(1)}, s32[4,2]{0,1:T(2,128)}, u32[]{:S(2)}) copy-start(s32[4,2]{0,1:T(2,128)} %param.13) | copy-start | bytes 100
  0.7 2.3 %copy-start.6 = (s32[4,1]{0,1:T(1,128)S(1)}, s32[4,1]{0,1:T(1,128)}, u32[]{:S(2)}) copy-start(s32[4,1]{0,1:T(1,128)} %param.12) | copy-start | bytes 52
  0.7 2.3 %copy-start.7 = (f32[4]{0:T(128)S(1)}, f32[4]{0:T(128)}, u32[]{:S(2)}) copy-start(f32[4]{0:T(128)} %param.14) | copy-start | bytes 52
  0.7 2.3 %copy-start.8 = (f32[4]{0:T(128)S(1)}, f32[4]{0:T(128)}, u32[]{:S(2)}) copy-start(f32[4]{0:T(128)} %param.15) | copy-start | bytes 52
  48.8 2.9 %copy-start.2 = (f32[128,128]{1,0:T(8,128)S(1)}, f32[128,128]{1,0:T(8,128)}, u32[]{:S(2)}) copy-start(f32[128,128]{1,0:T(8,128)} %get-tuple-element.21) | copy-start | bytes 196612
  52.2 2.5 %copy-start = (f32[12,16,128]{2,1,0:T(8,128)S(1)}, f32[12,16,128]{2,1,0:T(8,128)}, u32[]{:S(2)}) copy-start(f32[12,16,128]{2,1,0:T(8,128)} %get-tuple-element.14.low_ref) | copy-start | bytes 294916
  52.2 2.5 %copy-start.1 = (f32[12,16,128]{2,1,0:T(8,128)S(1)}, f32[12,16,128]{2,1,0:T(8,128)}, u32[]{:S(2)}) copy-start(f32[12,16,128]{2,1,0:T(8,128)} %get-tuple-element.13.high_ref) | copy-start | bytes 294916

commit v3 on v2

--- a/solution.py
+++ b/solution.py
@@ -56,24 +56,36 @@
     )
 
 
-def open_kernel(n_gx, n_gy, *refs):
+def open_kernel(n_gx, n_gy, m, info_ref, block_ref, *refs):
     n_dev = n_gx * n_gy
-    n_halo = len(HALO_MOVES)
-    info_ref = refs[0]
-    pieces = refs[1 : 1 + n_halo]
-    gathered = refs[1 + n_halo]
-    landed = refs[2 + n_halo : 2 + 2 * n_halo]
-    slots, send_sem, recv_sem, local_sem, halo_send, halo_recv = refs[2 + 2 * n_halo :]
+    n_corner = len(HALO_MOVES) - 4
+    corners = refs[:n_corner]
+    gathered = refs[n_corner]
+    landed = refs[n_corner + 1 : n_corner + 1 + len(HALO_MOVES)]
+    columns, slots, send_sem, recv_sem, local_sem, halo_send, halo_recv = refs[
+        n_corner + 1 + len(HALO_MOVES) :
+    ]
+    depth, rows, cols = block_ref.shape
+    for index in range(depth):
+        turned = block_ref[index].T
+        columns[0, index] = turned[cols - m :]
+        columns[1, index] = turned[:m]
     gx = lax.axis_index("gx")
     gy = lax.axis_index("gy")
     me = gx * n_gy + gy
     enter(n_gy, n_dev, me)
     local = pltpu.make_async_copy(info_ref, slots.at[pl.ds(me, 1)], local_sem)
     local.start()
+    sources = (
+        block_ref.at[:, rows - m :, :],
+        block_ref.at[:, :m, :],
+        columns.at[0],
+        columns.at[1],
+    ) + tuple(corners)
     halo = []
     for index, (dx, dy) in enumerate(HALO_MOVES):
         copy = pltpu.make_async_remote_copy(
-            pieces[index],
+            sources[index],
             landed[index],
             halo_send.at[index],
             halo_recv.at[index],
@@ -91,29 +103,33 @@
     gathered[...] = slots[...]
 
 
-def open_exchange(info_row, pieces):
+def open_exchange(info_row, block, corners, m):
     n_gx = lax.axis_size("gx")
     n_gy = lax.axis_size("gy")
     n_dev = n_gx * n_gy
+    depth, rows, cols = block.shape
     vmem = pl.BlockSpec(memory_space=pltpu.VMEM)
+    piece_shapes = [(depth, m, cols), (depth, m, cols), (depth, m, rows), (depth, m, rows)]
+    piece_shapes += [corner.shape for corner in corners]
     out_shape = [jax.ShapeDtypeStruct((n_dev, info_row.shape[1]), jnp.float32)] + [
-        jax.ShapeDtypeStruct(piece.shape, piece.dtype) for piece in pieces
+        jax.ShapeDtypeStruct(shape, jnp.float32) for shape in piece_shapes
     ]
     return pl.pallas_call(
-        functools.partial(open_kernel, n_gx, n_gy),
+        functools.partial(open_kernel, n_gx, n_gy, m),
         out_shape=out_shape,
-        in_specs=[vmem] * (1 + len(pieces)),
+        in_specs=[vmem] * (2 + len(corners)),
         out_specs=[vmem] * len(out_shape),
         scratch_shapes=[
+            pltpu.VMEM((2, depth, m, rows), jnp.float32),
             pltpu.VMEM((n_dev, info_row.shape[1]), jnp.float32),
             pltpu.SemaphoreType.DMA,
             pltpu.SemaphoreType.DMA,
             pltpu.SemaphoreType.DMA,
-            pltpu.SemaphoreType.DMA((len(pieces),)),
-            pltpu.SemaphoreType.DMA((len(pieces),)),
+            pltpu.SemaphoreType.DMA((len(piece_shapes),)),
+            pltpu.SemaphoreType.DMA((len(piece_shapes),)),
         ],
         compiler_params=pltpu.CompilerParams(has_side_effects=True, collective_id=0),
-    )(info_row, *pieces)
+    )(info_row, block, *corners)
 
 
 def close_kernel(n_gy, n_dev, src_ref, out_ref, slots, send_sem, recv_sem, local_sem):
@@ -151,17 +167,13 @@
     )(rows)
 
 
-def halo_pieces(block, m):
+def corner_pieces(block, m):
     last_r, first_r = block[:, -m:, :], block[:, :m, :]
     return (
-        last_r,
-        first_r,
-        jnp.swapaxes(block[:, :, -m:], 1, 2),
-        jnp.swapaxes(block[:, :, :m], 1, 2),
-        last_r[:, :, -m:],
-        last_r[:, :, :m],
-        first_r[:, :, -m:],
-        first_r[:, :, :m],
+        jnp.swapaxes(last_r[:, :, -m:], 1, 2),
+        jnp.swapaxes(last_r[:, :, :m], 1, 2),
+        jnp.swapaxes(first_r[:, :, -m:], 1, 2),
+        jnp.swapaxes(first_r[:, :, :m], 1, 2),
     )
 
 
@@ -174,7 +186,7 @@
     def edge(column, high_corner, low_corner):
         fill = jnp.zeros((depth, m, span - size_r), jnp.float32)
         return jnp.concatenate(
-            [column, jnp.swapaxes(high_corner, 1, 2), jnp.swapaxes(low_corner, 1, 2), fill],
+            [column, high_corner, low_corner, fill],
             axis=2,
         )
 
@@ -184,7 +196,7 @@
 
 def stencil_kernel(
     levels, steps, block_ref, high_ref, low_ref, band_ref, drag_ref, lam_out, sens_out,
-    ext_ref, states, lams,
+    ext_ref, states, lams, sens_all,
 ):
     size_r, size_c = ext_ref.shape[1:]
     rows, cols = block_ref.shape[1:]
@@ -237,7 +249,7 @@
     lax.fori_loop(0, steps - 1, forward, 0)
     for level in range(levels):
         lams[0, level] = ext_ref[3 * levels + level]
-        sens_out[level] = jnp.zeros(sens_out.shape[1:], jnp.float32)
+        sens_all[level] = jnp.zeros(sens_all.shape[1:], jnp.float32)
 
     def backward(i, carry):
         n = steps - 1 - i
@@ -245,7 +257,7 @@
         for level in range(levels):
             adjoint = lams[now, level]
             state = states[n, level]
-            sens_out[level] = sens_out[level] - adjoint * (state * jnp.sqrt(state * state + 1.0))
+            sens_all[level] = sens_all[level] - adjoint * (state * jnp.sqrt(state * state + 1.0))
             flux_adv = ext_ref[levels + level] * adjoint
             flux_dif = ext_ref[2 * levels + level] * adjoint
             square_one = state * state + 1.0
@@ -263,14 +275,16 @@
 
     lax.fori_loop(0, steps, backward, 0)
     for level in range(levels):
-        lam_out[level] = lams[steps % 2, level]
+        sens_out[level] = sens_all[level, :rows, :cols]
+    for level in range(levels):
+        lam_out[level] = lams[steps % 2, level, :rows, :cols]
 
 
 def stencil(block, landed, band, drag, levels):
     size_r, size_c = drag.shape[1:]
     depth = block.shape[0]
     vmem = pl.BlockSpec(memory_space=pltpu.VMEM)
-    plane = jax.ShapeDtypeStruct((levels, size_r, size_c), jnp.float32)
+    plane = jax.ShapeDtypeStruct((levels,) + block.shape[1:], jnp.float32)
     cells = levels * size_r * size_c
     return pl.pallas_call(
         functools.partial(stencil_kernel, levels, STEPS),
@@ -281,6 +295,7 @@
             pltpu.VMEM((depth, size_r, size_c), jnp.float32),
             pltpu.VMEM((STEPS, levels, size_r, size_c), jnp.float32),
             pltpu.VMEM((2, levels, size_r, size_c), jnp.float32),
+            pltpu.VMEM((levels, size_r, size_c), jnp.float32),
         ],
         compiler_params=pltpu.CompilerParams(vmem_limit_bytes=48 * 1024 * 1024),
         cost_estimate=pl.CostEstimate(
@@ -378,7 +393,7 @@
     )
     info_row = jnp.pad(jnp.concatenate(fields)[None, :], ((0, 0), (0, 128 - len(fields) * per)))
     stack = jnp.concatenate([velocity, courant, viscosity, adjoint_seed], axis=0)
-    opened = open_exchange(info_row, halo_pieces(stack, m))
+    opened = open_exchange(info_row, stack, corner_pieces(stack, m), m)
     info = opened[0]
     tiles = info[:, 0:per].astype(jnp.int32)
     row_start = tiles // n_gy * rows + info[:, per : 2 * per].astype(jnp.int32)
@@ -398,8 +413,8 @@
     drag = gain[:, None, None] * plane[None]
     band = column_band(opened[1:], m, size_r, size_c, cols)
     adjoint_full, sens_full = stencil(stack, opened[1:], band, drag, levels)
-    adjoint = adjoint_full[:, :rows, :cols]
-    sensitivity = sens_full[:, :rows, :cols]
+    adjoint = adjoint_full
+    sensitivity = sens_full
 
     weighted = jnp.einsum("l,lrc->rc", gain, sensitivity, precision=HIGHEST)
     own_r = prof_r[..., :rows]

time: 95.2 us -> 86.5 us (0.909)
  local copies, waits for them, and re-layouts: 16.7 us -> 9.11 us
  other arithmetic: 4.45 us -> 3.18 us
    pallas_call x4 -> x0, local copies, waits for them, and re-layouts: 3.9 us -> none  [open_exchange(): pl.pallas_call(functools.partial(open_kernel, n_gx, n_gy), out_shape=out_...]
    transpose x3 -> x5, local copies, waits for them, and re-layouts: 5.36 us -> 3 us  [the longest x2 0.82 us: corner_pieces(): jnp.swapaxes(first_r[:, :, :m], 1, 2)]
    slice x4 -> x0, local copies, waits for them, and re-layouts: 2.34 us -> none  [the longest x1 0.85 us: halo_pieces(): first_r[:, :, :m]]
    concatenate x1, other arithmetic: 2.85 us -> 1.58 us  [column_band(): jnp.concatenate([edge(col_high, c_hh, c_lh), fill, edge(col_low, c_hl, c_...]
    unnamed x21 -> x23, local copies, waits for them, and re-layouts: 2.18 us -> 3.16 us
where the time goes in v3:
time: 86.5 us; the launch traced here: 86.2 us
  Pallas kernels  68.8 us (80%)
  local copies, waits for them, and re-layouts  9.11 us (11%)
  matrix products  4.15 us (5%)
  other arithmetic  3.18 us (4%)
  between operations  0.91 us (1%)
    pallas_call x1, Pallas kernels, open_exchange(): pl.pallas_call(functools.partial(open_kernel, n_gx, n_gy, m), out_shape=o...  35.2 us
    pallas_call x1, Pallas kernels, stencil(): pl.pallas_call(functools.partial(stencil_kernel, levels, STEPS), out_shap...  21.1 us
    pallas_call x1, Pallas kernels, close_scatter(): pl.pallas_call(functools.partial(close_kernel, n_gy, n_dev), out_shape=ja...  12.5 us
    unnamed x23, local copies, waits for them, and re-layouts  3.16 us
    dot_general x1, matrix products, shards(): jnp.einsum('dkr,dkc->rc', thrusts[..., None] * prof_r, prof_c, precision=...  2.33 us

profile of v3, /device:TPU:1, one launch (start us, length us, event | category | flops | bytes accessed | tf_op | source)
XLA Modules:
  0.0 86.2 jit_solution(3549357891435555426)
XLA Ops:
  0.6 0.0 copy-start.5
  0.6 0.0 copy-start.6
  0.7 0.0 copy-start.7
  0.7 0.0 copy-start.8
  0.7 0.0 copy-start.9
  0.7 1.1 %constant_dynamic-update-slice_fusion.3 = f32[12,256,128]{2,1,0:T(8,128)S(1)} fusion(f32[3,256,128]{2,1,0:T(8,128)} %param.8), kind=kLoop, calls=%fused_computation.45 | loop fusion | bytes 786432
  1.7 1.0 %constant_dynamic-update-slice_fusion.2 = f32[12,256,128]{2,1,0:T(8,128)S(1)} fusion(f32[12,256,128]{2,1,0:T(8,128)S(1)} %constant_dynamic-update-slice_fusion.3, f32[3,256,128]{2,1,0:T(8,128)} %param.10), kind=kLoop, calls=%fused_computation.44 | loop fusion | bytes 786432
  2.8 1.0 %constant_dynamic-update-slice_fusion.1 = f32[12,256,128]{2,1,0:T(8,128)S(1)} fusion(f32[12,256,128]{2,1,0:T(8,128)S(1)} %constant_dynamic-update-slice_fusion.2, f32[3,256,128]{2,1,0:T(8,128)} %param.11), kind=kLoop, calls=%fused_computation.43 | loop fusion | bytes 786432
  3.8 0.0 copy-done.5
  3.9 0.0 copy-done.6
  3.9 0.0 copy-done.7
  3.9 0.0 copy-start
  3.9 0.0 copy-done.8
  3.9 0.0 copy-done.9
  3.9 0.1 concatenate.16
  4.0 0.6 pad.8.info_ref
  4.6 0.1 slice_bitcast_fusion
  4.8 0.7 copy.31.refs_0_
  5.5 0.7 copy.32.refs_1_
  6.2 0.7 copy.33.refs_2_
  6.9 0.7 copy.34.refs_3_
  7.7 0.0 copy-done
  7.7 35.2 %shard_map.95 = (f32[128,128]{1,0:T(8,128)}, f32[12,16,128]{2,1,0:T(8,128)}, f32[12,16,128]{2,1,0:T(8,128)}, f32[12,16,256]{2,1,0:T(8,128)}, f32[12,16,256]{2,1,...) custom-call(f32[1,128]{1,0:T(1,128)} %pad.8.info_ref, ...), custom_call_target="tpu_custom_call" | custom-call | tf_op jit(solution)/shard_map/pallas_call | solution.py:117
  42.9 0.0 copy-start.4
  42.9 0.1 pad.14.clone
  43.0 1.6 %maximum_maximum_fusion.band_ref = f32[12,128,384]{2,1,0:T(8,128)S(1)} fusion(f32[12,16,96]{2,1,0:T(8,128)S(1)} %broadcast.97, f32[12,16,16]{2,1,0:T(8,128)} %get-tuple-element.20, f32[12,16,16]{2,1,0:T(8,128)} %get-tuple-element.19, f32[12,16,256]{2,1,0:T(8,128)} %get-tuple-element.18, f32[12,16,16]{2,1,0:T(8,128)} %get-tuple-element.17, ...), kind=kLoop, calls=%fused_computation | loop fusion | flops 4718592 | bytes 2875904 | tf_op jit(solution)/shard_map/concatenate | solution.py:194
  44.6 0.0 copy-done.4
  44.6 0.1 multiply_multiply_fusion
  44.7 0.1 copy.35
  44.8 0.1 copy.39
  44.8 0.1 fusion.11
  45.0 0.1 fusion.9
  45.0 0.1 copy.37
  45.1 0.1 copy.41
  45.2 0.0 copy-start.1
  45.2 0.0 copy-start.2
  45.2 0.0 copy-start.3
  45.2 2.3 %convolution_bitcast_fusion = f32[288,256]{1,0:T(8,128)S(1)} fusion(f32[128,4]{0,1:T(4,128)S(1)} %copy.35, f32[128,4]{0,1:T(4,128)S(1)} %copy.39, s32[128,4]{0,1:T(4,128)S(1)} %copy.37, s32[288]{0:T(512)S(1)} %fusion.14, s32[128,4]{0,1:T(4,128)S(1)} %copy.41, s32[256]{0:T(256)S(1)} %fusion.15), kind=kOutput, calls=%fused_computation.7 | convolution fusion | flops 458424320 | bytes 305280 | tf_op jit(solution)/shard_map/dkr,dkc->rc/dot_general | solution.py:412
  47.6 0.1 broadcast_multiply_fusion.drag_ref
  47.7 0.0 copy-done.1
  47.7 0.0 copy-done.2
  47.7 0.0 copy-done.3
  47.8 21.1 %shard_map.96 = (f32[3,256,128]{2,1,0:T(8,128)}, f32[3,256,128]{2,1,0:T(8,128)S(1)}) custom-call(f32[12,256,128]{2,1,0:T(8,128)S(1)} %copy-done.1, f32[12,16,128]{2,1,0:T(8,128)S(1)} %copy-done.3, f32[12,16,128]{2,1,0:T(8,128)S(1)} %copy-done.2, f32[12,128,384]{2,1,0:T(8,128)S(1)} %maximum_maximum_fusion.band_ref, ...), custom_call_target="tpu_custom_call" | custom-call | flops 106168320 | bytes 6193152 | tf_op jit(solution)/shard_map/pallas_call | solution.py:289
  68.8 1.2 %fusion.4 = f32[1,256,128]{2,0,1:T(1,128)S(1)} fusion(f32[3,256,128]{2,1,0:T(8,128)S(1)} %get-tuple-element.23), kind=kOutput, calls=%fused_computation.18 | convolution fusion | flops 1179660 | bytes 524288 | tf_op jit(solution)/shard_map/l,lrc->rc/dot_general | solution.py:419
  70.0 0.6 exponential_select_fusion
  70.6 0.4 exponential_select_fusion.1
  71.1 0.7 fusion
  71.7 0.1 copy.44
  71.8 0.1 slice_multiply_fusion
  71.9 0.6 pad.9.src_ref
  72.6 12.5 %shard_map.97 = f32[1,128]{1,0:T(1,128)} custom-call(f32[128,128]{1,0:T(8,128)} %pad.9.src_ref), custom_call_target="tpu_custom_call" | custom-call | tf_op jit(solution)/shard_map/pallas_call | solution.py:155
  85.1 1.1 %slice_bitcast_fusion.4 = f32[4]{0:T(128)} fusion(f32[1,128]{1,0:T(1,128)} %shard_map.97), kind=kLoop, calls=%fused_computation.54 | loop fusion | bytes 32 | tf_op jit(solution)/shard_map/squeeze | solution.py:426
  (7 shorter events, 0.1 us)
Async XLA Ops:
  0.6 3.2 %copy-start.5 = (f32[3,256,128]{2,1,0:T(8,128)S(1)}, f32[3,256,128]{2,1,0:T(8,128)}, u32[]{:S(2)}) copy-start(f32[3,256,128]{2,1,0:T(8,128)} %param.9) | copy-start | bytes 1179652
  0.6 3.2 %copy-start.6 = (s32[4,2]{0,1:T(2,128)S(1)}, s32[4,2]{0,1:T(2,128)}, u32[]{:S(2)}) copy-start(s32[4,2]{0,1:T(2,128)} %param.13) | copy-start | bytes 100
  0.7 3.2 %copy-start.7 = (s32[4,1]{0,1:T(1,128)S(1)}, s32[4,1]{0,1:T(1,128)}, u32[]{:S(2)}) copy-start(s32[4,1]{0,1:T(1,128)} %param.12) | copy-start | bytes 52
  0.7 3.2 %copy-start.8 = (f32[4]{0:T(128)S(1)}, f32[4]{0:T(128)}, u32[]{:S(2)}) copy-start(f32[4]{0:T(128)} %param.14) | copy-start | bytes 52
  0.7 3.2 %copy-start.9 = (f32[4]{0:T(128)S(1)}, f32[4]{0:T(128)}, u32[]{:S(2)}) copy-start(f32[4]{0:T(128)} %param.15) | copy-start | bytes 52
  3.9 3.8 %copy-start = (f32[12,256,128]{2,1,0:T(8,128)}, f32[12,256,128]{2,1,0:T(8,128)S(1)}, u32[]{:S(2)}) copy-start(f32[12,256,128]{2,1,0:T(8,128)S(1)} %constant_dynamic-update-slice_fusion.block_ref) | copy-start | bytes 4718596
  42.9 1.7 %copy-start.4 = (f32[128,128]{1,0:T(8,128)S(1)}, f32[128,128]{1,0:T(8,128)}, u32[]{:S(2)}) copy-start(f32[128,128]{1,0:T(8,128)} %get-tuple-element.21) | copy-start | bytes 196612
  45.2 2.5 %copy-start.1 = (f32[12,256,128]{2,1,0:T(8,128)S(1)}, f32[12,256,128]{2,1,0:T(8,128)}, u32[]{:S(2)}) copy-start(f32[12,256,128]{2,1,0:T(8,128)} %copy-done) | copy-start | bytes 4718596
  45.2 2.5 %copy-start.2 = (f32[12,16,128]{2,1,0:T(8,128)S(1)}, f32[12,16,128]{2,1,0:T(8,128)}, u32[]{:S(2)}) copy-start(f32[12,16,128]{2,1,0:T(8,128)} %get-tuple-element.14.low_ref) | copy-start | bytes 294916
  45.2 2.5 %copy-start.3 = (f32[12,16,128]{2,1,0:T(8,128)S(1)}, f32[12,16,128]{2,1,0:T(8,128)}, u32[]{:S(2)}) copy-start(f32[12,16,128]{2,1,0:T(8,128)} %get-tuple-element.13.high_ref) | copy-start | bytes 294916

commit v4 on v3

--- a/solution.py
+++ b/solution.py
@@ -56,58 +56,77 @@
     )
 
 
-def open_kernel(n_gx, n_gy, m, info_ref, block_ref, *refs):
+def open_kernel(n_gx, n_gy, m, n_block, info_ref, *refs):
     n_dev = n_gx * n_gy
     n_corner = len(HALO_MOVES) - 4
-    corners = refs[:n_corner]
-    gathered = refs[n_corner]
-    landed = refs[n_corner + 1 : n_corner + 1 + len(HALO_MOVES)]
+    blocks = refs[:n_block]
+    corners = refs[n_block : n_block + n_corner]
+    gathered = refs[n_block + n_corner]
+    landed = refs[n_block + n_corner + 1 : n_block + n_corner + 1 + len(HALO_MOVES)]
     columns, slots, send_sem, recv_sem, local_sem, halo_send, halo_recv = refs[
-        n_corner + 1 + len(HALO_MOVES) :
+        n_block + n_corner + 1 + len(HALO_MOVES) :
     ]
-    depth, rows, cols = block_ref.shape
-    for index in range(depth):
-        turned = block_ref[index].T
-        columns[0, index] = turned[cols - m :]
-        columns[1, index] = turned[:m]
+    levels, rows, cols = blocks[0].shape
+    for field, block_ref in enumerate(blocks):
+        for level in range(levels):
+            turned = block_ref[level].T
+            columns[0, field * levels + level] = turned[cols - m :]
+            columns[1, field * levels + level] = turned[:m]
     gx = lax.axis_index("gx")
     gy = lax.axis_index("gy")
     me = gx * n_gy + gy
     enter(n_gy, n_dev, me)
     local = pltpu.make_async_copy(info_ref, slots.at[pl.ds(me, 1)], local_sem)
     local.start()
+    parts = lambda window: [
+        (block_ref.at[:, window, :], pl.ds(field * levels, levels))
+        for field, block_ref in enumerate(blocks)
+    ]
+    whole = pl.ds(0, n_block * levels)
     sources = (
-        block_ref.at[:, rows - m :, :],
-        block_ref.at[:, :m, :],
-        columns.at[0],
-        columns.at[1],
-    ) + tuple(corners)
-    halo = []
+        parts(pl.ds(rows - m, m)),
+        parts(pl.ds(0, m)),
+        [(columns.at[0], whole)],
+        [(columns.at[1], whole)],
+    ) + tuple([(corner, whole)] for corner in corners)
+    waits = []
     for index, (dx, dy) in enumerate(HALO_MOVES):
-        copy = pltpu.make_async_remote_copy(
-            sources[index],
-            landed[index],
-            halo_send.at[index],
-            halo_recv.at[index],
-            device_id=(lax.rem(gx + dx + n_gx, n_gx), lax.rem(gy + dy + n_gy, n_gy)),
-            device_id_type=MESH_ID,
+        target = (lax.rem(gx + dx + n_gx, n_gx), lax.rem(gy + dy + n_gy, n_gy))
+        for source, depth in sources[index]:
+            pltpu.make_async_remote_copy(
+                source,
+                landed[index].at[depth],
+                halo_send.at[index],
+                halo_recv.at[index],
+                device_id=target,
+                device_id_type=MESH_ID,
+            ).start()
+        waits.append(
+            pltpu.make_async_remote_copy(
+                landed[index],
+                landed[index],
+                halo_send.at[index],
+                halo_recv.at[index],
+                device_id=target,
+                device_id_type=MESH_ID,
+            )
         )
-        copy.start()
-        halo.append(copy)
     every = spread_rows(n_gy, n_dev, me, lambda target: info_ref, slots, send_sem, recv_sem)
     local.wait()
-    for copy in halo:
-        copy.wait()
+    for copy in waits:
+        copy.wait_send()
+        copy.wait_recv()
     every.wait_send()
     every.wait_recv()
     gathered[...] = slots[...]
 
 
-def open_exchange(info_row, block, corners, m):
+def open_exchange(info_row, blocks, corners, m):
     n_gx = lax.axis_size("gx")
     n_gy = lax.axis_size("gy")
     n_dev = n_gx * n_gy
-    depth, rows, cols = block.shape
+    levels, rows, cols = blocks[0].shape
+    depth = levels * len(blocks)
     vmem = pl.BlockSpec(memory_space=pltpu.VMEM)
     piece_shapes = [(depth, m, cols), (depth, m, cols), (depth, m, rows), (depth, m, rows)]
     piece_shapes += [corner.shape for corner in corners]
@@ -115,9 +134,9 @@
         jax.ShapeDtypeStruct(shape, jnp.float32) for shape in piece_shapes
     ]
     return pl.pallas_call(
-        functools.partial(open_kernel, n_gx, n_gy, m),
+        functools.partial(open_kernel, n_gx, n_gy, m, len(blocks)),
         out_shape=out_shape,
-        in_specs=[vmem] * (2 + len(corners)),
+        in_specs=[vmem] * (1 + len(blocks) + len(corners)),
         out_specs=[vmem] * len(out_shape),
         scratch_shapes=[
             pltpu.VMEM((2, depth, m, rows), jnp.float32),
@@ -129,7 +148,7 @@
             pltpu.SemaphoreType.DMA((len(piece_shapes),)),
         ],
         compiler_params=pltpu.CompilerParams(has_side_effects=True, collective_id=0),
-    )(info_row, block, *corners)
+    )(info_row, *blocks, *corners)
 
 
 def close_kernel(n_gy, n_dev, src_ref, out_ref, slots, send_sem, recv_sem, local_sem):
@@ -167,7 +186,10 @@
     )(rows)
 
 
-def corner_pieces(block, m):
+def corner_pieces(blocks, m):
+    block = jnp.concatenate(
+        [jnp.concatenate([piece[:, :m], piece[:, -m:]], axis=1) for piece in blocks], axis=0
+    )
     last_r, first_r = block[:, -m:, :], block[:, :m, :]
     return (
         jnp.swapaxes(last_r[:, :, -m:], 1, 2),
@@ -194,15 +216,16 @@
     return jnp.concatenate([edge(col_high, c_hh, c_lh), fill, edge(col_low, c_hl, c_ll)], axis=1)
 
 
-def stencil_kernel(
-    levels, steps, block_ref, high_ref, low_ref, band_ref, drag_ref, lam_out, sens_out,
-    ext_ref, states, lams, sens_all,
-):
+def stencil_kernel(levels, steps, n_block, *refs):
+    blocks = refs[:n_block]
+    high_ref, low_ref, band_ref, drag_ref, lam_out, sens_out, ext_ref, states, lams, sens_all = refs[
+        n_block:
+    ]
     size_r, size_c = ext_ref.shape[1:]
-    rows, cols = block_ref.shape[1:]
+    rows, cols = blocks[0].shape[1:]
     m = high_ref.shape[1]
     for depth in range(ext_ref.shape[0]):
-        ext_ref[depth, :rows, :cols] = block_ref[depth]
+        ext_ref[depth, :rows, :cols] = blocks[depth // levels][depth % levels]
         ext_ref[depth, rows : rows + m, :cols] = high_ref[depth]
         ext_ref[depth, size_r - m :, :cols] = low_ref[depth]
         ext_ref[depth, :, cols:] = band_ref[depth].T[:size_r]
@@ -280,16 +303,16 @@
         lam_out[level] = lams[steps % 2, level, :rows, :cols]
 
 
-def stencil(block, landed, band, drag, levels):
+def stencil(blocks, landed, band, drag, levels):
     size_r, size_c = drag.shape[1:]
-    depth = block.shape[0]
+    depth = levels * len(blocks)
     vmem = pl.BlockSpec(memory_space=pltpu.VMEM)
-    plane = jax.ShapeDtypeStruct((levels,) + block.shape[1:], jnp.float32)
+    plane = jax.ShapeDtypeStruct(blocks[0].shape, jnp.float32)
     cells = levels * size_r * size_c
     return pl.pallas_call(
-        functools.partial(stencil_kernel, levels, STEPS),
+        functools.partial(stencil_kernel, levels, STEPS, len(blocks)),
         out_shape=[plane, plane],
-        in_specs=[vmem] * 5,
+        in_specs=[vmem] * (len(blocks) + 4),
         out_specs=[vmem, vmem],
         scratch_shapes=[
             pltpu.VMEM((depth, size_r, size_c), jnp.float32),
@@ -301,7 +324,7 @@
         cost_estimate=pl.CostEstimate(
             flops=60 * STEPS * cells, transcendentals=3 * STEPS * cells, bytes_accessed=28 * cells
         ),
-    )(block, landed[1], landed[0], band, drag)
+    )(*blocks, landed[1], landed[0], band, drag)
 
 
 def drag_law(state):
@@ -392,8 +415,8 @@
         disk_width,
     )
     info_row = jnp.pad(jnp.concatenate(fields)[None, :], ((0, 0), (0, 128 - len(fields) * per)))
-    stack = jnp.concatenate([velocity, courant, viscosity, adjoint_seed], axis=0)
-    opened = open_exchange(info_row, stack, corner_pieces(stack, m), m)
+    blocks = (velocity, courant, viscosity, adjoint_seed)
+    opened = open_exchange(info_row, blocks, corner_pieces(blocks, m), m)
     info = opened[0]
     tiles = info[:, 0:per].astype(jnp.int32)
     row_start = tiles // n_gy * rows + info[:, per : 2 * per].astype(jnp.int32)
@@ -412,7 +435,7 @@
     plane = jnp.einsum("dkr,dkc->rc", thrusts[..., None] * prof_r, prof_c, precision=HIGHEST)
     drag = gain[:, None, None] * plane[None]
     band = column_band(opened[1:], m, size_r, size_c, cols)
-    adjoint_full, sens_full = stencil(stack, opened[1:], band, drag, levels)
+    adjoint_full, sens_full = stencil(blocks, opened[1:], band, drag, levels)
     adjoint = adjoint_full
     sensitivity = sens_full
 

time: 86.5 us -> 86.4 us (level)
  local copies, waits for them, and re-layouts: 9.11 us -> 8.19 us
    transpose x5 -> x0, local copies, waits for them, and re-layouts: 3 us -> none  [the longest x2 0.82 us: corner_pieces(): jnp.swapaxes(first_r[:, :, :m], 1, 2)]
    slice x0 -> x3, local copies, waits for them, and re-layouts: none -> 1.71 us  [the longest x2 1.6 us: corner_pieces(): piece[:, :m]]
    unnamed x23 -> x18, local copies, waits for them, and re-layouts: 3.16 us -> 2.97 us
where the time goes in v4:
time: 86.4 us; the launch traced here: 86 us
  Pallas kernels  68.8 us (80%)
  local copies, waits for them, and re-layouts  8.19 us (9%)
  matrix products  4.15 us (5%)
  other arithmetic  3.96 us (5%)
    pallas_call x1, Pallas kernels, open_exchange(): pl.pallas_call(functools.partial(open_kernel, n_gx, n_gy, m, len(blocks))...  35.2 us
    pallas_call x1, Pallas kernels, stencil(): pl.pallas_call(functools.partial(stencil_kernel, levels, STEPS, len(block...  21.1 us
    pallas_call x1, Pallas kernels, close_scatter(): pl.pallas_call(functools.partial(close_kernel, n_gy, n_dev), out_shape=ja...  12.6 us
    unnamed x18, local copies, waits for them, and re-layouts  2.97 us
    dot_general x1, matrix products, shards(): jnp.einsum('dkr,dkc->rc', thrusts[..., None] * prof_r, prof_c, precision=...  2.33 us

profile of v4, /device:TPU:1, one launch (start us, length us, event | category | flops | bytes accessed | tf_op | source)
XLA Modules:
  0.0 86.0 jit_solution(16350703209090171717)
XLA Ops:
  0.6 0.8 convert_bitcast_fusion
  1.4 0.7 concatenate.27
  2.1 0.5 pad.8.info_ref
  2.7 0.8 fusion.34
  3.5 0.8 fusion.32
  4.3 0.1 fusion.36
  4.4 0.7 copy.52
  5.1 0.7 copy.53
  5.9 0.7 copy.54
  6.6 0.7 copy.55
  7.3 35.2 %shard_map.95 = (f32[128,128]{1,0:T(8,128)}, f32[12,16,128]{2,1,0:T(8,128)}, f32[12,16,128]{2,1,0:T(8,128)}, f32[12,16,256]{2,1,0:T(8,128)}, f32[12,16,256]{2,1,...) custom-call(f32[1,128]{1,0:T(1,128)} %pad.8.info_ref, ...), custom_call_target="tpu_custom_call" | custom-call | tf_op jit(solution)/shard_map/pallas_call | solution.py:136
  42.5 0.0 copy-start.6
  42.6 0.1 pad.14.clone
  42.6 1.6 %maximum_maximum_fusion.refs_6_ = f32[12,128,384]{2,1,0:T(8,128)S(1)} fusion(f32[12,16,96]{2,1,0:T(8,128)S(1)} %broadcast.97, f32[12,16,16]{2,1,0:T(8,128)} %get-tuple-element.20, f32[12,16,16]{2,1,0:T(8,128)} %get-tuple-element.19, f32[12,16,256]{2,1,0:T(8,128)} %get-tuple-element.18, f32[12,16,16]{2,1,0:T(8,128)} %get-tuple-element.17, ...), kind=kLoop, calls=%fused_computation | loop fusion | flops 4718592 | bytes 2875904 | tf_op jit(solution)/shard_map/concatenate | solution.py:216
  44.2 0.0 copy-done.6
  44.2 0.1 multiply_multiply_fusion
  44.3 0.1 copy.39
  44.4 0.1 copy.43
  44.5 0.1 fusion.11
  44.6 0.1 fusion.9
  44.7 0.1 copy.41
  44.8 0.1 copy.45
  44.8 0.0 copy-start
  44.8 0.0 copy-start.1
  44.9 0.0 copy-start.2
  44.9 0.0 copy-start.3
  44.9 0.0 copy-start.4
  44.9 0.0 copy-start.5
  44.9 2.3 %convolution_bitcast_fusion = f32[288,256]{1,0:T(8,128)S(1)} fusion(f32[128,4]{0,1:T(4,128)S(1)} %copy.39, f32[128,4]{0,1:T(4,128)S(1)} %copy.43, s32[128,4]{0,1:T(4,128)S(1)} %copy.41, s32[288]{0:T(512)S(1)} %fusion.14, s32[128,4]{0,1:T(4,128)S(1)} %copy.45, s32[256]{0:T(256)S(1)} %fusion.15), kind=kOutput, calls=%fused_computation.7 | convolution fusion | flops 458424320 | bytes 305280 | tf_op jit(solution)/shard_map/dkr,dkc->rc/dot_general | solution.py:435
  47.3 0.1 broadcast_multiply_fusion.refs_7_
  47.4 0.0 copy-done
  47.4 0.0 copy-done.1
  47.4 0.0 copy-done.2
  47.4 0.0 copy-done.3
  47.4 0.0 copy-done.4
  47.5 0.0 copy-done.5
  47.5 21.1 %shard_map.96 = (f32[3,256,128]{2,1,0:T(8,128)}, f32[3,256,128]{2,1,0:T(8,128)S(1)}) custom-call(f32[3,256,128]{2,1,0:T(8,128)S(1)} %copy-done, f32[3,256,128]{2,1,0:T(8,128)S(1)} %copy-done.1, f32[3,256,128]{2,1,0:T(8,128)S(1)} %copy-done.2, f32[3,256,128]{2,1,0:T(8,128)S(1)} %copy-done.3, f32[12,16,128]{2,1,0:T(8,128)S(1)} %copy-done.5, ...), custom_call_target="tpu_custom_call" | custom-call | flops 106168320 | bytes 6193152 | tf_op jit(solution)/shard_map/pallas_call | solution.py:312
  68.5 1.2 %fusion.4 = f32[1,256,128]{2,0,1:T(1,128)S(1)} fusion(f32[3,256,128]{2,1,0:T(8,128)S(1)} %get-tuple-element.23), kind=kOutput, calls=%fused_computation.18 | convolution fusion | flops 1179660 | bytes 524288 | tf_op jit(solution)/shard_map/l,lrc->rc/dot_general | solution.py:442
  69.7 0.6 exponential_select_fusion
  70.3 0.4 exponential_select_fusion.1
  70.8 0.7 fusion
  71.4 0.1 copy.48
  71.5 0.1 slice_multiply_fusion
  71.6 0.6 pad.9.src_ref
  72.3 12.6 %shard_map.97 = f32[1,128]{1,0:T(1,128)} custom-call(f32[128,128]{1,0:T(8,128)} %pad.9.src_ref), custom_call_target="tpu_custom_call" | custom-call | tf_op jit(solution)/shard_map/pallas_call | solution.py:174
  84.9 1.1 %slice_bitcast_fusion = f32[4]{0:T(128)} fusion(f32[1,128]{1,0:T(1,128)} %shard_map.97), kind=kLoop, calls=%fused_computation.47 | loop fusion | bytes 32 | tf_op jit(solution)/shard_map/squeeze | solution.py:449
  (6 shorter events, 0.1 us)
Async XLA Ops:
  42.5 1.7 %copy-start.6 = (f32[128,128]{1,0:T(8,128)S(1)}, f32[128,128]{1,0:T(8,128)}, u32[]{:S(2)}) copy-start(f32[128,128]{1,0:T(8,128)} %get-tuple-element.21) | copy-start | bytes 196612
  44.8 2.6 %copy-start = (f32[3,256,128]{2,1,0:T(8,128)S(1)}, f32[3,256,128]{2,1,0:T(8,128)}, u32[]{:S(2)}) copy-start(f32[3,256,128]{2,1,0:T(8,128)} %refs_0_.3) | copy-start | bytes 1179652
  44.8 2.6 %copy-start.1 = (f32[3,256,128]{2,1,0:T(8,128)S(1)}, f32[3,256,128]{2,1,0:T(8,128)}, u32[]{:S(2)}) copy-start(f32[3,256,128]{2,1,0:T(8,128)} %refs_1_.3) | copy-start | bytes 1179652
  44.9 2.6 %copy-start.2 = (f32[3,256,128]{2,1,0:T(8,128)S(1)}, f32[3,256,128]{2,1,0:T(8,128)}, u32[]{:S(2)}) copy-start(f32[3,256,128]{2,1,0:T(8,128)} %refs_2_.3) | copy-start | bytes 1179652
  44.9 2.6 %copy-start.3 = (f32[3,256,128]{2,1,0:T(8,128)S(1)}, f32[3,256,128]{2,1,0:T(8,128)}, u32[]{:S(2)}) copy-start(f32[3,256,128]{2,1,0:T(8,128)} %refs_3_.3) | copy-start | bytes 1179652
  44.9 2.6 %copy-start.4 = (f32[12,16,128]{2,1,0:T(8,128)S(1)}, f32[12,16,128]{2,1,0:T(8,128)}, u32[]{:S(2)}) copy-start(f32[12,16,128]{2,1,0:T(8,128)} %get-tuple-element.14.refs_5_) | copy-start | bytes 294916
  44.9 2.6 %copy-start.5 = (f32[12,16,128]{2,1,0:T(8,128)S(1)}, f32[12,16,128]{2,1,0:T(8,128)}, u32[]{:S(2)}) copy-start(f32[12,16,128]{2,1,0:T(8,128)} %get-tuple-element.13.refs_4_) | copy-start | bytes 294916

commit v5 on v4

--- a/solution.py
+++ b/solution.py
@@ -58,20 +58,24 @@
 
 def open_kernel(n_gx, n_gy, m, n_block, info_ref, *refs):
     n_dev = n_gx * n_gy
-    n_corner = len(HALO_MOVES) - 4
+    n_corner = 0
     blocks = refs[:n_block]
-    corners = refs[n_block : n_block + n_corner]
     gathered = refs[n_block + n_corner]
     landed = refs[n_block + n_corner + 1 : n_block + n_corner + 1 + len(HALO_MOVES)]
-    columns, slots, send_sem, recv_sem, local_sem, halo_send, halo_recv = refs[
+    columns, corners, slots, send_sem, recv_sem, local_sem, halo_send, halo_recv = refs[
         n_block + n_corner + 1 + len(HALO_MOVES) :
     ]
     levels, rows, cols = blocks[0].shape
     for field, block_ref in enumerate(blocks):
         for level in range(levels):
             turned = block_ref[level].T
-            columns[0, field * levels + level] = turned[cols - m :]
-            columns[1, field * levels + level] = turned[:m]
+            depth = field * levels + level
+            columns[0, depth] = turned[cols - m :]
+            columns[1, depth] = turned[:m]
+            for index, (side, window) in enumerate(
+                ((cols - m, rows - m), (0, rows - m), (cols - m, 0), (0, 0))
+            ):
+                corners[index, depth] = turned[side : side + m, window : window + m]
     gx = lax.axis_index("gx")
     gy = lax.axis_index("gy")
     me = gx * n_gy + gy
@@ -88,7 +92,7 @@
         parts(pl.ds(0, m)),
         [(columns.at[0], whole)],
         [(columns.at[1], whole)],
-    ) + tuple([(corner, whole)] for corner in corners)
+    ) + tuple([(corners.at[index], whole)] for index in range(len(HALO_MOVES) - 4))
     waits = []
     for index, (dx, dy) in enumerate(HALO_MOVES):
         target = (lax.rem(gx + dx + n_gx, n_gx), lax.rem(gy + dy + n_gy, n_gy))
@@ -121,7 +125,7 @@
     gathered[...] = slots[...]
 
 
-def open_exchange(info_row, blocks, corners, m):
+def open_exchange(info_row, blocks, m):
     n_gx = lax.axis_size("gx")
     n_gy = lax.axis_size("gy")
     n_dev = n_gx * n_gy
@@ -129,17 +133,18 @@
     depth = levels * len(blocks)
     vmem = pl.BlockSpec(memory_space=pltpu.VMEM)
     piece_shapes = [(depth, m, cols), (depth, m, cols), (depth, m, rows), (depth, m, rows)]
-    piece_shapes += [corner.shape for corner in corners]
+    piece_shapes += [(depth, m, m)] * (len(HALO_MOVES) - 4)
     out_shape = [jax.ShapeDtypeStruct((n_dev, info_row.shape[1]), jnp.float32)] + [
         jax.ShapeDtypeStruct(shape, jnp.float32) for shape in piece_shapes
     ]
     return pl.pallas_call(
         functools.partial(open_kernel, n_gx, n_gy, m, len(blocks)),
         out_shape=out_shape,
-        in_specs=[vmem] * (1 + len(blocks) + len(corners)),
+        in_specs=[vmem] * (1 + len(blocks)),
         out_specs=[vmem] * len(out_shape),
         scratch_shapes=[
             pltpu.VMEM((2, depth, m, rows), jnp.float32),
+            pltpu.VMEM((len(HALO_MOVES) - 4, depth, m, m), jnp.float32),
             pltpu.VMEM((n_dev, info_row.shape[1]), jnp.float32),
             pltpu.SemaphoreType.DMA,
             pltpu.SemaphoreType.DMA,
@@ -148,7 +153,7 @@
             pltpu.SemaphoreType.DMA((len(piece_shapes),)),
         ],
         compiler_params=pltpu.CompilerParams(has_side_effects=True, collective_id=0),
-    )(info_row, *blocks, *corners)
+    )(info_row, *blocks)
 
 
 def close_kernel(n_gy, n_dev, src_ref, out_ref, slots, send_sem, recv_sem, local_sem):
@@ -184,19 +189,6 @@
         ],
         compiler_params=pltpu.CompilerParams(has_side_effects=True, collective_id=1),
     )(rows)
-
-
-def corner_pieces(blocks, m):
-    block = jnp.concatenate(
-        [jnp.concatenate([piece[:, :m], piece[:, -m:]], axis=1) for piece in blocks], axis=0
-    )
-    last_r, first_r = block[:, -m:, :], block[:, :m, :]
-    return (
-        jnp.swapaxes(last_r[:, :, -m:], 1, 2),
-        jnp.swapaxes(last_r[:, :, :m], 1, 2),
-        jnp.swapaxes(first_r[:, :, -m:], 1, 2),
-        jnp.swapaxes(first_r[:, :, :m], 1, 2),
-    )
 
 
 def column_band(landed, m, size_r, size_c, cols):
@@ -416,7 +408,7 @@
     )
     info_row = jnp.pad(jnp.concatenate(fields)[None, :], ((0, 0), (0, 128 - len(fields) * per)))
     blocks = (velocity, courant, viscosity, adjoint_seed)
-    opened = open_exchange(info_row, blocks, corner_pieces(blocks, m), m)
+    opened = open_exchange(info_row, blocks, m)
     info = opened[0]
     tiles = info[:, 0:per].astype(jnp.int32)
     row_start = tiles // n_gy * rows + info[:, per : 2 * per].astype(jnp.int32)

time: 86.4 us -> 81.1 us (0.939)
  local copies, waits for them, and re-layouts: 8.19 us -> 3.53 us
    unnamed x18 -> x14, local copies, waits for them, and re-layouts: 2.97 us -> 0.04 us
    slice x3 -> x0, local copies, waits for them, and re-layouts: 1.71 us -> none  [the longest x2 1.6 us: corner_pieces(): piece[:, :m]]
where the time goes in v5:
time: 81.1 us; the launch traced here: 80.9 us
  Pallas kernels  68.5 us (84%)
  matrix products  4.15 us (5%)
  other arithmetic  3.94 us (5%)
  local copies, waits for them, and re-layouts  3.53 us (4%)
  between operations  0.83 us (1%)
    pallas_call x1, Pallas kernels, open_exchange(): pl.pallas_call(functools.partial(open_kernel, n_gx, n_gy, m, len(blocks))...  35.1 us
    pallas_call x1, Pallas kernels, stencil(): pl.pallas_call(functools.partial(stencil_kernel, levels, STEPS, len(block...  20.8 us
    pallas_call x1, Pallas kernels, close_scatter(): pl.pallas_call(functools.partial(close_kernel, n_gy, n_dev), out_shape=ja...  12.5 us
    dot_general x1, matrix products, shards(): jnp.einsum('dkr,dkc->rc', thrusts[..., None] * prof_r, prof_c, precision=...  2.33 us

profile of v5, /device:TPU:1, one launch (start us, length us, event | category | flops | bytes accessed | tf_op | source)
XLA Modules:
  0.0 80.9 jit_solution(5410066423860443117)
XLA Ops:
  0.6 0.8 convert_bitcast_fusion
  1.4 0.7 concatenate.12
  2.1 0.5 pad.8.info_ref
  2.7 35.1 %shard_map.95 = (f32[128,128]{1,0:T(8,128)}, f32[12,16,128]{2,1,0:T(8,128)}, f32[12,16,128]{2,1,0:T(8,128)}, f32[12,16,256]{2,1,0:T(8,128)}, f32[12,16,256]{2,1,...) custom-call(f32[1,128]{1,0:T(1,128)} %pad.8.info_ref, ...), custom_call_target="tpu_custom_call" | custom-call | tf_op jit(solution)/shard_map/pallas_call | solution.py:140
  37.8 0.0 copy-start.6
  37.8 0.1 pad.14.clone
  37.9 1.6 %maximum_maximum_fusion.refs_6_ = f32[12,128,384]{2,1,0:T(8,128)S(1)} fusion(f32[12,16,96]{2,1,0:T(8,128)S(1)} %broadcast.97, f32[12,16,16]{2,1,0:T(8,128)} %get-tuple-element.20, f32[12,16,16]{2,1,0:T(8,128)} %get-tuple-element.19, f32[12,16,256]{2,1,0:T(8,128)} %get-tuple-element.18, f32[12,16,16]{2,1,0:T(8,128)} %get-tuple-element.17, ...), kind=kLoop, calls=%fused_computation | loop fusion | flops 4718592 | bytes 2875904 | tf_op jit(solution)/shard_map/concatenate | solution.py:208
  39.5 0.0 copy-done.6
  39.5 0.1 multiply_multiply_fusion
  39.6 0.1 copy.23
  39.7 0.1 copy.27
  39.8 0.1 fusion.11
  39.9 0.1 fusion.9
  40.0 0.1 copy.25
  40.0 0.1 copy.29
  40.1 0.0 copy-start
  40.1 0.0 copy-start.1
  40.1 0.0 copy-start.2
  40.1 0.0 copy-start.3
  40.2 0.0 copy-start.4
  40.2 0.0 copy-start.5
  40.2 2.3 %convolution_bitcast_fusion = f32[288,256]{1,0:T(8,128)S(1)} fusion(f32[128,4]{0,1:T(4,128)S(1)} %copy.23, f32[128,4]{0,1:T(4,128)S(1)} %copy.27, s32[128,4]{0,1:T(4,128)S(1)} %copy.25, s32[288]{0:T(512)S(1)} %fusion.14, s32[128,4]{0,1:T(4,128)S(1)} %copy.29, s32[256]{0:T(256)S(1)} %fusion.15), kind=kOutput, calls=%fused_computation.7 | convolution fusion | flops 458424320 | bytes 305280 | tf_op jit(solution)/shard_map/dkr,dkc->rc/dot_general | solution.py:427
  42.5 0.1 broadcast_multiply_fusion.refs_7_
  42.7 0.0 copy-done
  42.7 0.0 copy-done.1
  42.7 0.0 copy-done.2
  42.7 0.0 copy-done.3
  42.7 0.0 copy-done.4
  42.7 0.0 copy-done.5
  42.7 20.8 %shard_map.96 = (f32[3,256,128]{2,1,0:T(8,128)}, f32[3,256,128]{2,1,0:T(8,128)S(1)}) custom-call(f32[3,256,128]{2,1,0:T(8,128)S(1)} %copy-done, f32[3,256,128]{2,1,0:T(8,128)S(1)} %copy-done.1, f32[3,256,128]{2,1,0:T(8,128)S(1)} %copy-done.2, f32[3,256,128]{2,1,0:T(8,128)S(1)} %copy-done.3, f32[12,16,128]{2,1,0:T(8,128)S(1)} %copy-done.5, ...), custom_call_target="tpu_custom_call" | custom-call | flops 106168320 | bytes 6193152 | tf_op jit(solution)/shard_map/pallas_call | solution.py:304
  63.5 1.2 %fusion.4 = f32[1,256,128]{2,0,1:T(1,128)S(1)} fusion(f32[3,256,128]{2,1,0:T(8,128)S(1)} %get-tuple-element.23), kind=kOutput, calls=%fused_computation.18 | convolution fusion | flops 1179660 | bytes 524288 | tf_op jit(solution)/shard_map/l,lrc->rc/dot_general | solution.py:434
  64.7 0.6 exponential_select_fusion
  65.3 0.4 exponential_select_fusion.1
  65.7 0.7 fusion
  66.4 0.1 copy.32
  66.5 0.1 slice_multiply_fusion
  66.6 0.6 pad.9.src_ref
  67.2 12.5 %shard_map.97 = f32[1,128]{1,0:T(1,128)} custom-call(f32[128,128]{1,0:T(8,128)} %pad.9.src_ref), custom_call_target="tpu_custom_call" | custom-call | tf_op jit(solution)/shard_map/pallas_call | solution.py:179
  79.8 1.1 %slice_bitcast_fusion = f32[4]{0:T(128)} fusion(f32[1,128]{1,0:T(1,128)} %shard_map.97), kind=kLoop, calls=%fused_computation.46 | loop fusion | bytes 32 | tf_op jit(solution)/shard_map/squeeze | solution.py:441
  (5 shorter events, 0.0 us)
Async XLA Ops:
  37.8 1.7 %copy-start.6 = (f32[128,128]{1,0:T(8,128)S(1)}, f32[128,128]{1,0:T(8,128)}, u32[]{:S(2)}) copy-start(f32[128,128]{1,0:T(8,128)} %get-tuple-element.21) | copy-start | bytes 196612
  40.1 2.6 %copy-start = (f32[3,256,128]{2,1,0:T(8,128)S(1)}, f32[3,256,128]{2,1,0:T(8,128)}, u32[]{:S(2)}) copy-start(f32[3,256,128]{2,1,0:T(8,128)} %refs_0_.3) | copy-start | bytes 1179652
  40.1 2.6 %copy-start.1 = (f32[3,256,128]{2,1,0:T(8,128)S(1)}, f32[3,256,128]{2,1,0:T(8,128)}, u32[]{:S(2)}) copy-start(f32[3,256,128]{2,1,0:T(8,128)} %refs_1_.3) | copy-start | bytes 1179652
  40.1 2.6 %copy-start.2 = (f32[3,256,128]{2,1,0:T(8,128)S(1)}, f32[3,256,128]{2,1,0:T(8,128)}, u32[]{:S(2)}) copy-start(f32[3,256,128]{2,1,0:T(8,128)} %refs_2_.3) | copy-start | bytes 1179652
  40.1 2.6 %copy-start.3 = (f32[3,256,128]{2,1,0:T(8,128)S(1)}, f32[3,256,128]{2,1,0:T(8,128)}, u32[]{:S(2)}) copy-start(f32[3,256,128]{2,1,0:T(8,128)} %refs_3_.3) | copy-start | bytes 1179652
  40.2 2.6 %copy-start.4 = (f32[12,16,128]{2,1,0:T(8,128)S(1)}, f32[12,16,128]{2,1,0:T(8,128)}, u32[]{:S(2)}) copy-start(f32[12,16,128]{2,1,0:T(8,128)} %get-tuple-element.14.refs_5_) | copy-start | bytes 294916
  40.2 2.6 %copy-start.5 = (f32[12,16,128]{2,1,0:T(8,128)S(1)}, f32[12,16,128]{2,1,0:T(8,128)}, u32[]{:S(2)}) copy-start(f32[12,16,128]{2,1,0:T(8,128)} %get-tuple-element.13.refs_4_) | copy-start | bytes 294916

commit v6 on v5

--- a/solution.py
+++ b/solution.py
@@ -208,11 +208,21 @@
     return jnp.concatenate([edge(col_high, c_hh, c_lh), fill, edge(col_low, c_hl, c_ll)], axis=1)
 
 
-def stencil_kernel(levels, steps, n_block, *refs):
+def stencil_kernel(n_gx, n_gy, levels, steps, n_block, *refs):
     blocks = refs[:n_block]
-    high_ref, low_ref, band_ref, drag_ref, lam_out, sens_out, ext_ref, states, lams, sens_all = refs[
-        n_block:
-    ]
+    (
+        high_ref, low_ref, band_ref, drag_ref, row_ref, col_ref, thrust_ref, gain_ref,
+        lam_out, grad_out,
+        ext_ref, states, lams, sens_all, sending, slots, send_sem, recv_sem, local_sem,
+    ) = refs[n_block:]
+    n_dev = n_gx * n_gy
+    me = lax.axis_index("gx") * n_gy + lax.axis_index("gy")
+    barrier = pltpu.get_barrier_semaphore()
+    for step in range(1, n_dev):
+        target = lax.rem(me + step, n_dev)
+        pl.semaphore_signal(
+            barrier, inc=1, device_id=(target // n_gy, target % n_gy), device_id_type=MESH_ID
+        )
     size_r, size_c = ext_ref.shape[1:]
     rows, cols = blocks[0].shape[1:]
     m = high_ref.shape[1]
@@ -289,34 +299,64 @@
         return carry
 
     lax.fori_loop(0, steps, backward, 0)
-    for level in range(levels):
-        sens_out[level] = sens_all[level, :rows, :cols]
+    weighted = gain_ref[0] * sens_all[0, :rows, :cols]
+    for level in range(1, levels):
+        weighted = weighted + gain_ref[level] * sens_all[level, :rows, :cols]
+    sending[...] = jnp.zeros(sending.shape, jnp.float32)
+    for slot in range(row_ref.shape[0]):
+        across = jnp.dot(
+            weighted, col_ref[slot], precision=HIGHEST, preferred_element_type=jnp.float32
+        )
+        totals = jnp.sum(row_ref[slot] * across, axis=0, keepdims=True)
+        sending[slot : slot + 1, :] = thrust_ref[slot] * totals
+    sending[...] = sending[...].T
+    pl.semaphore_wait(barrier, n_dev - 1)
+    local = pltpu.make_async_copy(sending.at[pl.ds(me, 1)], slots.at[pl.ds(me, 1)], local_sem)
+    local.start()
+    every = spread_rows(
+        n_gy, n_dev, me, lambda target: sending.at[pl.ds(target, 1)], slots, send_sem, recv_sem
+    )
+    local.wait()
+    every.wait_send()
+    every.wait_recv()
+    grad_out[...] = jnp.sum(slots[...], axis=0, keepdims=True)
     for level in range(levels):
         lam_out[level] = lams[steps % 2, level, :rows, :cols]
 
 
-def stencil(blocks, landed, band, drag, levels):
+def stencil(blocks, landed, band, drag, levels, row_prof, col_prof, thrust_rows, gain_rows):
     size_r, size_c = drag.shape[1:]
     depth = levels * len(blocks)
     vmem = pl.BlockSpec(memory_space=pltpu.VMEM)
     plane = jax.ShapeDtypeStruct(blocks[0].shape, jnp.float32)
+    n_gx = lax.axis_size("gx")
+    n_gy = lax.axis_size("gy")
+    n_dev = n_gx * n_gy
+    width = row_prof.shape[2]
     cells = levels * size_r * size_c
     return pl.pallas_call(
-        functools.partial(stencil_kernel, levels, STEPS, len(blocks)),
-        out_shape=[plane, plane],
-        in_specs=[vmem] * (len(blocks) + 4),
+        functools.partial(stencil_kernel, n_gx, n_gy, levels, STEPS, len(blocks)),
+        out_shape=[plane, jax.ShapeDtypeStruct((1, width), jnp.float32)],
+        in_specs=[vmem] * (len(blocks) + 8),
         out_specs=[vmem, vmem],
         scratch_shapes=[
             pltpu.VMEM((depth, size_r, size_c), jnp.float32),
             pltpu.VMEM((STEPS, levels, size_r, size_c), jnp.float32),
             pltpu.VMEM((2, levels, size_r, size_c), jnp.float32),
             pltpu.VMEM((levels, size_r, size_c), jnp.float32),
+            pltpu.VMEM((width, width), jnp.float32),
+            pltpu.VMEM((n_dev, width), jnp.float32),
+            pltpu.SemaphoreType.DMA,
+            pltpu.SemaphoreType.DMA,
+            pltpu.SemaphoreType.DMA,
         ],
-        compiler_params=pltpu.CompilerParams(vmem_limit_bytes=48 * 1024 * 1024),
+        compiler_params=pltpu.CompilerParams(
+            vmem_limit_bytes=48 * 1024 * 1024, has_side_effects=True, collective_id=1
+        ),
         cost_estimate=pl.CostEstimate(
             flops=60 * STEPS * cells, transcendentals=3 * STEPS * cells, bytes_accessed=28 * cells
         ),
-    )(*blocks, landed[1], landed[0], band, drag)
+    )(*blocks, landed[1], landed[0], band, drag, row_prof, col_prof, thrust_rows, gain_rows)
 
 
 def drag_law(state):
@@ -427,19 +467,15 @@
     plane = jnp.einsum("dkr,dkc->rc", thrusts[..., None] * prof_r, prof_c, precision=HIGHEST)
     drag = gain[:, None, None] * plane[None]
     band = column_band(opened[1:], m, size_r, size_c, cols)
-    adjoint_full, sens_full = stencil(blocks, opened[1:], band, drag, levels)
-    adjoint = adjoint_full
-    sensitivity = sens_full
-
-    weighted = jnp.einsum("l,lrc->rc", gain, sensitivity, precision=HIGHEST)
-    own_r = prof_r[..., :rows]
-    own_c = prof_c[..., :cols]
-    across = jnp.einsum("rc,dkc->dkr", weighted, own_c, precision=HIGHEST)
-    totals = jnp.sum(own_r * across, axis=2)
-    values = thrusts * totals
-    spread = jnp.pad(values, ((0, 0), (0, 128 - per)))
-    grad = close_scatter(spread)[0, :per]
-    return adjoint, grad
+    spare = ((0, 0), (0, 0), (0, -(-n_gx * n_gy // 128) * 128 - n_gx * n_gy))
+    row_prof = jnp.pad(jnp.transpose(prof_r[..., :rows], (1, 2, 0)), spare)
+    col_prof = jnp.pad(jnp.transpose(prof_c[..., :cols], (1, 2, 0)), spare)
+    thrust_rows = jnp.pad(jnp.transpose(thrusts)[:, None, :], spare)
+    gain_rows = jnp.broadcast_to(gain[:, None, None], (levels, 1, cols))
+    adjoint, grad = stencil(
+        blocks, opened[1:], band, drag, levels, row_prof, col_prof, thrust_rows, gain_rows
+    )
+    return adjoint, grad[0, :per]
 
 
 def solution(mesh):

time: 81.1 us -> 72.3 us (0.89)
  Pallas kernels: 68.5 us -> 63 us
  matrix products: 4.15 us -> 1.49 us
    pallas_call x2 -> x1, Pallas kernels: 33.3 us -> 27.8 us  [stencil(): pl.pallas_call(functools.partial(stencil_kernel, n_gx, n_gy, levels, STEP...]
    dot_general x2 -> x0, matrix products: 1.82 us -> none  [the longest x1 1.15 us: shards(): weighted = jnp.einsum('l,lrc->rc', gain, sensitivity, precision=HIGHEST)]
    dot_general x1, matrix products: 2.33 us -> 1.49 us  [shards(): jnp.einsum('dkr,dkc->rc', thrusts[..., None] * prof_r, prof_c, precision=...]
    unnamed x14 -> x15, local copies, waits for them, and re-layouts: 0.04 us -> 0.88 us
where the time goes in v6:
time: 72.3 us; the launch traced here: 72.1 us
  Pallas kernels  63 us (87%)
  other arithmetic  3.68 us (5%)
  local copies, waits for them, and re-layouts  3.16 us (4%)
  matrix products  1.49 us (2%)
  between operations  0.81 us (1%)
    pallas_call x1, Pallas kernels, open_exchange(): pl.pallas_call(functools.partial(open_kernel, n_gx, n_gy, m, len(blocks))...  35.2 us
    pallas_call x1, Pallas kernels, stencil(): pl.pallas_call(functools.partial(stencil_kernel, n_gx, n_gy, levels, STEP...  27.8 us
    concatenate x1, other arithmetic, column_band(): jnp.concatenate([edge(col_high, c_hh, c_lh), fill, edge(col_low, c_hl, c_...  1.58 us
    dot_general x1, matrix products, shards(): jnp.einsum('dkr,dkc->rc', thrusts[..., None] * prof_r, prof_c, precision=...  1.49 us

profile of v6, /device:TPU:1, one launch (start us, length us, event | category | flops | bytes accessed | tf_op | source)
XLA Modules:
  0.0 72.1 jit_solution(9972931544222674152)
XLA Ops:
  0.6 0.8 %convert_bitcast_fusion = (f32[4]{0:T(128)S(1)}, f32[4]{0:T(128)S(1)}, f32[4]{0:T(128)S(1)}) fusion(s32[4,2]{0,1:T(2,128)} %param.13, s32[4,1]{0,1:T(1,128)} %param.12), kind=kLoop, calls=%fused_computation.43 | loop fusion | flops 12 | bytes 96 | tf_op jit(solution)/shard_map/convert_element_type | solution.py:445
  1.4 0.7 %concatenate.12 = f32[20]{0:T(128)S(1)} concatenate(f32[4]{0:T(128)S(1)} %get-tuple-element.28, f32[4]{0:T(128)S(1)} %get-tuple-element.27, f32[4]{0:T(128)S(1)} %get-tuple-element.26, f32[4]{0:T(128)} %param.14, f32[4]{0:T(128)} %param.15), dimensions={0} | concatenate | bytes 160 | tf_op jit(solution)/shard_map/concatenate | solution.py:449
  2.1 0.5 pad.4.info_ref
  2.7 35.2 %shard_map.95 = (f32[128,128]{1,0:T(8,128)}, f32[12,16,128]{2,1,0:T(8,128)}, f32[12,16,128]{2,1,0:T(8,128)}, f32[12,16,256]{2,1,0:T(8,128)}, f32[12,16,256]{2,1,...) custom-call(f32[1,128]{1,0:T(1,128)} %pad.4.info_ref, ...), custom_call_target="tpu_custom_call" | custom-call | tf_op jit(solution)/shard_map/pallas_call | solution.py:140
  37.8 0.0 copy-start.6
  37.9 0.1 pad.9.clone
  38.0 1.6 %maximum_maximum_fusion.refs_6_ = f32[12,128,384]{2,1,0:T(8,128)S(1)} fusion(f32[12,16,96]{2,1,0:T(8,128)S(1)} %broadcast.90, f32[12,16,16]{2,1,0:T(8,128)} %get-tuple-element.20, f32[12,16,16]{2,1,0:T(8,128)} %get-tuple-element.19, f32[12,16,256]{2,1,0:T(8,128)} %get-tuple-element.18, f32[12,16,16]{2,1,0:T(8,128)} %get-tuple-element.17, ...), kind=kLoop, calls=%fused_computation | loop fusion | flops 4718592 | bytes 2875904 | tf_op jit(solution)/shard_map/concatenate | solution.py:208
  39.5 0.0 copy-done.6
  39.5 0.1 copy.16
  39.7 0.1 multiply_multiply_fusion
  39.7 0.1 copy.20
  39.8 0.1 fusion.7
  39.9 0.1 fusion.5
  40.0 0.1 copy.18
  40.1 0.1 copy.22
  40.2 1.5 %convolution_bitcast_fusion = f32[288,256]{1,0:T(8,128)S(1)} fusion(f32[128,4]{0,1:T(4,128)S(1)} %slice.40, f32[128,4]{0,1:T(4,128)S(1)} %copy.20, s32[128,4]{0,1:T(4,128)S(1)} %copy.18, s32[288]{0:T(512)S(1)} %fusion.10, s32[128,4]{0,1:T(4,128)S(1)} %copy.22, s32[256]{0:T(256)S(1)} %fusion.11), kind=kOutput, calls=%fused_computation.1 | convolution fusion | flops 458424320 | bytes 305280 | tf_op jit(solution)/shard_map/dkr,dkc->rc/dot_general | solution.py:467
  41.6 0.0 copy-start
  41.7 0.0 copy-start.1
  41.7 0.0 copy-start.2
  41.7 0.0 copy-start.3
  41.7 0.0 copy-start.4
  41.7 0.0 copy-start.5
  41.7 0.1 broadcast_multiply_fusion.refs_7_
  41.9 0.5 exponential_select_fusion
  42.4 0.4 exponential_select_fusion.1
  42.9 0.1 broadcast_in_dim.21.refs_11_
  42.9 0.0 copy-done
  42.9 0.0 copy-done.1
  42.9 0.0 copy-done.2
  42.9 0.1 copy-done.3
  43.0 0.0 copy-done.4
  43.0 0.0 copy-done.5
  43.1 27.8 %shard_map.96 = (f32[3,256,128]{2,1,0:T(8,128)S(1)}, f32[1,128]{1,0:T(1,128)S(1)}) custom-call(f32[3,256,128]{2,1,0:T(8,128)S(1)} %copy-done, f32[3,256,128]{2,1,0:T(8,128)S(1)} %copy-done.1, f32[3,256,128]{2,1,0:T(8,128)S(1)} %copy-done.2, f32[3,256,128]{2,1,0:T(8,128)S(1)} %copy-done.3, f32[12,16,128]{2,1,0:T(8,128)S(1)} %copy-done.5, ...), custom_call_target="tpu_custom_call" | custom-call | flops 106168320 | bytes 6193152 | tf_op jit(solution)/shard_map/pallas_call | solution.py:337
  70.9 0.5 slice_bitcast_fusion.2
  71.4 0.7 %copy.29 = f32[3,256,128]{2,1,0:T(8,128)} copy(f32[3,256,128]{2,1,0:T(8,128)S(1)} %get-tuple-element.31) | data formatting | bytes 786432
  (8 shorter events, 0.1 us)
Async XLA Ops:
  37.8 1.7 %copy-start.6 = (f32[128,128]{1,0:T(8,128)S(1)}, f32[128,128]{1,0:T(8,128)}, u32[]{:S(2)}) copy-start(f32[128,128]{1,0:T(8,128)} %get-tuple-element.21) | copy-start | bytes 196612
  41.6 1.3 %copy-start = (f32[3,256,128]{2,1,0:T(8,128)S(1)}, f32[3,256,128]{2,1,0:T(8,128)}, u32[]{:S(2)}) copy-start(f32[3,256,128]{2,1,0:T(8,128)} %refs_0_.3) | copy-start | bytes 1179652
  41.7 1.3 %copy-start.1 = (f32[3,256,128]{2,1,0:T(8,128)S(1)}, f32[3,256,128]{2,1,0:T(8,128)}, u32[]{:S(2)}) copy-start(f32[3,256,128]{2,1,0:T(8,128)} %refs_1_.3) | copy-start | bytes 1179652
  41.7 1.3 %copy-start.2 = (f32[3,256,128]{2,1,0:T(8,128)S(1)}, f32[3,256,128]{2,1,0:T(8,128)}, u32[]{:S(2)}) copy-start(f32[3,256,128]{2,1,0:T(8,128)} %refs_2_.3) | copy-start | bytes 1179652
  41.7 1.3 %copy-start.3 = (f32[3,256,128]{2,1,0:T(8,128)S(1)}, f32[3,256,128]{2,1,0:T(8,128)}, u32[]{:S(2)}) copy-start(f32[3,256,128]{2,1,0:T(8,128)} %refs_3_.3) | copy-start | bytes 1179652
  41.7 1.3 %copy-start.4 = (f32[12,16,128]{2,1,0:T(8,128)S(1)}, f32[12,16,128]{2,1,0:T(8,128)}, u32[]{:S(2)}) copy-start(f32[12,16,128]{2,1,0:T(8,128)} %get-tuple-element.14.refs_5_) | copy-start | bytes 294916
  41.7 1.3 %copy-start.5 = (f32[12,16,128]{2,1,0:T(8,128)S(1)}, f32[12,16,128]{2,1,0:T(8,128)}, u32[]{:S(2)}) copy-start(f32[12,16,128]{2,1,0:T(8,128)} %get-tuple-element.13.refs_4_) | copy-start | bytes 294916

commit v7 on v6

--- a/solution.py
+++ b/solution.py
@@ -23,14 +23,14 @@
 HALO_MOVES = ((1, 0), (-1, 0), (0, 1), (0, -1), (1, 1), (1, -1), (-1, 1), (-1, -1))
 
 
-def enter(n_gy, n_dev, me):
+def greet(n_gy, n_dev, me):
     barrier = pltpu.get_barrier_semaphore()
     for step in range(1, n_dev):
         target = lax.rem(me + step, n_dev)
         pl.semaphore_signal(
             barrier, inc=1, device_id=(target // n_gy, target % n_gy), device_id_type=MESH_ID
         )
-    pl.semaphore_wait(barrier, n_dev - 1)
+    return barrier
 
 
 def spread_rows(n_gy, n_dev, me, src_of, slots, send_sem, recv_sem):
@@ -66,6 +66,10 @@
         n_block + n_corner + 1 + len(HALO_MOVES) :
     ]
     levels, rows, cols = blocks[0].shape
+    gx = lax.axis_index("gx")
+    gy = lax.axis_index("gy")
+    me = gx * n_gy + gy
+    barrier = greet(n_gy, n_dev, me)
     for field, block_ref in enumerate(blocks):
         for level in range(levels):
             turned = block_ref[level].T
@@ -76,10 +80,7 @@
                 ((cols - m, rows - m), (0, rows - m), (cols - m, 0), (0, 0))
             ):
                 corners[index, depth] = turned[side : side + m, window : window + m]
-    gx = lax.axis_index("gx")
-    gy = lax.axis_index("gy")
-    me = gx * n_gy + gy
-    enter(n_gy, n_dev, me)
+    pl.semaphore_wait(barrier, n_dev - 1)
     local = pltpu.make_async_copy(info_ref, slots.at[pl.ds(me, 1)], local_sem)
     local.start()
     parts = lambda window: [
@@ -156,41 +157,6 @@
     )(info_row, *blocks)
 
 
-def close_kernel(n_gy, n_dev, src_ref, out_ref, slots, send_sem, recv_sem, local_sem):
-    gx = lax.axis_index("gx")
-    gy = lax.axis_index("gy")
-    me = gx * n_gy + gy
-    enter(n_gy, n_dev, me)
-    local = pltpu.make_async_copy(src_ref.at[pl.ds(me, 1)], slots.at[pl.ds(me, 1)], local_sem)
-    local.start()
-    every = spread_rows(
-        n_gy, n_dev, me, lambda target: src_ref.at[pl.ds(target, 1)], slots, send_sem, recv_sem
-    )
-    local.wait()
-    every.wait_send()
-    every.wait_recv()
-    out_ref[...] = jnp.sum(slots[...], axis=0, keepdims=True)
-
-
-def close_scatter(rows):
-    n_gy = lax.axis_size("gy")
-    n_dev = lax.axis_size("gx") * n_gy
-    vmem = pl.BlockSpec(memory_space=pltpu.VMEM)
-    return pl.pallas_call(
-        functools.partial(close_kernel, n_gy, n_dev),
-        out_shape=jax.ShapeDtypeStruct((1, rows.shape[1]), jnp.float32),
-        in_specs=[vmem],
-        out_specs=vmem,
-        scratch_shapes=[
-            pltpu.VMEM(rows.shape, jnp.float32),
-            pltpu.SemaphoreType.DMA,
-            pltpu.SemaphoreType.DMA,
-            pltpu.SemaphoreType.DMA,
-        ],
-        compiler_params=pltpu.CompilerParams(has_side_effects=True, collective_id=1),
-    )(rows)
-
-
 def column_band(landed, m, size_r, size_c, cols):
     row_low, row_high, col_low, col_high, c_ll, c_lh, c_hl, c_hh = landed
     depth = col_low.shape[0]
@@ -217,12 +183,7 @@
     ) = refs[n_block:]
     n_dev = n_gx * n_gy
     me = lax.axis_index("gx") * n_gy + lax.axis_index("gy")
-    barrier = pltpu.get_barrier_semaphore()
-    for step in range(1, n_dev):
-        target = lax.rem(me + step, n_dev)
-        pl.semaphore_signal(
-            barrier, inc=1, device_id=(target // n_gy, target % n_gy), device_id_type=MESH_ID
-        )
+    barrier = greet(n_gy, n_dev, me)
     size_r, size_c = ext_ref.shape[1:]
     rows, cols = blocks[0].shape[1:]
     m = high_ref.shape[1]
@@ -446,7 +407,8 @@
         thrust,
         disk_width,
     )
-    info_row = jnp.pad(jnp.concatenate(fields)[None, :], ((0, 0), (0, 128 - len(fields) * per)))
+    spare = jnp.zeros((128 - len(fields) * per,), jnp.float32)
+    info_row = jnp.concatenate(fields + (spare,))[None, :]
     blocks = (velocity, courant, viscosity, adjoint_seed)
     opened = open_exchange(info_row, blocks, m)
     info = opened[0]

time: 72.3 us -> 71.5 us (0.989)
  Pallas kernels: 63 us -> 62.1 us
    pallas_call x1, Pallas kernels: 35.2 us -> 34.4 us  [open_exchange(): pl.pallas_call(functools.partial(open_kernel, n_gx, n_gy, m, len(blocks))...]
where the time goes in v7:
time: 71.5 us; the launch traced here: 71.3 us
  Pallas kernels  62.1 us (87%)
  other arithmetic  3.68 us (5%)
  local copies, waits for them, and re-layouts  3.16 us (4%)
  matrix products  1.49 us (2%)
  between operations  0.81 us (1%)
    pallas_call x1, Pallas kernels, open_exchange(): pl.pallas_call(functools.partial(open_kernel, n_gx, n_gy, m, len(blocks))...  34.4 us
    pallas_call x1, Pallas kernels, stencil(): pl.pallas_call(functools.partial(stencil_kernel, n_gx, n_gy, levels, STEP...  27.8 us
    concatenate x1, other arithmetic, column_band(): jnp.concatenate([edge(col_high, c_hh, c_lh), fill, edge(col_low, c_hl, c_...  1.58 us
    dot_general x1, matrix products, shards(): jnp.einsum('dkr,dkc->rc', thrusts[..., None] * prof_r, prof_c, precision=...  1.49 us

profile of v7, /device:TPU:1, one launch (start us, length us, event | category | flops | bytes accessed | tf_op | source)
XLA Modules:
  0.0 71.3 jit_solution(15406045165853622872)
XLA Ops:
  0.6 0.8 %convert_bitcast_fusion = (f32[4]{0:T(128)S(1)}, f32[4]{0:T(128)S(1)}, f32[4]{0:T(128)S(1)}) fusion(s32[4,2]{0,1:T(2,128)} %param.13, s32[4,1]{0,1:T(1,128)} %param.12), kind=kLoop, calls=%fused_computation.43 | loop fusion | flops 12 | bytes 96 | tf_op jit(solution)/shard_map/convert_element_type | solution.py:406
  1.4 1.3 %concatenate.12 = f32[128]{0:T(128)} concatenate(f32[4]{0:T(128)S(1)} %get-tuple-element.28, f32[4]{0:T(128)S(1)} %get-tuple-element.27, f32[4]{0:T(128)S(1)} %get-tuple-element.26, f32[4]{0:T(128)} %param.14, f32[4]{0:T(128)} %param.15, f32[108]{0:T(128)S(1)} %broadcast_in_dim.18), dimensions={0} | concatenate | bytes 1024 | tf_op jit(solution)/shard_map/concatenate | solution.py:411
  2.7 34.4 %shard_map.95 = (f32[128,128]{1,0:T(8,128)}, f32[12,16,128]{2,1,0:T(8,128)}, f32[12,16,128]{2,1,0:T(8,128)}, f32[12,16,256]{2,1,0:T(8,128)}, f32[12,16,256]{2,1,...) custom-call(f32[1,128]{1,0:T(1,128)} %bitcast.19, ...), custom_call_target="tpu_custom_call" | custom-call | tf_op jit(solution)/shard_map/pallas_call | solution.py:141
  37.0 0.0 copy-start.6
  37.0 0.1 pad.4.clone
  37.1 1.6 %maximum_maximum_fusion.refs_6_ = f32[12,128,384]{2,1,0:T(8,128)S(1)} fusion(f32[12,16,96]{2,1,0:T(8,128)S(1)} %broadcast.88, f32[12,16,16]{2,1,0:T(8,128)} %get-tuple-element.20, f32[12,16,16]{2,1,0:T(8,128)} %get-tuple-element.19, f32[12,16,256]{2,1,0:T(8,128)} %get-tuple-element.18, f32[12,16,16]{2,1,0:T(8,128)} %get-tuple-element.17, ...), kind=kLoop, calls=%fused_computation | loop fusion | flops 4718592 | bytes 2875904 | tf_op jit(solution)/shard_map/concatenate | solution.py:174
  38.7 0.0 copy-done.6
  38.7 0.1 copy.16
  38.8 0.1 multiply_multiply_fusion
  38.9 0.1 copy.20
  39.0 0.1 fusion.7
  39.1 0.1 fusion.5
  39.2 0.1 copy.18
  39.2 0.1 copy.22
  39.3 1.5 %convolution_bitcast_fusion = f32[288,256]{1,0:T(8,128)S(1)} fusion(f32[128,4]{0,1:T(4,128)S(1)} %slice.40, f32[128,4]{0,1:T(4,128)S(1)} %copy.20, s32[128,4]{0,1:T(4,128)S(1)} %copy.18, s32[288]{0:T(512)S(1)} %fusion.10, s32[128,4]{0,1:T(4,128)S(1)} %copy.22, s32[256]{0:T(256)S(1)} %fusion.11), kind=kOutput, calls=%fused_computation.1 | convolution fusion | flops 458424320 | bytes 305280 | tf_op jit(solution)/shard_map/dkr,dkc->rc/dot_general | solution.py:429
  40.8 0.0 copy-start
  40.8 0.0 copy-start.1
  40.8 0.0 copy-start.2
  40.9 0.0 copy-start.3
  40.9 0.0 copy-start.4
  40.9 0.0 copy-start.5
  40.9 0.1 broadcast_multiply_fusion.refs_7_
  41.1 0.5 exponential_select_fusion
  41.6 0.4 exponential_select_fusion.1
  42.0 0.1 broadcast_in_dim.43.refs_11_
  42.1 0.0 copy-done
  42.1 0.0 copy-done.1
  42.1 0.0 copy-done.2
  42.1 0.1 copy-done.3
  42.2 0.0 copy-done.4
  42.2 0.0 copy-done.5
  42.2 27.8 %shard_map.96 = (f32[3,256,128]{2,1,0:T(8,128)S(1)}, f32[1,128]{1,0:T(1,128)S(1)}) custom-call(f32[3,256,128]{2,1,0:T(8,128)S(1)} %copy-done, f32[3,256,128]{2,1,0:T(8,128)S(1)} %copy-done.1, f32[3,256,128]{2,1,0:T(8,128)S(1)} %copy-done.2, f32[3,256,128]{2,1,0:T(8,128)S(1)} %copy-done.3, f32[12,16,128]{2,1,0:T(8,128)S(1)} %copy-done.5, ...), custom_call_target="tpu_custom_call" | custom-call | flops 106168320 | bytes 6193152 | tf_op jit(solution)/shard_map/pallas_call | solution.py:298
  70.0 0.5 slice_bitcast_fusion.2
  70.5 0.7 %copy.29 = f32[3,256,128]{2,1,0:T(8,128)} copy(f32[3,256,128]{2,1,0:T(8,128)S(1)} %get-tuple-element.31) | data formatting | bytes 786432
  (9 shorter events, 0.1 us)
Async XLA Ops:
  37.0 1.7 %copy-start.6 = (f32[128,128]{1,0:T(8,128)S(1)}, f32[128,128]{1,0:T(8,128)}, u32[]{:S(2)}) copy-start(f32[128,128]{1,0:T(8,128)} %get-tuple-element.21) | copy-start | bytes 196612
  40.8 1.3 %copy-start = (f32[3,256,128]{2,1,0:T(8,128)S(1)}, f32[3,256,128]{2,1,0:T(8,128)}, u32[]{:S(2)}) copy-start(f32[3,256,128]{2,1,0:T(8,128)} %refs_0_.3) | copy-start | bytes 1179652
  40.8 1.3 %copy-start.1 = (f32[3,256,128]{2,1,0:T(8,128)S(1)}, f32[3,256,128]{2,1,0:T(8,128)}, u32[]{:S(2)}) copy-start(f32[3,256,128]{2,1,0:T(8,128)} %refs_1_.3) | copy-start | bytes 1179652
  40.8 1.3 %copy-start.2 = (f32[3,256,128]{2,1,0:T(8,128)S(1)}, f32[3,256,128]{2,1,0:T(8,128)}, u32[]{:S(2)}) copy-start(f32[3,256,128]{2,1,0:T(8,128)} %refs_2_.3) | copy-start | bytes 1179652
  40.9 1.3 %copy-start.3 = (f32[3,256,128]{2,1,0:T(8,128)S(1)}, f32[3,256,128]{2,1,0:T(8,128)}, u32[]{:S(2)}) copy-start(f32[3,256,128]{2,1,0:T(8,128)} %refs_3_.3) | copy-start | bytes 1179652
  40.9 1.3 %copy-start.4 = (f32[12,16,128]{2,1,0:T(8,128)S(1)}, f32[12,16,128]{2,1,0:T(8,128)}, u32[]{:S(2)}) copy-start(f32[12,16,128]{2,1,0:T(8,128)} %get-tuple-element.14.refs_5_) | copy-start | bytes 294916
  40.9 1.3 %copy-start.5 = (f32[12,16,128]{2,1,0:T(8,128)S(1)}, f32[12,16,128]{2,1,0:T(8,128)}, u32[]{:S(2)}) copy-start(f32[12,16,128]{2,1,0:T(8,128)} %get-tuple-element.13.refs_4_) | copy-start | bytes 294916

commit v8 on v7

--- a/solution.py
+++ b/solution.py
@@ -157,29 +157,13 @@
     )(info_row, *blocks)
 
 
-def column_band(landed, m, size_r, size_c, cols):
-    row_low, row_high, col_low, col_high, c_ll, c_lh, c_hl, c_hh = landed
-    depth = col_low.shape[0]
-    width = size_c - cols
-    span = -(-size_r // 128) * 128
-
-    def edge(column, high_corner, low_corner):
-        fill = jnp.zeros((depth, m, span - size_r), jnp.float32)
-        return jnp.concatenate(
-            [column, high_corner, low_corner, fill],
-            axis=2,
-        )
-
-    fill = jnp.zeros((depth, width - 2 * m, span), jnp.float32)
-    return jnp.concatenate([edge(col_high, c_hh, c_lh), fill, edge(col_low, c_hl, c_ll)], axis=1)
-
-
 def stencil_kernel(n_gx, n_gy, levels, steps, n_block, *refs):
     blocks = refs[:n_block]
     (
-        high_ref, low_ref, band_ref, drag_ref, row_ref, col_ref, thrust_ref, gain_ref,
+        high_ref, low_ref, col_low, col_high, c_ll, c_lh, c_hl, c_hh,
+        drag_ref, row_ref, col_ref, thrust_ref, gain_ref,
         lam_out, grad_out,
-        ext_ref, states, lams, sens_all, sending, slots, send_sem, recv_sem, local_sem,
+        ext_ref, states, lams, sens_all, sending, slots, band, send_sem, recv_sem, local_sem,
     ) = refs[n_block:]
     n_dev = n_gx * n_gy
     me = lax.axis_index("gx") * n_gy + lax.axis_index("gy")
@@ -187,11 +171,20 @@
     size_r, size_c = ext_ref.shape[1:]
     rows, cols = blocks[0].shape[1:]
     m = high_ref.shape[1]
+    band[...] = jnp.zeros(band.shape, jnp.float32)
+    width = size_c - cols
     for depth in range(ext_ref.shape[0]):
         ext_ref[depth, :rows, :cols] = blocks[depth // levels][depth % levels]
         ext_ref[depth, rows : rows + m, :cols] = high_ref[depth]
         ext_ref[depth, size_r - m :, :cols] = low_ref[depth]
-        ext_ref[depth, :, cols:] = band_ref[depth].T[:size_r]
+        for first, column, high_corner, low_corner in (
+            (0, col_high, c_hh, c_lh),
+            (width - m, col_low, c_hl, c_ll),
+        ):
+            band[first : first + m, :rows] = column[depth]
+            band[first : first + m, rows : rows + m] = high_corner[depth]
+            band[first : first + m, size_r - m : size_r] = low_corner[depth]
+        ext_ref[depth, :, cols:] = band[...].T[:size_r]
 
     def west(x):
         return pltpu.roll(x, 1, 0)
@@ -252,8 +245,7 @@
                 adjoint
                 - flux_adv
                 - 4.0 * flux_dif
-                + east(flux_adv)
-                + (east(flux_dif) + west(flux_dif) + north(flux_dif) + south(flux_dif))
+                + (east(flux_adv + flux_dif) + west(flux_dif) + north(flux_dif) + south(flux_dif))
                 + VERTICAL_MIX * vertical(lambda l: lams[now, l], level, adjoint)
                 - drag_ref[level] * slope * adjoint
             )
@@ -285,7 +277,7 @@
         lam_out[level] = lams[steps % 2, level, :rows, :cols]
 
 
-def stencil(blocks, landed, band, drag, levels, row_prof, col_prof, thrust_rows, gain_rows):
+def stencil(blocks, landed, drag, levels, row_prof, col_prof, thrust_rows, gain_rows):
     size_r, size_c = drag.shape[1:]
     depth = levels * len(blocks)
     vmem = pl.BlockSpec(memory_space=pltpu.VMEM)
@@ -298,7 +290,7 @@
     return pl.pallas_call(
         functools.partial(stencil_kernel, n_gx, n_gy, levels, STEPS, len(blocks)),
         out_shape=[plane, jax.ShapeDtypeStruct((1, width), jnp.float32)],
-        in_specs=[vmem] * (len(blocks) + 8),
+        in_specs=[vmem] * (len(blocks) + 13),
         out_specs=[vmem, vmem],
         scratch_shapes=[
             pltpu.VMEM((depth, size_r, size_c), jnp.float32),
@@ -307,6 +299,7 @@
             pltpu.VMEM((levels, size_r, size_c), jnp.float32),
             pltpu.VMEM((width, width), jnp.float32),
             pltpu.VMEM((n_dev, width), jnp.float32),
+            pltpu.VMEM((size_c - blocks[0].shape[2], -(-size_r // 128) * 128), jnp.float32),
             pltpu.SemaphoreType.DMA,
             pltpu.SemaphoreType.DMA,
             pltpu.SemaphoreType.DMA,
@@ -317,7 +310,7 @@
         cost_estimate=pl.CostEstimate(
             flops=60 * STEPS * cells, transcendentals=3 * STEPS * cells, bytes_accessed=28 * cells
         ),
-    )(*blocks, landed[1], landed[0], band, drag, row_prof, col_prof, thrust_rows, gain_rows)
+    )(*blocks, landed[1], landed[0], *landed[2:], drag, row_prof, col_prof, thrust_rows, gain_rows)
 
 
 def drag_law(state):
@@ -428,14 +421,13 @@
     gain = level_gain()
     plane = jnp.einsum("dkr,dkc->rc", thrusts[..., None] * prof_r, prof_c, precision=HIGHEST)
     drag = gain[:, None, None] * plane[None]
-    band = column_band(opened[1:], m, size_r, size_c, cols)
     spare = ((0, 0), (0, 0), (0, -(-n_gx * n_gy // 128) * 128 - n_gx * n_gy))
     row_prof = jnp.pad(jnp.transpose(prof_r[..., :rows], (1, 2, 0)), spare)
     col_prof = jnp.pad(jnp.transpose(prof_c[..., :cols], (1, 2, 0)), spare)
     thrust_rows = jnp.pad(jnp.transpose(thrusts)[:, None, :], spare)
     gain_rows = jnp.broadcast_to(gain[:, None, None], (levels, 1, cols))
     adjoint, grad = stencil(
-        blocks, opened[1:], band, drag, levels, row_prof, col_prof, thrust_rows, gain_rows
+        blocks, opened[1:], drag, levels, row_prof, col_prof, thrust_rows, gain_rows
     )
     return adjoint, grad[0, :per]
 

time: 71.5 us -> 72 us (level)
  local copies, waits for them, and re-layouts: 3.16 us -> 5.62 us
  other arithmetic: 3.68 us -> 2.18 us
    unnamed x15 -> x35, local copies, waits for them, and re-layouts: 0.88 us -> 4.11 us
    concatenate x1 -> x0, other arithmetic: 1.58 us -> none  [column_band(): jnp.concatenate([edge(col_high, c_hh, c_lh), fill, edge(col_low, c_hl, c_...]
    mul x1, other arithmetic: 0.08 us -> 0.92 us  [profiles(): 2.0 * widths[..., None] * widths[..., None]]
    convert_element_type x1, other arithmetic: 0.76 us -> 0.01 us  [shards(): turbine_offset[:, 1].astype(jnp.float32)]
where the time goes in v8:
time: 72 us; the launch traced here: 71.7 us
  Pallas kernels  61.5 us (85%)
  local copies, waits for them, and re-layouts  5.62 us (8%)
  other arithmetic  2.18 us (3%)
  matrix products  1.48 us (2%)
  between operations  0.89 us (1%)
    pallas_call x1, Pallas kernels, open_exchange(): pl.pallas_call(functools.partial(open_kernel, n_gx, n_gy, m, len(blocks))...  34.4 us
    pallas_call x1, Pallas kernels, stencil(): pl.pallas_call(functools.partial(stencil_kernel, n_gx, n_gy, levels, STEP...  27.2 us
    unnamed x35, local copies, waits for them, and re-layouts  4.11 us
    dot_general x1, matrix products, shards(): jnp.einsum('dkr,dkc->rc', thrusts[..., None] * prof_r, prof_c, precision=...  1.48 us

profile of v8, /device:TPU:1, one launch (start us, length us, event | category | flops | bytes accessed | tf_op | source)
XLA Modules:
  0.0 71.7 jit_solution(1073809577022051563)
XLA Ops:
  0.7 0.0 copy-start.13
  0.7 0.0 copy-start.16
  0.7 0.1 broadcast_in_dim.21.refs_16_
  0.8 0.6 copy-done.13
  1.4 0.0 copy-done.16
  1.4 0.0 copy-start.14
  1.4 0.0 copy-start.15
  1.4 0.6 copy-done.14
  2.0 0.0 copy-done.15
  2.0 0.6 concatenate.3
  2.6 34.4 %shard_map.95 = (f32[128,128]{1,0:T(8,128)}, f32[12,16,128]{2,1,0:T(8,128)}, f32[12,16,128]{2,1,0:T(8,128)}, f32[12,16,256]{2,1,0:T(8,128)}, f32[12,16,256]{2,1,...) custom-call(f32[1,128]{1,0:T(1,128)} %bitcast.19, ...), custom_call_target="tpu_custom_call" | custom-call | tf_op jit(solution)/shard_map/pallas_call | solution.py:141
  37.0 0.9 %multiply_multiply_fusion = f32[128,4]{1,0:T(8,128)S(1)} fusion(f32[128,128]{1,0:T(8,128)} %get-tuple-element.21), kind=kLoop, calls=%fused_computation.21 | loop fusion | flops 1024 | bytes 4096 | tf_op jit(solution)/shard_map/mul | solution.py:379
  37.9 0.0 copy-start.12
  37.9 0.1 copy.20
  38.0 0.8 %copy-done.12 = f32[128,128]{1,0:T(8,128)S(1)} copy-done((f32[128,128]{1,0:T(8,128)S(1)}, f32[128,128]{1,0:T(8,128)}, u32[]{:S(2)}) %copy-start.12) | copy-done | bytes 65560
  38.8 0.1 copy.16
  38.9 0.1 fusion.7
  39.0 0.1 copy.22
  39.0 0.1 fusion.5
  39.1 0.1 copy.18
  39.2 1.5 %convolution_bitcast_fusion = f32[288,256]{1,0:T(8,128)S(1)} fusion(f32[128,4]{0,1:T(4,128)S(1)} %slice.40, f32[128,4]{0,1:T(4,128)S(1)} %copy.20, s32[128,4]{0,1:T(4,128)S(1)} %copy.18, s32[288]{0:T(512)S(1)} %fusion.10, s32[128,4]{0,1:T(4,128)S(1)} %copy.22, s32[256]{0:T(256)S(1)} %fusion.11), kind=kOutput, calls=%fused_computation | convolution fusion | flops 458424320 | bytes 305280 | tf_op jit(solution)/shard_map/dkr,dkc->rc/dot_general | solution.py:422
  40.7 0.4 exponential_select_fusion.1
  41.2 0.0 copy-start.8
  41.2 0.0 copy-start.9
  41.2 0.0 copy-start.10
  41.2 0.0 copy-start.11
  41.2 0.5 exponential_select_fusion
  41.7 0.0 copy-start.3
  41.7 0.0 copy-start.4
  41.7 0.0 copy-start.5
  41.7 0.0 copy-start.6
  41.7 0.0 copy-start.7
  41.8 0.0 copy-start
  41.8 0.0 copy-start.1
  41.8 0.0 copy-start.2
  41.8 0.1 broadcast_multiply_fusion.refs_12_
  42.0 0.1 copy-done.8
  42.1 0.0 copy-done.9
  42.1 0.0 copy-done.10
  42.2 0.0 copy-done.11
  42.2 0.5 copy-done.3
  42.7 0.0 copy-done.4
  42.8 0.1 copy-done.5
  42.8 0.0 copy-done.6
  42.9 0.0 copy-done.7
  42.9 0.1 copy-done
  43.0 0.1 copy-done.1
  43.2 0.1 copy-done.2
  43.3 27.2 %shard_map.96 = (f32[3,256,128]{2,1,0:T(8,128)S(1)}, f32[1,128]{1,0:T(1,128)S(1)}) custom-call(f32[3,256,128]{2,1,0:T(8,128)S(1)} %copy-done, f32[3,256,128]{2,1,0:T(8,128)S(1)} %copy-done.1, f32[3,256,128]{2,1,0:T(8,128)S(1)} %copy-done.2, f32[3,256,128]{2,1,0:T(8,128)S(1)} %copy-done.3, f32[12,16,128]{2,1,0:T(8,128)S(1)} %copy-done.7, ...), custom_call_target="tpu_custom_call" | custom-call | flops 106168320 | bytes 6193152 | tf_op jit(solution)/shard_map/pallas_call | solution.py:290
  70.5 0.5 slice_bitcast_fusion.2
  71.0 0.7 %copy.29 = f32[3,256,128]{2,1,0:T(8,128)} copy(f32[3,256,128]{2,1,0:T(8,128)S(1)} %get-tuple-element.31) | data formatting | bytes 786432
  (8 shorter events, 0.1 us)
Async XLA Ops:
  0.7 0.7 copy-start.13
  0.7 0.7 copy-start.16
  1.4 0.7 copy-start.14
  1.4 0.7 copy-start.15
  37.9 0.8 %copy-start.12 = (f32[128,128]{1,0:T(8,128)S(1)}, f32[128,128]{1,0:T(8,128)}, u32[]{:S(2)}) copy-start(f32[128,128]{1,0:T(8,128)} %get-tuple-element.21) | copy-start | bytes 196612
  41.2 0.9 %copy-start.8 = (f32[12,16,16]{2,1,0:T(8,128)S(1)}, f32[12,16,16]{2,1,0:T(8,128)}, u32[]{:S(2)}) copy-start(f32[12,16,16]{2,1,0:T(8,128)} %get-tuple-element.17.refs_8_) | copy-start | bytes 36868
  41.2 0.9 %copy-start.9 = (f32[12,16,16]{2,1,0:T(8,128)S(1)}, f32[12,16,16]{2,1,0:T(8,128)}, u32[]{:S(2)}) copy-start(f32[12,16,16]{2,1,0:T(8,128)} %get-tuple-element.18.refs_9_) | copy-start | bytes 36868
  41.2 1.0 %copy-start.10 = (f32[12,16,16]{2,1,0:T(8,128)S(1)}, f32[12,16,16]{2,1,0:T(8,128)}, u32[]{:S(2)}) copy-start(f32[12,16,16]{2,1,0:T(8,128)} %get-tuple-element.19.refs_10_) | copy-start | bytes 36868
  41.2 1.0 %copy-start.11 = (f32[12,16,16]{2,1,0:T(8,128)S(1)}, f32[12,16,16]{2,1,0:T(8,128)}, u32[]{:S(2)}) copy-start(f32[12,16,16]{2,1,0:T(8,128)} %get-tuple-element.20.refs_11_) | copy-start | bytes 36868
  41.7 1.0 %copy-start.3 = (f32[3,256,128]{2,1,0:T(8,128)S(1)}, f32[3,256,128]{2,1,0:T(8,128)}, u32[]{:S(2)}) copy-start(f32[3,256,128]{2,1,0:T(8,128)} %refs_3_.3) | copy-start | bytes 1179652
  41.7 1.1 %copy-start.4 = (f32[12,16,256]{2,1,0:T(8,128)S(1)}, f32[12,16,256]{2,1,0:T(8,128)}, u32[]{:S(2)}) copy-start(f32[12,16,256]{2,1,0:T(8,128)} %get-tuple-element.15.refs_6_) | copy-start | bytes 589828
  41.7 1.1 %copy-start.5 = (f32[12,16,256]{2,1,0:T(8,128)S(1)}, f32[12,16,256]{2,1,0:T(8,128)}, u32[]{:S(2)}) copy-start(f32[12,16,256]{2,1,0:T(8,128)} %get-tuple-element.16.refs_7_) | copy-start | bytes 589828
  41.7 1.1 %copy-start.6 = (f32[12,16,128]{2,1,0:T(8,128)S(1)}, f32[12,16,128]{2,1,0:T(8,128)}, u32[]{:S(2)}) copy-start(f32[12,16,128]{2,1,0:T(8,128)} %get-tuple-element.14.refs_5_) | copy-start | bytes 294916
  41.7 1.2 %copy-start.7 = (f32[12,16,128]{2,1,0:T(8,128)S(1)}, f32[12,16,128]{2,1,0:T(8,128)}, u32[]{:S(2)}) copy-start(f32[12,16,128]{2,1,0:T(8,128)} %get-tuple-element.13.refs_4_) | copy-start | bytes 294916
  41.8 1.3 %copy-start = (f32[3,256,128]{2,1,0:T(8,128)S(1)}, f32[3,256,128]{2,1,0:T(8,128)}, u32[]{:S(2)}) copy-start(f32[3,256,128]{2,1,0:T(8,128)} %refs_0_.3) | copy-start | bytes 1179652
  41.8 1.4 %copy-start.1 = (f32[3,256,128]{2,1,0:T(8,128)S(1)}, f32[3,256,128]{2,1,0:T(8,128)}, u32[]{:S(2)}) copy-start(f32[3,256,128]{2,1,0:T(8,128)} %refs_1_.3) | copy-start | bytes 1179652
  41.8 1.5 %copy-start.2 = (f32[3,256,128]{2,1,0:T(8,128)S(1)}, f32[3,256,128]{2,1,0:T(8,128)}, u32[]{:S(2)}) copy-start(f32[3,256,128]{2,1,0:T(8,128)} %refs_2_.3) | copy-start | bytes 1179652

commit v9 on v7

--- a/solution.py
+++ b/solution.py
@@ -179,7 +179,7 @@
     (
         high_ref, low_ref, band_ref, drag_ref, row_ref, col_ref, thrust_ref, gain_ref,
         lam_out, grad_out,
-        ext_ref, states, lams, sens_all, sending, slots, send_sem, recv_sem, local_sem,
+        ext_ref, states, lams, sens_all, sending, slots, roots, send_sem, recv_sem, local_sem,
     ) = refs[n_block:]
     n_dev = n_gx * n_gy
     me = lax.axis_index("gx") * n_gy + lax.axis_index("gy")
@@ -220,6 +220,8 @@
     def forward(n, carry):
         for level in range(levels):
             center = states[n, level]
+            root = jnp.sqrt(center * center + 1.0)
+            roots[n, level] = root
             upwind = west(center)
             advect = ext_ref[levels + level]
             diffuse = ext_ref[2 * levels + level]
@@ -228,11 +230,14 @@
                 + advect * (upwind - center)
                 + diffuse * (east(center) + upwind + north(center) + south(center) - 4.0 * center)
                 + VERTICAL_MIX * vertical(lambda l: states[n, l], level, center)
-                - drag_ref[level] * (center * jnp.sqrt(center * center + 1.0))
+                - drag_ref[level] * (center * root)
             )
         return carry
 
     lax.fori_loop(0, steps - 1, forward, 0)
+    for level in range(levels):
+        last = states[steps - 1, level]
+        roots[steps - 1, level] = jnp.sqrt(last * last + 1.0)
     for level in range(levels):
         lams[0, level] = ext_ref[3 * levels + level]
         sens_all[level] = jnp.zeros(sens_all.shape[1:], jnp.float32)
@@ -243,17 +248,17 @@
         for level in range(levels):
             adjoint = lams[now, level]
             state = states[n, level]
-            sens_all[level] = sens_all[level] - adjoint * (state * jnp.sqrt(state * state + 1.0))
+            root = roots[n, level]
+            sens_all[level] = sens_all[level] - adjoint * (state * root)
             flux_adv = ext_ref[levels + level] * adjoint
             flux_dif = ext_ref[2 * levels + level] * adjoint
-            square_one = state * state + 1.0
-            slope = (square_one + state * state) / jnp.sqrt(square_one)
+            square = state * state
+            slope = ((square + 1.0) + square) / root
             lams[1 - now, level] = (
                 adjoint
                 - flux_adv
                 - 4.0 * flux_dif
-                + east(flux_adv)
-                + (east(flux_dif) + west(flux_dif) + north(flux_dif) + south(flux_dif))
+                + (east(flux_adv + flux_dif) + west(flux_dif) + north(flux_dif) + south(flux_dif))
                 + VERTICAL_MIX * vertical(lambda l: lams[now, l], level, adjoint)
                 - drag_ref[level] * slope * adjoint
             )
@@ -307,6 +312,7 @@
             pltpu.VMEM((levels, size_r, size_c), jnp.float32),
             pltpu.VMEM((width, width), jnp.float32),
             pltpu.VMEM((n_dev, width), jnp.float32),
+            pltpu.VMEM((STEPS, levels, size_r, size_c), jnp.float32),
             pltpu.SemaphoreType.DMA,
             pltpu.SemaphoreType.DMA,
             pltpu.SemaphoreType.DMA,

time: 71.5 us -> 68.9 us (0.964)
  Pallas kernels: 62.1 us -> 59.5 us
    pallas_call x1, Pallas kernels: 27.8 us -> 25.1 us  [stencil(): pl.pallas_call(functools.partial(stencil_kernel, n_gx, n_gy, levels, STEP...]
where the time goes in v9:
time: 68.9 us; the launch traced here: 68.6 us
  Pallas kernels  59.5 us (86%)
  other arithmetic  3.68 us (5%)
  local copies, waits for them, and re-layouts  3.16 us (5%)
  matrix products  1.49 us (2%)
  between operations  0.81 us (1%)
    pallas_call x1, Pallas kernels, open_exchange(): pl.pallas_call(functools.partial(open_kernel, n_gx, n_gy, m, len(blocks))...  34.4 us
    pallas_call x1, Pallas kernels, stencil(): pl.pallas_call(functools.partial(stencil_kernel, n_gx, n_gy, levels, STEP...  25.1 us
    concatenate x1, other arithmetic, column_band(): jnp.concatenate([edge(col_high, c_hh, c_lh), fill, edge(col_low, c_hl, c_...  1.58 us
    dot_general x1, matrix products, shards(): jnp.einsum('dkr,dkc->rc', thrusts[..., None] * prof_r, prof_c, precision=...  1.49 us

profile of v9, /device:TPU:1, one launch (start us, length us, event | category | flops | bytes accessed | tf_op | source)
XLA Modules:
  0.0 68.6 jit_solution(10225415545409543134)
XLA Ops:
  0.6 0.8 %convert_bitcast_fusion = (f32[4]{0:T(128)S(1)}, f32[4]{0:T(128)S(1)}, f32[4]{0:T(128)S(1)}) fusion(s32[4,2]{0,1:T(2,128)} %param.13, s32[4,1]{0,1:T(1,128)} %param.12), kind=kLoop, calls=%fused_computation.43 | loop fusion | flops 12 | bytes 96 | tf_op jit(solution)/shard_map/convert_element_type | solution.py:412
  1.4 1.3 %concatenate.12 = f32[128]{0:T(128)} concatenate(f32[4]{0:T(128)S(1)} %get-tuple-element.28, f32[4]{0:T(128)S(1)} %get-tuple-element.27, f32[4]{0:T(128)S(1)} %get-tuple-element.26, f32[4]{0:T(128)} %param.14, f32[4]{0:T(128)} %param.15, f32[108]{0:T(128)S(1)} %broadcast_in_dim.18), dimensions={0} | concatenate | bytes 1024 | tf_op jit(solution)/shard_map/concatenate | solution.py:417
  2.7 34.4 %shard_map.95 = (f32[128,128]{1,0:T(8,128)}, f32[12,16,128]{2,1,0:T(8,128)}, f32[12,16,128]{2,1,0:T(8,128)}, f32[12,16,256]{2,1,0:T(8,128)}, f32[12,16,256]{2,1,...) custom-call(f32[1,128]{1,0:T(1,128)} %bitcast.19, ...), custom_call_target="tpu_custom_call" | custom-call | tf_op jit(solution)/shard_map/pallas_call | solution.py:141
  37.0 0.0 copy-start.6
  37.0 0.1 pad.4.clone
  37.1 1.6 %maximum_maximum_fusion.refs_6_ = f32[12,128,384]{2,1,0:T(8,128)S(1)} fusion(f32[12,16,96]{2,1,0:T(8,128)S(1)} %broadcast.88, f32[12,16,16]{2,1,0:T(8,128)} %get-tuple-element.20, f32[12,16,16]{2,1,0:T(8,128)} %get-tuple-element.19, f32[12,16,256]{2,1,0:T(8,128)} %get-tuple-element.18, f32[12,16,16]{2,1,0:T(8,128)} %get-tuple-element.17, ...), kind=kLoop, calls=%fused_computation | loop fusion | flops 4718592 | bytes 2875904 | tf_op jit(solution)/shard_map/concatenate | solution.py:174
  38.7 0.0 copy-done.6
  38.7 0.1 copy.16
  38.8 0.1 multiply_multiply_fusion
  38.9 0.1 copy.20
  39.0 0.1 fusion.7
  39.1 0.1 fusion.5
  39.2 0.1 copy.18
  39.2 0.1 copy.22
  39.3 1.5 %convolution_bitcast_fusion = f32[288,256]{1,0:T(8,128)S(1)} fusion(f32[128,4]{0,1:T(4,128)S(1)} %slice.40, f32[128,4]{0,1:T(4,128)S(1)} %copy.20, s32[128,4]{0,1:T(4,128)S(1)} %copy.18, s32[288]{0:T(512)S(1)} %fusion.10, s32[128,4]{0,1:T(4,128)S(1)} %copy.22, s32[256]{0:T(256)S(1)} %fusion.11), kind=kOutput, calls=%fused_computation.1 | convolution fusion | flops 458424320 | bytes 305280 | tf_op jit(solution)/shard_map/dkr,dkc->rc/dot_general | solution.py:435
  40.8 0.0 copy-start
  40.8 0.0 copy-start.1
  40.8 0.0 copy-start.2
  40.9 0.0 copy-start.3
  40.9 0.0 copy-start.4
  40.9 0.0 copy-start.5
  40.9 0.1 broadcast_multiply_fusion.refs_7_
  41.1 0.5 exponential_select_fusion
  41.6 0.4 exponential_select_fusion.1
  42.0 0.1 broadcast_in_dim.43.refs_11_
  42.1 0.0 copy-done
  42.1 0.0 copy-done.1
  42.1 0.0 copy-done.2
  42.1 0.1 copy-done.3
  42.2 0.0 copy-done.4
  42.2 0.0 copy-done.5
  42.2 25.1 %shard_map.96 = (f32[3,256,128]{2,1,0:T(8,128)S(1)}, f32[1,128]{1,0:T(1,128)S(1)}) custom-call(f32[3,256,128]{2,1,0:T(8,128)S(1)} %copy-done, f32[3,256,128]{2,1,0:T(8,128)S(1)} %copy-done.1, f32[3,256,128]{2,1,0:T(8,128)S(1)} %copy-done.2, f32[3,256,128]{2,1,0:T(8,128)S(1)} %copy-done.3, f32[12,16,128]{2,1,0:T(8,128)S(1)} %copy-done.5, ...), custom_call_target="tpu_custom_call" | custom-call | flops 106168320 | bytes 6193152 | tf_op jit(solution)/shard_map/pallas_call | solution.py:303
  67.4 0.5 slice_bitcast_fusion.2
  67.9 0.7 %copy.29 = f32[3,256,128]{2,1,0:T(8,128)} copy(f32[3,256,128]{2,1,0:T(8,128)S(1)} %get-tuple-element.31) | data formatting | bytes 786432
  (9 shorter events, 0.1 us)
Async XLA Ops:
  37.0 1.7 %copy-start.6 = (f32[128,128]{1,0:T(8,128)S(1)}, f32[128,128]{1,0:T(8,128)}, u32[]{:S(2)}) copy-start(f32[128,128]{1,0:T(8,128)} %get-tuple-element.21) | copy-start | bytes 196612
  40.8 1.3 %copy-start = (f32[3,256,128]{2,1,0:T(8,128)S(1)}, f32[3,256,128]{2,1,0:T(8,128)}, u32[]{:S(2)}) copy-start(f32[3,256,128]{2,1,0:T(8,128)} %refs_0_.3) | copy-start | bytes 1179652
  40.8 1.3 %copy-start.1 = (f32[3,256,128]{2,1,0:T(8,128)S(1)}, f32[3,256,128]{2,1,0:T(8,128)}, u32[]{:S(2)}) copy-start(f32[3,256,128]{2,1,0:T(8,128)} %refs_1_.3) | copy-start | bytes 1179652
  40.8 1.3 %copy-start.2 = (f32[3,256,128]{2,1,0:T(8,128)S(1)}, f32[3,256,128]{2,1,0:T(8,128)}, u32[]{:S(2)}) copy-start(f32[3,256,128]{2,1,0:T(8,128)} %refs_2_.3) | copy-start | bytes 1179652
  40.9 1.3 %copy-start.3 = (f32[3,256,128]{2,1,0:T(8,128)S(1)}, f32[3,256,128]{2,1,0:T(8,128)}, u32[]{:S(2)}) copy-start(f32[3,256,128]{2,1,0:T(8,128)} %refs_3_.3) | copy-start | bytes 1179652
  40.9 1.3 %copy-start.4 = (f32[12,16,128]{2,1,0:T(8,128)S(1)}, f32[12,16,128]{2,1,0:T(8,128)}, u32[]{:S(2)}) copy-start(f32[12,16,128]{2,1,0:T(8,128)} %get-tuple-element.14.refs_5_) | copy-start | bytes 294916
  40.9 1.3 %copy-start.5 = (f32[12,16,128]{2,1,0:T(8,128)S(1)}, f32[12,16,128]{2,1,0:T(8,128)}, u32[]{:S(2)}) copy-start(f32[12,16,128]{2,1,0:T(8,128)} %get-tuple-element.13.refs_4_) | copy-start | bytes 294916

commit v10 on v9

--- a/solution.py
+++ b/solution.py
@@ -234,7 +234,7 @@
             )
         return carry
 
-    lax.fori_loop(0, steps - 1, forward, 0)
+    lax.fori_loop(0, steps - 1, forward, 0, unroll=True)
     for level in range(levels):
         last = states[steps - 1, level]
         roots[steps - 1, level] = jnp.sqrt(last * last + 1.0)
@@ -264,7 +264,7 @@
             )
         return carry
 
-    lax.fori_loop(0, steps, backward, 0)
+    lax.fori_loop(0, steps, backward, 0, unroll=True)
     weighted = gain_ref[0] * sens_all[0, :rows, :cols]
     for level in range(1, levels):
         weighted = weighted + gain_ref[level] * sens_all[level, :rows, :cols]

time: 68.9 us -> 66.7 us (0.968)
  Pallas kernels: 59.5 us -> 57.3 us
    pallas_call x1, Pallas kernels: 25.1 us -> 23 us  [stencil(): pl.pallas_call(functools.partial(stencil_kernel, n_gx, n_gy, levels, STEP...]
where the time goes in v10:
time: 66.7 us; the launch traced here: 66.5 us
  Pallas kernels  57.3 us (86%)
  other arithmetic  3.68 us (6%)
  local copies, waits for them, and re-layouts  3.16 us (5%)
  matrix products  1.49 us (2%)
  between operations  0.81 us (1%)
    pallas_call x1, Pallas kernels, open_exchange(): pl.pallas_call(functools.partial(open_kernel, n_gx, n_gy, m, len(blocks))...  34.4 us
    pallas_call x1, Pallas kernels, stencil(): pl.pallas_call(functools.partial(stencil_kernel, n_gx, n_gy, levels, STEP...  23 us
    concatenate x1, other arithmetic, column_band(): jnp.concatenate([edge(col_high, c_hh, c_lh), fill, edge(col_low, c_hl, c_...  1.58 us
    dot_general x1, matrix products, shards(): jnp.einsum('dkr,dkc->rc', thrusts[..., None] * prof_r, prof_c, precision=...  1.49 us

profile of v10, /device:TPU:1, one launch (start us, length us, event | category | flops | bytes accessed | tf_op | source)
XLA Modules:
  0.0 66.5 jit_solution(12917509989643559412)
XLA Ops:
  0.6 0.8 %convert_bitcast_fusion = (f32[4]{0:T(128)S(1)}, f32[4]{0:T(128)S(1)}, f32[4]{0:T(128)S(1)}) fusion(s32[4,2]{0,1:T(2,128)} %param.13, s32[4,1]{0,1:T(1,128)} %param.12), kind=kLoop, calls=%fused_computation.43 | loop fusion | flops 12 | bytes 96 | tf_op jit(solution)/shard_map/convert_element_type | solution.py:412
  1.4 1.3 %concatenate.12 = f32[128]{0:T(128)} concatenate(f32[4]{0:T(128)S(1)} %get-tuple-element.28, f32[4]{0:T(128)S(1)} %get-tuple-element.27, f32[4]{0:T(128)S(1)} %get-tuple-element.26, f32[4]{0:T(128)} %param.14, f32[4]{0:T(128)} %param.15, f32[108]{0:T(128)S(1)} %broadcast_in_dim.18), dimensions={0} | concatenate | bytes 1024 | tf_op jit(solution)/shard_map/concatenate | solution.py:417
  2.7 34.4 %shard_map.95 = (f32[128,128]{1,0:T(8,128)}, f32[12,16,128]{2,1,0:T(8,128)}, f32[12,16,128]{2,1,0:T(8,128)}, f32[12,16,256]{2,1,0:T(8,128)}, f32[12,16,256]{2,1,...) custom-call(f32[1,128]{1,0:T(1,128)} %bitcast.19, ...), custom_call_target="tpu_custom_call" | custom-call | tf_op jit(solution)/shard_map/pallas_call | solution.py:141
  37.0 0.0 copy-start.6
  37.0 0.1 pad.4.clone
  37.1 1.6 %maximum_maximum_fusion.refs_6_ = f32[12,128,384]{2,1,0:T(8,128)S(1)} fusion(f32[12,16,96]{2,1,0:T(8,128)S(1)} %broadcast.88, f32[12,16,16]{2,1,0:T(8,128)} %get-tuple-element.20, f32[12,16,16]{2,1,0:T(8,128)} %get-tuple-element.19, f32[12,16,256]{2,1,0:T(8,128)} %get-tuple-element.18, f32[12,16,16]{2,1,0:T(8,128)} %get-tuple-element.17, ...), kind=kLoop, calls=%fused_computation | loop fusion | flops 4718592 | bytes 2875904 | tf_op jit(solution)/shard_map/concatenate | solution.py:174
  38.7 0.0 copy-done.6
  38.7 0.1 copy.16
  38.8 0.1 multiply_multiply_fusion
  38.9 0.1 copy.20
  39.0 0.1 fusion.7
  39.1 0.1 fusion.5
  39.2 0.1 copy.18
  39.2 0.1 copy.22
  39.3 1.5 %convolution_bitcast_fusion = f32[288,256]{1,0:T(8,128)S(1)} fusion(f32[128,4]{0,1:T(4,128)S(1)} %slice.40, f32[128,4]{0,1:T(4,128)S(1)} %copy.20, s32[128,4]{0,1:T(4,128)S(1)} %copy.18, s32[288]{0:T(512)S(1)} %fusion.10, s32[128,4]{0,1:T(4,128)S(1)} %copy.22, s32[256]{0:T(256)S(1)} %fusion.11), kind=kOutput, calls=%fused_computation.1 | convolution fusion | flops 458424320 | bytes 305280 | tf_op jit(solution)/shard_map/dkr,dkc->rc/dot_general | solution.py:435
  40.8 0.0 copy-start
  40.8 0.0 copy-start.1
  40.8 0.0 copy-start.2
  40.9 0.0 copy-start.3
  40.9 0.0 copy-start.4
  40.9 0.0 copy-start.5
  40.9 0.1 broadcast_multiply_fusion.refs_7_
  41.1 0.5 exponential_select_fusion
  41.6 0.4 exponential_select_fusion.1
  42.0 0.1 broadcast_in_dim.43.refs_11_
  42.1 0.0 copy-done
  42.1 0.0 copy-done.1
  42.1 0.0 copy-done.2
  42.1 0.1 copy-done.3
  42.2 0.0 copy-done.4
  42.2 0.0 copy-done.5
  42.2 23.0 %shard_map.96 = (f32[3,256,128]{2,1,0:T(8,128)S(1)}, f32[1,128]{1,0:T(1,128)S(1)}) custom-call(f32[3,256,128]{2,1,0:T(8,128)S(1)} %copy-done, f32[3,256,128]{2,1,0:T(8,128)S(1)} %copy-done.1, f32[3,256,128]{2,1,0:T(8,128)S(1)} %copy-done.2, f32[3,256,128]{2,1,0:T(8,128)S(1)} %copy-done.3, f32[12,16,128]{2,1,0:T(8,128)S(1)} %copy-done.5, ...), custom_call_target="tpu_custom_call" | custom-call | flops 106168320 | bytes 6193152 | tf_op jit(solution)/shard_map/pallas_call | solution.py:303
  65.2 0.5 slice_bitcast_fusion.2
  65.7 0.7 %copy.29 = f32[3,256,128]{2,1,0:T(8,128)} copy(f32[3,256,128]{2,1,0:T(8,128)S(1)} %get-tuple-element.31) | data formatting | bytes 786432
  (9 shorter events, 0.1 us)
Async XLA Ops:
  37.0 1.7 %copy-start.6 = (f32[128,128]{1,0:T(8,128)S(1)}, f32[128,128]{1,0:T(8,128)}, u32[]{:S(2)}) copy-start(f32[128,128]{1,0:T(8,128)} %get-tuple-element.21) | copy-start | bytes 196612
  40.8 1.3 %copy-start = (f32[3,256,128]{2,1,0:T(8,128)S(1)}, f32[3,256,128]{2,1,0:T(8,128)}, u32[]{:S(2)}) copy-start(f32[3,256,128]{2,1,0:T(8,128)} %refs_0_.3) | copy-start | bytes 1179652
  40.8 1.3 %copy-start.1 = (f32[3,256,128]{2,1,0:T(8,128)S(1)}, f32[3,256,128]{2,1,0:T(8,128)}, u32[]{:S(2)}) copy-start(f32[3,256,128]{2,1,0:T(8,128)} %refs_1_.3) | copy-start | bytes 1179652
  40.8 1.3 %copy-start.2 = (f32[3,256,128]{2,1,0:T(8,128)S(1)}, f32[3,256,128]{2,1,0:T(8,128)}, u32[]{:S(2)}) copy-start(f32[3,256,128]{2,1,0:T(8,128)} %refs_2_.3) | copy-start | bytes 1179652
  40.9 1.3 %copy-start.3 = (f32[3,256,128]{2,1,0:T(8,128)S(1)}, f32[3,256,128]{2,1,0:T(8,128)}, u32[]{:S(2)}) copy-start(f32[3,256,128]{2,1,0:T(8,128)} %refs_3_.3) | copy-start | bytes 1179652
  40.9 1.3 %copy-start.4 = (f32[12,16,128]{2,1,0:T(8,128)S(1)}, f32[12,16,128]{2,1,0:T(8,128)}, u32[]{:S(2)}) copy-start(f32[12,16,128]{2,1,0:T(8,128)} %get-tuple-element.14.refs_5_) | copy-start | bytes 294916
  40.9 1.3 %copy-start.5 = (f32[12,16,128]{2,1,0:T(8,128)S(1)}, f32[12,16,128]{2,1,0:T(8,128)}, u32[]{:S(2)}) copy-start(f32[12,16,128]{2,1,0:T(8,128)} %get-tuple-element.13.refs_4_) | copy-start | bytes 294916

commit v11 on v10

--- a/solution.py
+++ b/solution.py
@@ -177,9 +177,10 @@
 def stencil_kernel(n_gx, n_gy, levels, steps, n_block, *refs):
     blocks = refs[:n_block]
     (
-        high_ref, low_ref, band_ref, drag_ref, row_ref, col_ref, thrust_ref, gain_ref,
+        high_ref, low_ref, band_ref, plane_ref, row_ref, col_ref, thrust_ref, gain_ref,
         lam_out, grad_out,
-        ext_ref, states, lams, sens_all, sending, slots, roots, send_sem, recv_sem, local_sem,
+        ext_ref, states, lams, sens_all, sending, slots, roots, drag_ref,
+        send_sem, recv_sem, local_sem,
     ) = refs[n_block:]
     n_dev = n_gx * n_gy
     me = lax.axis_index("gx") * n_gy + lax.axis_index("gy")
@@ -187,6 +188,8 @@
     size_r, size_c = ext_ref.shape[1:]
     rows, cols = blocks[0].shape[1:]
     m = high_ref.shape[1]
+    for level in range(levels):
+        drag_ref[level] = gain_ref[level][:, :1] * plane_ref[...]
     for depth in range(ext_ref.shape[0]):
         ext_ref[depth, :rows, :cols] = blocks[depth // levels][depth % levels]
         ext_ref[depth, rows : rows + m, :cols] = high_ref[depth]
@@ -291,7 +294,7 @@
 
 
 def stencil(blocks, landed, band, drag, levels, row_prof, col_prof, thrust_rows, gain_rows):
-    size_r, size_c = drag.shape[1:]
+    size_r, size_c = drag.shape
     depth = levels * len(blocks)
     vmem = pl.BlockSpec(memory_space=pltpu.VMEM)
     plane = jax.ShapeDtypeStruct(blocks[0].shape, jnp.float32)
@@ -313,6 +316,7 @@
             pltpu.VMEM((width, width), jnp.float32),
             pltpu.VMEM((n_dev, width), jnp.float32),
             pltpu.VMEM((STEPS, levels, size_r, size_c), jnp.float32),
+            pltpu.VMEM((levels, size_r, size_c), jnp.float32),
             pltpu.SemaphoreType.DMA,
             pltpu.SemaphoreType.DMA,
             pltpu.SemaphoreType.DMA,
@@ -433,7 +437,6 @@
     prof_c = profiles(gy * cols, col_start, widths, n_gy * cols, size_c, inner_c)
     gain = level_gain()
     plane = jnp.einsum("dkr,dkc->rc", thrusts[..., None] * prof_r, prof_c, precision=HIGHEST)
-    drag = gain[:, None, None] * plane[None]
     band = column_band(opened[1:], m, size_r, size_c, cols)
     spare = ((0, 0), (0, 0), (0, -(-n_gx * n_gy // 128) * 128 - n_gx * n_gy))
     row_prof = jnp.pad(jnp.transpose(prof_r[..., :rows], (1, 2, 0)), spare)
@@ -441,7 +444,7 @@
     thrust_rows = jnp.pad(jnp.transpose(thrusts)[:, None, :], spare)
     gain_rows = jnp.broadcast_to(gain[:, None, None], (levels, 1, cols))
     adjoint, grad = stencil(
-        blocks, opened[1:], band, drag, levels, row_prof, col_prof, thrust_rows, gain_rows
+        blocks, opened[1:], band, plane, levels, row_prof, col_prof, thrust_rows, gain_rows
     )
     return adjoint, grad[0, :per]
 

time: 66.7 us -> 67.5 us (1.012)
  Pallas kernels: 57.3 us -> 58.1 us
    pallas_call x1, Pallas kernels: 23 us -> 23.8 us  [stencil(): pl.pallas_call(functools.partial(stencil_kernel, n_gx, n_gy, levels, STEP...]
where the time goes in v11:
time: 67.5 us; the launch traced here: 67.3 us
  Pallas kernels  58.1 us (86%)
  other arithmetic  3.55 us (5%)
  local copies, waits for them, and re-layouts  3.31 us (5%)
  matrix products  1.49 us (2%)
  between operations  0.8 us (1%)
    pallas_call x1, Pallas kernels, open_exchange(): pl.pallas_call(functools.partial(open_kernel, n_gx, n_gy, m, len(blocks))...  34.4 us
    pallas_call x1, Pallas kernels, stencil(): pl.pallas_call(functools.partial(stencil_kernel, n_gx, n_gy, levels, STEP...  23.8 us
    concatenate x1, other arithmetic, column_band(): jnp.concatenate([edge(col_high, c_hh, c_lh), fill, edge(col_low, c_hl, c_...  1.58 us
    dot_general x1, matrix products, shards(): jnp.einsum('dkr,dkc->rc', thrusts[..., None] * prof_r, prof_c, precision=...  1.49 us

profile of v11, /device:TPU:1, one launch (start us, length us, event | category | flops | bytes accessed | tf_op | source)
XLA Modules:
  0.0 67.3 jit_solution(13346440489027477643)
XLA Ops:
  0.6 0.8 %convert_bitcast_fusion = (f32[4]{0:T(128)S(1)}, f32[4]{0:T(128)S(1)}, f32[4]{0:T(128)S(1)}) fusion(s32[4,2]{0,1:T(2,128)} %param.13, s32[4,1]{0,1:T(1,128)} %param.12), kind=kLoop, calls=%fused_computation.42 | loop fusion | flops 12 | bytes 96 | tf_op jit(solution)/shard_map/convert_element_type | solution.py:416
  1.4 1.3 %concatenate.12 = f32[128]{0:T(128)} concatenate(f32[4]{0:T(128)S(1)} %get-tuple-element.28, f32[4]{0:T(128)S(1)} %get-tuple-element.27, f32[4]{0:T(128)S(1)} %get-tuple-element.26, f32[4]{0:T(128)} %param.14, f32[4]{0:T(128)} %param.15, f32[108]{0:T(128)S(1)} %broadcast_in_dim.18), dimensions={0} | concatenate | bytes 1024 | tf_op jit(solution)/shard_map/concatenate | solution.py:421
  2.7 34.4 %shard_map.95 = (f32[128,128]{1,0:T(8,128)}, f32[12,16,128]{2,1,0:T(8,128)}, f32[12,16,128]{2,1,0:T(8,128)}, f32[12,16,256]{2,1,0:T(8,128)}, f32[12,16,256]{2,1,...) custom-call(f32[1,128]{1,0:T(1,128)} %bitcast.19, ...), custom_call_target="tpu_custom_call" | custom-call | tf_op jit(solution)/shard_map/pallas_call | solution.py:141
  37.0 0.0 copy-start.6
  37.0 0.1 pad.4.clone
  37.1 1.6 %maximum_maximum_fusion.refs_6_ = f32[12,128,384]{2,1,0:T(8,128)S(1)} fusion(f32[12,16,96]{2,1,0:T(8,128)S(1)} %broadcast.93, f32[12,16,16]{2,1,0:T(8,128)} %get-tuple-element.20, f32[12,16,16]{2,1,0:T(8,128)} %get-tuple-element.19, f32[12,16,256]{2,1,0:T(8,128)} %get-tuple-element.18, f32[12,16,16]{2,1,0:T(8,128)} %get-tuple-element.17, ...), kind=kLoop, calls=%fused_computation | loop fusion | flops 4718592 | bytes 2875904 | tf_op jit(solution)/shard_map/concatenate | solution.py:174
  38.7 0.0 copy-done.6
  38.7 0.1 copy.16
  38.8 0.1 multiply_multiply_fusion
  38.9 0.1 copy.20
  39.0 0.1 fusion.7
  39.1 0.1 fusion.5
  39.2 0.1 copy.18
  39.2 0.1 copy.22
  39.3 1.5 %convolution_bitcast_fusion.refs_7_ = f32[288,256]{1,0:T(8,128)S(1)} fusion(f32[128,4]{0,1:T(4,128)S(1)} %slice.40, f32[128,4]{0,1:T(4,128)S(1)} %copy.20, s32[128,4]{0,1:T(4,128)S(1)} %copy.18, s32[288]{0:T(512)S(1)} %fusion.10, s32[128,4]{0,1:T(4,128)S(1)} %copy.22, s32[256]{0:T(256)S(1)} %fusion.11), kind=kOutput, calls=%fused_computation.1 | convolution fusion | flops 458424320 | bytes 305280 | tf_op jit(solution)/shard_map/dkr,dkc->rc/dot_general | solution.py:439
  40.8 0.0 copy-start
  40.8 0.0 copy-start.1
  40.8 0.0 copy-start.2
  40.9 0.0 copy-start.3
  40.9 0.0 copy-start.4
  40.9 0.0 copy-start.5
  40.9 0.5 exponential_select_fusion
  41.4 0.4 exponential_select_fusion.1
  41.9 0.1 broadcast_in_dim.41.refs_11_
  42.0 0.0 copy-done
  42.0 0.0 copy-done.1
  42.0 0.1 copy-done.2
  42.1 0.1 copy-done.3
  42.2 0.0 copy-done.4
  42.2 0.0 copy-done.5
  42.2 23.8 %shard_map.96 = (f32[3,256,128]{2,1,0:T(8,128)S(1)}, f32[1,128]{1,0:T(1,128)S(1)}) custom-call(f32[3,256,128]{2,1,0:T(8,128)S(1)} %copy-done, f32[3,256,128]{2,1,0:T(8,128)S(1)} %copy-done.1, f32[3,256,128]{2,1,0:T(8,128)S(1)} %copy-done.2, f32[3,256,128]{2,1,0:T(8,128)S(1)} %copy-done.3, f32[12,16,128]{2,1,0:T(8,128)S(1)} %copy-done.5, ...), custom_call_target="tpu_custom_call" | custom-call | flops 106168320 | bytes 6193152 | tf_op jit(solution)/shard_map/pallas_call | solution.py:306
  66.0 0.5 slice_bitcast_fusion.2
  66.5 0.7 %copy.29 = f32[3,256,128]{2,1,0:T(8,128)} copy(f32[3,256,128]{2,1,0:T(8,128)S(1)} %get-tuple-element.31) | data formatting | bytes 786432
  (9 shorter events, 0.1 us)
Async XLA Ops:
  37.0 1.7 %copy-start.6 = (f32[128,128]{1,0:T(8,128)S(1)}, f32[128,128]{1,0:T(8,128)}, u32[]{:S(2)}) copy-start(f32[128,128]{1,0:T(8,128)} %get-tuple-element.21) | copy-start | bytes 196612
  40.8 1.1 %copy-start = (f32[3,256,128]{2,1,0:T(8,128)S(1)}, f32[3,256,128]{2,1,0:T(8,128)}, u32[]{:S(2)}) copy-start(f32[3,256,128]{2,1,0:T(8,128)} %refs_0_.3) | copy-start | bytes 1179652
  40.8 1.1 %copy-start.1 = (f32[3,256,128]{2,1,0:T(8,128)S(1)}, f32[3,256,128]{2,1,0:T(8,128)}, u32[]{:S(2)}) copy-start(f32[3,256,128]{2,1,0:T(8,128)} %refs_1_.3) | copy-start | bytes 1179652
  40.8 1.2 %copy-start.2 = (f32[3,256,128]{2,1,0:T(8,128)S(1)}, f32[3,256,128]{2,1,0:T(8,128)}, u32[]{:S(2)}) copy-start(f32[3,256,128]{2,1,0:T(8,128)} %refs_2_.3) | copy-start | bytes 1179652
  40.9 1.3 %copy-start.3 = (f32[3,256,128]{2,1,0:T(8,128)S(1)}, f32[3,256,128]{2,1,0:T(8,128)}, u32[]{:S(2)}) copy-start(f32[3,256,128]{2,1,0:T(8,128)} %refs_3_.3) | copy-start | bytes 1179652
  40.9 1.3 %copy-start.4 = (f32[12,16,128]{2,1,0:T(8,128)S(1)}, f32[12,16,128]{2,1,0:T(8,128)}, u32[]{:S(2)}) copy-start(f32[12,16,128]{2,1,0:T(8,128)} %get-tuple-element.14.refs_5_) | copy-start | bytes 294916
  40.9 1.3 %copy-start.5 = (f32[12,16,128]{2,1,0:T(8,128)S(1)}, f32[12,16,128]{2,1,0:T(8,128)}, u32[]{:S(2)}) copy-start(f32[12,16,128]{2,1,0:T(8,128)} %get-tuple-element.13.refs_4_) | copy-start | bytes 294916

commit v12 on v10

--- a/solution.py
+++ b/solution.py
@@ -253,7 +253,7 @@
             flux_adv = ext_ref[levels + level] * adjoint
             flux_dif = ext_ref[2 * levels + level] * adjoint
             square = state * state
-            slope = ((square + 1.0) + square) / root
+            slope = ((square + 1.0) + square) * lax.rsqrt(square + 1.0)
             lams[1 - now, level] = (
                 adjoint
                 - flux_adv

time: 66.7 us -> 66.3 us (level)
  no operation moved by 1% of the time
where the time goes in v12:
time: 66.3 us; the launch traced here: 66.1 us
  Pallas kernels  56.9 us (86%)
  other arithmetic  3.68 us (6%)
  local copies, waits for them, and re-layouts  3.16 us (5%)
  matrix products  1.49 us (2%)
  between operations  0.81 us (1%)
    pallas_call x1, Pallas kernels, open_exchange(): pl.pallas_call(functools.partial(open_kernel, n_gx, n_gy, m, len(blocks))...  34.4 us
    pallas_call x1, Pallas kernels, stencil(): pl.pallas_call(functools.partial(stencil_kernel, n_gx, n_gy, levels, STEP...  22.6 us
    concatenate x1, other arithmetic, column_band(): jnp.concatenate([edge(col_high, c_hh, c_lh), fill, edge(col_low, c_hl, c_...  1.58 us
    dot_general x1, matrix products, shards(): jnp.einsum('dkr,dkc->rc', thrusts[..., None] * prof_r, prof_c, precision=...  1.49 us

profile of v12, /device:TPU:1, one launch (start us, length us, event | category | flops | bytes accessed | tf_op | source)
XLA Modules:
  0.0 66.1 jit_solution(11720149815253272225)
XLA Ops:
  0.6 0.8 %convert_bitcast_fusion = (f32[4]{0:T(128)S(1)}, f32[4]{0:T(128)S(1)}, f32[4]{0:T(128)S(1)}) fusion(s32[4,2]{0,1:T(2,128)} %param.13, s32[4,1]{0,1:T(1,128)} %param.12), kind=kLoop, calls=%fused_computation.43 | loop fusion | flops 12 | bytes 96 | tf_op jit(solution)/shard_map/convert_element_type | solution.py:412
  1.4 1.3 %concatenate.12 = f32[128]{0:T(128)} concatenate(f32[4]{0:T(128)S(1)} %get-tuple-element.28, f32[4]{0:T(128)S(1)} %get-tuple-element.27, f32[4]{0:T(128)S(1)} %get-tuple-element.26, f32[4]{0:T(128)} %param.14, f32[4]{0:T(128)} %param.15, f32[108]{0:T(128)S(1)} %broadcast_in_dim.18), dimensions={0} | concatenate | bytes 1024 | tf_op jit(solution)/shard_map/concatenate | solution.py:417
  2.7 34.4 %shard_map.95 = (f32[128,128]{1,0:T(8,128)}, f32[12,16,128]{2,1,0:T(8,128)}, f32[12,16,128]{2,1,0:T(8,128)}, f32[12,16,256]{2,1,0:T(8,128)}, f32[12,16,256]{2,1,...) custom-call(f32[1,128]{1,0:T(1,128)} %bitcast.19, ...), custom_call_target="tpu_custom_call" | custom-call | tf_op jit(solution)/shard_map/pallas_call | solution.py:141
  37.0 0.0 copy-start.6
  37.0 0.1 pad.4.clone
  37.1 1.6 %maximum_maximum_fusion.refs_6_ = f32[12,128,384]{2,1,0:T(8,128)S(1)} fusion(f32[12,16,96]{2,1,0:T(8,128)S(1)} %broadcast.88, f32[12,16,16]{2,1,0:T(8,128)} %get-tuple-element.20, f32[12,16,16]{2,1,0:T(8,128)} %get-tuple-element.19, f32[12,16,256]{2,1,0:T(8,128)} %get-tuple-element.18, f32[12,16,16]{2,1,0:T(8,128)} %get-tuple-element.17, ...), kind=kLoop, calls=%fused_computation | loop fusion | flops 4718592 | bytes 2875904 | tf_op jit(solution)/shard_map/concatenate | solution.py:174
  38.7 0.0 copy-done.6
  38.7 0.1 copy.16
  38.8 0.1 multiply_multiply_fusion
  38.9 0.1 copy.20
  39.0 0.1 fusion.7
  39.1 0.1 fusion.5
  39.2 0.1 copy.18
  39.2 0.1 copy.22
  39.3 1.5 %convolution_bitcast_fusion = f32[288,256]{1,0:T(8,128)S(1)} fusion(f32[128,4]{0,1:T(4,128)S(1)} %slice.40, f32[128,4]{0,1:T(4,128)S(1)} %copy.20, s32[128,4]{0,1:T(4,128)S(1)} %copy.18, s32[288]{0:T(512)S(1)} %fusion.10, s32[128,4]{0,1:T(4,128)S(1)} %copy.22, s32[256]{0:T(256)S(1)} %fusion.11), kind=kOutput, calls=%fused_computation.1 | convolution fusion | flops 458424320 | bytes 305280 | tf_op jit(solution)/shard_map/dkr,dkc->rc/dot_general | solution.py:435
  40.8 0.0 copy-start
  40.8 0.0 copy-start.1
  40.8 0.0 copy-start.2
  40.9 0.0 copy-start.3
  40.9 0.0 copy-start.4
  40.9 0.0 copy-start.5
  40.9 0.1 broadcast_multiply_fusion.refs_7_
  41.1 0.5 exponential_select_fusion
  41.6 0.4 exponential_select_fusion.1
  42.0 0.1 broadcast_in_dim.43.refs_11_
  42.1 0.0 copy-done
  42.1 0.0 copy-done.1
  42.1 0.0 copy-done.2
  42.1 0.1 copy-done.3
  42.2 0.0 copy-done.4
  42.2 0.0 copy-done.5
  42.2 22.6 %shard_map.96 = (f32[3,256,128]{2,1,0:T(8,128)S(1)}, f32[1,128]{1,0:T(1,128)S(1)}) custom-call(f32[3,256,128]{2,1,0:T(8,128)S(1)} %copy-done, f32[3,256,128]{2,1,0:T(8,128)S(1)} %copy-done.1, f32[3,256,128]{2,1,0:T(8,128)S(1)} %copy-done.2, f32[3,256,128]{2,1,0:T(8,128)S(1)} %copy-done.3, f32[12,16,128]{2,1,0:T(8,128)S(1)} %copy-done.5, ...), custom_call_target="tpu_custom_call" | custom-call | flops 106168320 | bytes 6193152 | tf_op jit(solution)/shard_map/pallas_call | solution.py:303
  64.8 0.5 slice_bitcast_fusion.2
  65.3 0.7 %copy.29 = f32[3,256,128]{2,1,0:T(8,128)} copy(f32[3,256,128]{2,1,0:T(8,128)S(1)} %get-tuple-element.31) | data formatting | bytes 786432
  (9 shorter events, 0.1 us)
Async XLA Ops:
  37.0 1.7 %copy-start.6 = (f32[128,128]{1,0:T(8,128)S(1)}, f32[128,128]{1,0:T(8,128)}, u32[]{:S(2)}) copy-start(f32[128,128]{1,0:T(8,128)} %get-tuple-element.21) | copy-start | bytes 196612
  40.8 1.3 %copy-start = (f32[3,256,128]{2,1,0:T(8,128)S(1)}, f32[3,256,128]{2,1,0:T(8,128)}, u32[]{:S(2)}) copy-start(f32[3,256,128]{2,1,0:T(8,128)} %refs_0_.3) | copy-start | bytes 1179652
  40.8 1.3 %copy-start.1 = (f32[3,256,128]{2,1,0:T(8,128)S(1)}, f32[3,256,128]{2,1,0:T(8,128)}, u32[]{:S(2)}) copy-start(f32[3,256,128]{2,1,0:T(8,128)} %refs_1_.3) | copy-start | bytes 1179652
  40.8 1.3 %copy-start.2 = (f32[3,256,128]{2,1,0:T(8,128)S(1)}, f32[3,256,128]{2,1,0:T(8,128)}, u32[]{:S(2)}) copy-start(f32[3,256,128]{2,1,0:T(8,128)} %refs_2_.3) | copy-start | bytes 1179652
  40.9 1.3 %copy-start.3 = (f32[3,256,128]{2,1,0:T(8,128)S(1)}, f32[3,256,128]{2,1,0:T(8,128)}, u32[]{:S(2)}) copy-start(f32[3,256,128]{2,1,0:T(8,128)} %refs_3_.3) | copy-start | bytes 1179652
  40.9 1.3 %copy-start.4 = (f32[12,16,128]{2,1,0:T(8,128)S(1)}, f32[12,16,128]{2,1,0:T(8,128)}, u32[]{:S(2)}) copy-start(f32[12,16,128]{2,1,0:T(8,128)} %get-tuple-element.14.refs_5_) | copy-start | bytes 294916
  40.9 1.3 %copy-start.5 = (f32[12,16,128]{2,1,0:T(8,128)S(1)}, f32[12,16,128]{2,1,0:T(8,128)}, u32[]{:S(2)}) copy-start(f32[12,16,128]{2,1,0:T(8,128)} %get-tuple-element.13.refs_4_) | copy-start | bytes 294916

commit v13 on v10

--- a/solution.py
+++ b/solution.py
@@ -95,7 +95,8 @@
         [(columns.at[1], whole)],
     ) + tuple([(corners.at[index], whole)] for index in range(len(HALO_MOVES) - 4))
     waits = []
-    for index, (dx, dy) in enumerate(HALO_MOVES):
+    for index in (2, 3, 4, 5, 6, 7, 0, 1):
+        dx, dy = HALO_MOVES[index]
         target = (lax.rem(gx + dx + n_gx, n_gx), lax.rem(gy + dy + n_gy, n_gy))
         for source, depth in sources[index]:
             pltpu.make_async_remote_copy(

time: 66.7 us -> 67.1 us (level)
  no operation moved by 1% of the time
where the time goes in v13:
time: 67.1 us; the launch traced here: 66.9 us
  Pallas kernels  57.7 us (86%)
  other arithmetic  3.68 us (5%)
  local copies, waits for them, and re-layouts  3.16 us (5%)
  matrix products  1.49 us (2%)
  between operations  0.81 us (1%)
    pallas_call x1, Pallas kernels, open_exchange(): pl.pallas_call(functools.partial(open_kernel, n_gx, n_gy, m, len(blocks))...  34.3 us
    pallas_call x1, Pallas kernels, stencil(): pl.pallas_call(functools.partial(stencil_kernel, n_gx, n_gy, levels, STEP...  23.4 us
    concatenate x1, other arithmetic, column_band(): jnp.concatenate([edge(col_high, c_hh, c_lh), fill, edge(col_low, c_hl, c_...  1.58 us
    dot_general x1, matrix products, shards(): jnp.einsum('dkr,dkc->rc', thrusts[..., None] * prof_r, prof_c, precision=...  1.49 us

profile of v13, /device:TPU:1, one launch (start us, length us, event | category | flops | bytes accessed | tf_op | source)
XLA Modules:
  0.0 66.9 jit_solution(2253092897905696690)
XLA Ops:
  0.6 0.8 %convert_bitcast_fusion = (f32[4]{0:T(128)S(1)}, f32[4]{0:T(128)S(1)}, f32[4]{0:T(128)S(1)}) fusion(s32[4,2]{0,1:T(2,128)} %param.13, s32[4,1]{0,1:T(1,128)} %param.12), kind=kLoop, calls=%fused_computation.43 | loop fusion | flops 12 | bytes 96 | tf_op jit(solution)/shard_map/convert_element_type | solution.py:413
  1.4 1.3 %concatenate.12 = f32[128]{0:T(128)} concatenate(f32[4]{0:T(128)S(1)} %get-tuple-element.28, f32[4]{0:T(128)S(1)} %get-tuple-element.27, f32[4]{0:T(128)S(1)} %get-tuple-element.26, f32[4]{0:T(128)} %param.14, f32[4]{0:T(128)} %param.15, f32[108]{0:T(128)S(1)} %broadcast_in_dim.18), dimensions={0} | concatenate | bytes 1024 | tf_op jit(solution)/shard_map/concatenate | solution.py:418
  2.7 34.3 %shard_map.95 = (f32[128,128]{1,0:T(8,128)}, f32[12,16,128]{2,1,0:T(8,128)}, f32[12,16,128]{2,1,0:T(8,128)}, f32[12,16,256]{2,1,0:T(8,128)}, f32[12,16,256]{2,1,...) custom-call(f32[1,128]{1,0:T(1,128)} %bitcast.19, ...), custom_call_target="tpu_custom_call" | custom-call | tf_op jit(solution)/shard_map/pallas_call | solution.py:142
  37.0 0.0 copy-start.6
  37.0 0.1 pad.4.clone
  37.1 1.6 %maximum_maximum_fusion.refs_6_ = f32[12,128,384]{2,1,0:T(8,128)S(1)} fusion(f32[12,16,96]{2,1,0:T(8,128)S(1)} %broadcast.88, f32[12,16,16]{2,1,0:T(8,128)} %get-tuple-element.20, f32[12,16,16]{2,1,0:T(8,128)} %get-tuple-element.19, f32[12,16,256]{2,1,0:T(8,128)} %get-tuple-element.18, f32[12,16,16]{2,1,0:T(8,128)} %get-tuple-element.17, ...), kind=kLoop, calls=%fused_computation | loop fusion | flops 4718592 | bytes 2875904 | tf_op jit(solution)/shard_map/concatenate | solution.py:175
  38.7 0.0 copy-done.6
  38.7 0.1 copy.16
  38.8 0.1 multiply_multiply_fusion
  38.9 0.1 copy.20
  38.9 0.1 fusion.7
  39.0 0.1 fusion.5
  39.1 0.1 copy.18
  39.2 0.1 copy.22
  39.3 1.5 %convolution_bitcast_fusion = f32[288,256]{1,0:T(8,128)S(1)} fusion(f32[128,4]{0,1:T(4,128)S(1)} %slice.40, f32[128,4]{0,1:T(4,128)S(1)} %copy.20, s32[128,4]{0,1:T(4,128)S(1)} %copy.18, s32[288]{0:T(512)S(1)} %fusion.10, s32[128,4]{0,1:T(4,128)S(1)} %copy.22, s32[256]{0:T(256)S(1)} %fusion.11), kind=kOutput, calls=%fused_computation.1 | convolution fusion | flops 458424320 | bytes 305280 | tf_op jit(solution)/shard_map/dkr,dkc->rc/dot_general | solution.py:436
  40.8 0.0 copy-start
  40.8 0.0 copy-start.1
  40.8 0.0 copy-start.2
  40.8 0.0 copy-start.3
  40.8 0.0 copy-start.4
  40.8 0.0 copy-start.5
  40.9 0.1 broadcast_multiply_fusion.refs_7_
  41.0 0.5 exponential_select_fusion
  41.5 0.4 exponential_select_fusion.1
  42.0 0.1 broadcast_in_dim.43.refs_11_
  42.1 0.0 copy-done
  42.1 0.0 copy-done.1
  42.1 0.0 copy-done.2
  42.1 0.1 copy-done.3
  42.1 0.0 copy-done.4
  42.1 0.0 copy-done.5
  42.2 23.4 %shard_map.96 = (f32[3,256,128]{2,1,0:T(8,128)S(1)}, f32[1,128]{1,0:T(1,128)S(1)}) custom-call(f32[3,256,128]{2,1,0:T(8,128)S(1)} %copy-done, f32[3,256,128]{2,1,0:T(8,128)S(1)} %copy-done.1, f32[3,256,128]{2,1,0:T(8,128)S(1)} %copy-done.2, f32[3,256,128]{2,1,0:T(8,128)S(1)} %copy-done.3, f32[12,16,128]{2,1,0:T(8,128)S(1)} %copy-done.5, ...), custom_call_target="tpu_custom_call" | custom-call | flops 106168320 | bytes 6193152 | tf_op jit(solution)/shard_map/pallas_call | solution.py:304
  65.6 0.5 slice_bitcast_fusion.2
  66.1 0.7 %copy.29 = f32[3,256,128]{2,1,0:T(8,128)} copy(f32[3,256,128]{2,1,0:T(8,128)S(1)} %get-tuple-element.31) | data formatting | bytes 786432
  (9 shorter events, 0.1 us)
Async XLA Ops:
  37.0 1.7 %copy-start.6 = (f32[128,128]{1,0:T(8,128)S(1)}, f32[128,128]{1,0:T(8,128)}, u32[]{:S(2)}) copy-start(f32[128,128]{1,0:T(8,128)} %get-tuple-element.21) | copy-start | bytes 196612
  40.8 1.3 %copy-start = (f32[3,256,128]{2,1,0:T(8,128)S(1)}, f32[3,256,128]{2,1,0:T(8,128)}, u32[]{:S(2)}) copy-start(f32[3,256,128]{2,1,0:T(8,128)} %refs_0_.3) | copy-start | bytes 1179652
  40.8 1.3 %copy-start.1 = (f32[3,256,128]{2,1,0:T(8,128)S(1)}, f32[3,256,128]{2,1,0:T(8,128)}, u32[]{:S(2)}) copy-start(f32[3,256,128]{2,1,0:T(8,128)} %refs_1_.3) | copy-start | bytes 1179652
  40.8 1.3 %copy-start.2 = (f32[3,256,128]{2,1,0:T(8,128)S(1)}, f32[3,256,128]{2,1,0:T(8,128)}, u32[]{:S(2)}) copy-start(f32[3,256,128]{2,1,0:T(8,128)} %refs_2_.3) | copy-start | bytes 1179652
  40.8 1.3 %copy-start.3 = (f32[3,256,128]{2,1,0:T(8,128)S(1)}, f32[3,256,128]{2,1,0:T(8,128)}, u32[]{:S(2)}) copy-start(f32[3,256,128]{2,1,0:T(8,128)} %refs_3_.3) | copy-start | bytes 1179652
  40.8 1.3 %copy-start.4 = (f32[12,16,128]{2,1,0:T(8,128)S(1)}, f32[12,16,128]{2,1,0:T(8,128)}, u32[]{:S(2)}) copy-start(f32[12,16,128]{2,1,0:T(8,128)} %get-tuple-element.14.refs_5_) | copy-start | bytes 294916
  40.8 1.3 %copy-start.5 = (f32[12,16,128]{2,1,0:T(8,128)S(1)}, f32[12,16,128]{2,1,0:T(8,128)}, u32[]{:S(2)}) copy-start(f32[12,16,128]{2,1,0:T(8,128)} %get-tuple-element.13.refs_4_) | copy-start | bytes 294916
